TPU v7x, 768 devices: a whole 4x8x12 slice. The times are simulated.
768 devices in a mesh: blk: 96 (over y, z_lo, x), rep: 8 (over z_hi, core).
Axes of the slice: x: 4, y: 8, z: 12 (z_hi: 4, z_lo: 3; z = z_hi * 3 + z_lo), core: 2. Of those that a mesh axis runs over, the one named last changes fastest.
Arguments:
- features: bfloat16 [49152, 512], P('blk'), may hold values from -2000 to 2000
- labels: int32 [49152], P('blk'), may hold values from 0 to 127
- w_first: bfloat16 [512, 512], replicated, may hold values from -0.25 to 0.25
- w_second: bfloat16 [512, 128], replicated, may hold values from -0.25 to 0.25
- block_rows: int32 [96, 8, 12, 2], P('blk', 'rep'), may hold values from 0 to 1, as said below
- block_cols: int32 [96, 8, 12, 2], P('blk', 'rep'), may hold values from 0 to 1
- block_vals: bfloat16 [96, 8, 12, 2, 256, 256], P('blk', 'rep')
Outputs:
- logits: bfloat16 [49152, 128], P('blk')
- grad_first: float32 [512, 512], replicated
- grad_second: float32 [512, 128], replicated
- loss: float32 [], replicated
Inputs may be any that keep to these rules, and one draw needn't show every extreme that they name: `block_rows`: slot (i, r, t, p) holds a block of shard i's rows against shard (i - r * 12 - t) mod 96's columns; the matrix A assembled from all slots is symmetric; slots whose values are all zero are padding.
All inputs are finite; a program needn't handle non-finite values.
Results may differ from a plain program's by a relative error of at most 0.0083.
Values may be sent and summed in bfloat16 or wider, within the bound.
No kernel may reach another device: no remote copies, remote signals or barrier semaphores. Data moves between devices by JAX's collectives and lax.ppermute only.
A program may use at most 32 MiB of HBM per device.

v0:
```python
import math

import jax
import jax.numpy as jnp
from jax import lax
from jax.sharding import PartitionSpec as P

HOPS = 2


alpha_rate = 0.1


def passed_along(value, axis, by):
    size = lax.axis_size(axis)
    return lax.ppermute(value, axis, [(i, (i + by) % size) for i in range(size)])


def on_device(features, labels, w_first, w_second, block_rows, block_cols, block_vals):
    rows_all = features.shape[0]
    classes = w_second.shape[1]
    nrep = lax.axis_size("rep")
    rep_id = lax.axis_index("rep")
    share = rows_all // nrep
    nodes = rows_all * lax.axis_size("blk")
    index_rows = block_rows[0, 0]
    index_cols = block_cols[0, 0]
    tiles = block_vals[0, 0]
    steps = tiles.shape[0]
    slots = tiles.shape[1]
    width = tiles.shape[2]

    def add_step(total, step, panel):
        step_tiles = lax.dynamic_index_in_dim(tiles, step, 0, keepdims=False)
        step_rows = lax.dynamic_index_in_dim(index_rows, step, 0, keepdims=False)
        step_cols = lax.dynamic_index_in_dim(index_cols, step, 0, keepdims=False)
        for slot in range(slots):
            piece = lax.dynamic_slice_in_dim(panel, step_cols[slot] * width, width, 0)
            product = jnp.dot(step_tiles[slot], piece, preferred_element_type=jnp.float32)
            start = step_rows[slot] * width
            current = lax.dynamic_slice_in_dim(total, start, width, 0)
            total = lax.dynamic_update_slice_in_dim(total, current + product, start, 0)
        return total

    def propagate(panel):
        total = jnp.zeros((rows_all, classes), jnp.float32)
        near = panel
        for bit in range(nrep.bit_length() - 1):
            moved = passed_along(near, "blk", steps * (1 << bit))
            near = jnp.where(rep_id >> bit & 1 == 1, moved, near)

        def turn_one(turn, carry):
            acc, ahead = carry
            acc = add_step(acc, turn, ahead)
            ahead = passed_along(ahead, "blk", 1)
            return (acc, ahead)

        total, near = lax.fori_loop(0, steps - 1, turn_one, (total, near))
        total = add_step(total, steps - 1, near)
        return total

    def mine(full):
        return lax.dynamic_slice_in_dim(full, rep_id * share, share, 0)

    def reduce_rows(term):
        return lax.psum(term, "rep")

    def to_own(part_rows):
        return mine(part_rows)

    hidden = jax.nn.relu(jnp.dot(features, w_first, preferred_element_type=jnp.float32)).astype(
        jnp.bfloat16
    )
    base = jnp.dot(hidden, w_second, preferred_element_type=jnp.float32).astype(jnp.bfloat16)
    base_part = base.astype(jnp.float32)
    current = base
    for step in range(HOPS):
        mixed = (1.0 - alpha_rate) * reduce_rows(propagate(current)) + alpha_rate * base_part
        if step + 1 < HOPS:
            current = mixed.astype(jnp.bfloat16)
    logits = mixed.astype(jnp.bfloat16)
    onehot = (labels[:, None] == jnp.arange(classes, dtype=jnp.int32)[None, :]).astype(jnp.float32)
    lse = jax.nn.logsumexp(mixed, axis=1)
    picked = jnp.sum(mixed * onehot, axis=1)
    ce_sum = jnp.sum(to_own(lse - picked))
    grad_out = (jax.nn.softmax(mixed, axis=1) - onehot) * (1.0 / math.sqrt(nodes))
    grad_base = alpha_rate * grad_out
    moving = grad_out.astype(jnp.bfloat16)
    for step in range(HOPS):
        nxt = (1.0 - alpha_rate) * reduce_rows(propagate(moving))
        if step + 1 < HOPS:
            grad_base = grad_base + alpha_rate * nxt
            moving = nxt.astype(jnp.bfloat16)
        else:
            grad_base = grad_base + nxt
    grad_own = to_own(grad_base).astype(jnp.bfloat16)
    hidden_own = mine(hidden)
    feature_own = mine(features)
    grad_second = lax.dot_general(
        hidden_own, grad_own, (((0,), (0,)), ((), ())), preferred_element_type=jnp.float32
    )
    back = lax.dot_general(
        grad_own, w_second, (((1,), (1,)), ((), ())), preferred_element_type=jnp.float32
    )
    grad_hidden = jnp.where(hidden_own > 0, back, 0.0).astype(jnp.bfloat16)
    grad_first = lax.dot_general(
        feature_own, grad_hidden, (((0,), (0,)), ((), ())), preferred_element_type=jnp.float32
    )
    totals = lax.psum((grad_first, grad_second, ce_sum), ("blk", "rep"))
    return (logits, totals[0], totals[1], totals[2] / nodes)


def solution(mesh):
    in_specs = (
        P("blk", None),
        P("blk"),
        P(),
        P(),
        P("blk", "rep", None, None),
        P("blk", "rep", None, None),
        P("blk", "rep", None, None, None, None),
    )
    out_specs = (P("blk", None), P(), P(), P())
    return jax.shard_map(
        on_device, mesh=mesh, in_specs=in_specs, out_specs=out_specs, check_vma=False
    )
```

profile of v0, /device:TPU:1, one launch (start us, length us, event | category | flops | bytes accessed | tf_op | source)
XLA Modules:
  0.0 1595.1 jit_solution(7351675704544308300)
XLA Ops:
  10.9 4.0 collective-permute-start.4
  14.9 4.2 collective-permute-done.4
  19.2 3.0 collective-permute-start.5
  22.2 6.3 collective-permute-done.5
  28.5 6.1 collective-permute-start.6
  38.5 123.2 %while.60 = (s32[]{:T(128)}, f32[512,128]{1,0:T(8,128)S(1)}, bf16[512,128]{1,0:T(8,128)(2,1)S(1)}, s32[12,2]{0,1:T(2,128)S(1)}, bf16[12,2,256,256]{3,2,1,0:T(8,1...) while((s32[]{:T(128)}, f32[512,128]{1,0:T(8,128)S(1)}, ...), condition=%wide.region_1.2_spmd, body=%wide.region_0.1_spmd.sunk | while | flops 33619976 | bytes 1704385 | solution.py:58
  38.5 6.8 collective-permute-start
  51.3 3.1 collective-permute-start
  80.9 3.0 collective-permute-done
  91.7 3.0 collective-permute-done
  124.2 3.0 collective-permute-done
  145.9 3.3 collective-permute-done
  157.1 4.6 collective-permute-done
  164.7 121.6 %all-reduce.7.cloned.1.call-done = f32[512,128]{1,0:T(8,128)} async-done(((f32[512,128]{1,0:T(8,128)}), f32[512,128]{1,0:T(8,128)}) %all-reduce.7.cloned.1.call-update) | async-done | bytes 262160 | tf_op jit(solution)/shard_map/psum | solution.py:66
  287.2 3.1 collective-permute-start.7
  290.4 3.8 collective-permute-done.7
  297.0 6.2 collective-permute-done.8
  303.3 6.1 collective-permute-start.9
  309.3 3.5 collective-permute-done.9
  312.9 125.3 %while.61 = (s32[]{:T(128)}, f32[512,128]{1,0:T(8,128)S(1)}, bf16[512,128]{1,0:T(8,128)(2,1)S(1)}, s32[12,2]{0,1:T(2,128)S(1)}, bf16[12,2,256,256]{3,2,1,0:T(8,1...) while((s32[]{:T(128)}, f32[512,128]{1,0:T(8,128)S(1)}, ...), condition=%wide.region_4.5_spmd, body=%wide.region_3.4_spmd.sunk | while | flops 33619976 | bytes 1704385 | solution.py:58
  313.0 3.1 collective-permute-start.1
  322.0 5.9 collective-permute-done.1
  368.3 3.0 collective-permute-done.1
  400.8 3.8 collective-permute-done.1
  412.5 4.0 collective-permute-done.1
  441.2 114.9 %all-reduce.9.cloned.1.call-done = f32[512,128]{1,0:T(8,128)} async-done(((f32[512,128]{1,0:T(8,128)}), f32[512,128]{1,0:T(8,128)}) %all-reduce.9.cloned.1.call-update) | async-done | bytes 262160 | tf_op jit(solution)/shard_map/psum | solution.py:66
  558.6 3.1 collective-permute-start.10
  561.7 3.8 collective-permute-done.10
  568.4 6.2 collective-permute-done.11
  574.6 6.1 collective-permute-start.12
  580.7 3.5 collective-permute-done.12
  584.3 125.3 %while.62 = (s32[]{:T(128)}, f32[512,128]{1,0:T(8,128)S(1)}, bf16[512,128]{1,0:T(8,128)(2,1)S(1)}, s32[12,2]{0,1:T(2,128)S(1)}, bf16[12,2,256,256]{3,2,1,0:T(8,1...) while((s32[]{:T(128)}, f32[512,128]{1,0:T(8,128)S(1)}, ...), condition=%wide.region_9.10_spmd, body=%wide.region_8.9_spmd.sunk | while | flops 33619976 | bytes 1704385 | solution.py:58
  584.3 3.1 collective-permute-start.2
  593.4 5.9 collective-permute-done.2
  607.1 3.0 collective-permute-done.2
  617.9 3.0 collective-permute-done.2
  639.6 3.0 collective-permute-done.2
  650.5 3.0 collective-permute-done.2
  661.3 3.0 collective-permute-done.2
  672.1 3.9 collective-permute-done.2
  683.9 4.0 collective-permute-done.2
  695.8 3.0 collective-permute-done.2
  706.6 3.0 collective-permute-done.2
  712.5 114.9 %all-reduce.11.cloned.1.call-done = f32[512,128]{1,0:T(8,128)} async-done(((f32[512,128]{1,0:T(8,128)}), f32[512,128]{1,0:T(8,128)}) %all-reduce.11.cloned.1.call-update) | async-done | bytes 262160 | tf_op jit(solution)/shard_map/psum | solution.py:66
  828.4 3.1 collective-permute-start.13
  831.5 3.8 collective-permute-done.13
  839.2 6.2 collective-permute-done.14
  845.4 6.1 collective-permute-start.15
  851.5 3.5 collective-permute-done.15
  855.1 125.4 %while.63 = (s32[]{:T(128)}, f32[512,128]{1,0:T(8,128)S(1)}, bf16[512,128]{1,0:T(8,128)(2,1)S(1)}, s32[12,2]{0,1:T(2,128)S(1)}, bf16[12,2,256,256]{3,2,1,0:T(8,1...) while((s32[]{:T(128)}, f32[512,128]{1,0:T(8,128)S(1)}, ...), condition=%wide.region_12.13_spmd, body=%wide.region_11.12_spmd.sunk | while | flops 33619976 | bytes 1704385 | solution.py:58
  855.1 3.2 collective-permute-start.3
  864.2 6.0 collective-permute-done.3
  877.9 3.1 collective-permute-done.3
  888.8 3.1 collective-permute-done.3
  910.5 3.1 collective-permute-done.3
  921.3 3.1 collective-permute-done.3
  932.1 3.1 collective-permute-done.3
  943.0 3.9 collective-permute-done.3
  954.7 4.1 collective-permute-done.3
  966.6 3.1 collective-permute-done.3
  977.5 3.1 collective-permute-done.3
  983.5 114.9 %all-reduce.13.cloned.1.call-done = f32[512,128]{1,0:T(8,128)} async-done(((f32[512,128]{1,0:T(8,128)}), f32[512,128]{1,0:T(8,128)}) %all-reduce.13.cloned.1.call-update) | async-done | bytes 262160 | tf_op jit(solution)/shard_map/psum | solution.py:66
  1103.0 109.9 %psum.55 = f32[]{:T(128)} all-reduce(f32[]{:T(128)} %dynamic-slice_reduce_fusion), channel_id=1, replica_groups=mesh['blk'=96,'rep'=8] {'blk','rep'}, use_global_device_ids=true, to_apply=%region_19.20 | all-reduce | flops 1 | bytes 8 | tf_op jit(solution)/shard_map/psum | solution.py:109
  1213.5 369.9 %all-reduce.15.cloned.1.call-done = (f32[512,512]{1,0:T(8,128)}, f32[512,128]{1,0:T(8,128)}) async-done(((f32[512,512]{1,0:T(8,128)}, f32[512,128]{1,0:T(8,128)}), (f32[512,512]{1,0:T(8,128)}, f32[512,128]{1,0:T(8,128)})) %all-reduce.15.cloned.1.call-update) | async-done | bytes 1310736 | tf_op jit(solution)/shard_map/psum | solution.py:109
  (390 shorter events, 299.9 us)
Async XLA Ops:
  7.2 29.3 %copy-start.7 = (s32[1,1,12,2]{2,3,1,0:T(2,128)S(1)}, s32[1,1,12,2]{2,3,1,0:T(2,128)}, u32[]{:S(2)}) copy-start(s32[1,1,12,2]{2,3,1,0:T(2,128)} %param.20) | copy-start | bytes 292
  7.2 279.0 %all-reduce.7.cloned.1.call-start = ((), (), s32[]{:S(2)}) async-start(), calls=%async_computation | async-start | bytes 524288 | tf_op jit(solution)/shard_map/psum | solution.py:66
  10.9 8.3 collective-permute-start.4
  19.2 9.3 collective-permute-start.5
  28.5 9.9 collective-permute-start.6
  38.5 12.8 collective-permute-start
  51.3 10.8 collective-permute-start
  62.2 10.8 collective-permute-start
  73.0 10.8 collective-permute-start
  83.9 10.8 collective-permute-start
  94.7 10.8 collective-permute-start
  105.6 10.8 collective-permute-start
  116.4 10.8 collective-permute-start
  127.2 10.8 collective-permute-start
  138.1 11.2 collective-permute-start
  149.3 12.4 collective-permute-start
  164.6 391.5 %all-reduce.9.cloned.1.call-start = ((), (), s32[]{:S(2)}) async-start(), calls=%async_computation.1 | async-start | bytes 524288 | tf_op jit(solution)/shard_map/psum | solution.py:66
  287.2 6.9 collective-permute-start.7
  294.2 9.1 collective-permute-start.8
  303.3 9.6 collective-permute-start.9
  312.9 244.3 %copy-start.8 = (s32[512]{0:T(512)S(1)}, s32[512]{0:T(512)}, u32[]{:S(2)}) copy-start(s32[512]{0:T(512)} %param.16) | copy-start | bytes 6148
  313.0 14.9 collective-permute-start.1
  327.9 10.8 collective-permute-start.1
  338.7 10.8 collective-permute-start.1
  349.6 10.8 collective-permute-start.1
  360.4 10.8 collective-permute-start.1
  371.3 10.8 collective-permute-start.1
  382.1 10.8 collective-permute-start.1
  393.0 11.7 collective-permute-start.1
  404.7 11.9 collective-permute-start.1
  416.6 10.8 collective-permute-start.1
  427.4 10.8 collective-permute-start.1
  441.1 386.3 %all-reduce.11.cloned.1.call-start = ((), (), s32[]{:S(2)}) async-start(), calls=%async_computation.2 | async-start | bytes 524288 | tf_op jit(solution)/shard_map/psum | solution.py:66
  558.6 6.9 collective-permute-start.10
  565.6 9.1 collective-permute-start.11
  574.6 9.6 collective-permute-start.12
  584.3 14.9 collective-permute-start.2
  599.2 10.8 collective-permute-start.2
  610.1 10.8 collective-permute-start.2
  620.9 10.8 collective-permute-start.2
  631.8 10.8 collective-permute-start.2
  642.6 10.8 collective-permute-start.2
  653.5 10.8 collective-permute-start.2
  664.3 11.7 collective-permute-start.2
  676.0 11.9 collective-permute-start.2
  687.9 10.8 collective-permute-start.2
  698.8 10.8 collective-permute-start.2
  712.5 385.9 %all-reduce.13.cloned.1.call-start = ((), (), s32[]{:S(2)}) async-start(), calls=%async_computation.3 | async-start | bytes 524288 | tf_op jit(solution)/shard_map/psum | solution.py:66
  828.4 6.9 collective-permute-start.13
  836.3 9.1 collective-permute-start.14
  845.4 9.6 collective-permute-start.15
  855.1 245.0 %copy-start.5 = (bf16[512,128]{1,0:T(8,128)(2,1)S(1)}, bf16[512,128]{1,0:T(8,128)(2,1)}, u32[]{:S(2)}) copy-start(bf16[512,128]{1,0:T(8,128)(2,1)} %param.18) | copy-start | bytes 393220
  855.1 15.0 collective-permute-start.3
  870.2 10.8 collective-permute-start.3
  881.0 10.8 collective-permute-start.3
  891.9 10.8 collective-permute-start.3
  902.7 10.8 collective-permute-start.3
  913.5 10.8 collective-permute-start.3
  924.4 10.8 collective-permute-start.3
  935.2 11.7 collective-permute-start.3
  946.9 11.9 collective-permute-start.3
  958.9 10.8 collective-permute-start.3
  969.7 10.8 collective-permute-start.3
  983.4 600.0 %all-reduce.15.cloned.1.call-start = ((), (), s32[]{:S(2)}) async-start(), calls=%async_computation.4 | async-start | bytes 2621440 | tf_op jit(solution)/shard_map/psum | solution.py:109
  (6 other events, 31.3 us)
Sparse Core Ops, SparseCore 0:
  164.7 121.4 all-reduce.6
  441.3 114.7 all-reduce.8
  712.6 114.7 all-reduce.10
  983.6 114.7 all-reduce.12
  1104.5 478.9 all-reduce.14
where the time goes:
time: 1600 us
  waiting for transfers between devices  1030 us (64%)
  starting transfers between devices  145 us (9%)
  loops' own time  115 us (7%)
  matrix products  111 us (7%)
  blocking collectives  110 us (7%)
  local copies, waits for them, and re-layouts  58.9 us (4%)
  between operations  18.6 us (1%)
    psum x4, waiting for transfers between devices, reduce_rows(): return lax.psum(term, 'rep')  466 us
    psum x1, waiting for transfers between devices, on_device(): totals = lax.psum((grad_first, grad_second, ce_sum), ('blk', 'rep'))  370 us
    ppermute x56, waiting for transfers between devices, passed_along(): lax.ppermute(value, axis, [(i, (i + by) % size) for i in range(size)])  194 us
    ppermute x56, starting transfers between devices, passed_along(): lax.ppermute(value, axis, [(i, (i + by) % size) for i in range(size)])  145 us
    another operation x4, loops' own time, propagate(): total, near = lax.fori_loop(0, steps - 1, turn_one, (total, near))  115 us
    psum x1, blocking collectives, on_device(): totals = lax.psum((grad_first, grad_second, ce_sum), ('blk', 'rep'))  110 us
    dot_general x96, matrix products, add_step(): jnp.dot(step_tiles[slot], piece, preferred_element_type=jnp.float32)  104 us
  transfers between devices with their start and end apart: 61, of which 59 were waited for; matrix products, arithmetic and copies ran while one was open for 9% of the time, Pallas kernels for 0%

commit v1 on v0

v1 whole, which is shorter than its diff:
```python
import functools
import math

import jax
import jax.numpy as jnp
from jax import lax
from jax.experimental import pallas as pl
from jax.experimental.pallas import tpu as pltpu
from jax.sharding import Mesh
from jax.sharding import PartitionSpec as P

ALPHA = 0.1
BF = jnp.bfloat16
F32 = jnp.float32
REP = ("zh", "c")
BLK = ("y", "q")


def scatter_kernel(index_ref, tiles_ref, panel_ref, out_ref):
    steps, slots, width, _ = tiles_ref.shape
    blocks = out_ref.shape[1] // width
    q = index_ref[2 * steps * slots]
    share = jnp.where(index_ref[2 * steps * slots + 1] == 1, ALPHA / (1.0 - ALPHA), 0.0).astype(F32)
    for t in range(steps):
        place = lax.rem(q + (steps - t), steps)
        products = []
        for p in range(slots):
            row = index_ref[t * slots + p]
            piece = panel_ref[pl.ds(pl.multiple_of(row * width, width), width), :]
            products.append(
                lax.dot_general(
                    tiles_ref[t, p], piece, (((0,), (0,)), ((), ())), preferred_element_type=F32
                )
            )
        for b in range(blocks):
            total = jnp.zeros(products[0].shape, F32)
            for p in range(slots):
                col = index_ref[steps * slots + t * slots + p]
                total = total + jnp.where(col == b, products[p], 0.0)
            if t == 0:
                total = total + share * panel_ref[b * width : (b + 1) * width, :].astype(F32)
            out_ref[place, b * width : (b + 1) * width, :] = total.astype(BF)


def gather_kernel(index_ref, tiles_ref, panels_ref, out_ref):
    steps, slots, width, _ = tiles_ref.shape
    q = index_ref[2 * steps * slots]
    share = jnp.where(index_ref[2 * steps * slots + 1] == 1, ALPHA / (1.0 - ALPHA), 0.0).astype(F32)
    out_ref[...] = share * panels_ref[q].astype(F32)
    for t in range(steps):
        place = lax.rem(q + (steps - t), steps)
        for p in range(slots):
            row = index_ref[t * slots + p]
            col = index_ref[steps * slots + t * slots + p]
            piece = panels_ref[place, pl.ds(pl.multiple_of(col * width, width), width), :]
            rows = pl.ds(pl.multiple_of(row * width, width), width)
            out_ref[rows, :] += jnp.dot(tiles_ref[t, p], piece, preferred_element_type=F32)


def call(kernel, shape, dtype, index, *operands, interpret=False):
    vmem = pl.BlockSpec(memory_space=pltpu.VMEM)
    return pl.pallas_call(
        kernel,
        out_shape=jax.ShapeDtypeStruct(shape, dtype),
        in_specs=[pl.BlockSpec(memory_space=pltpu.SMEM)] + [vmem] * len(operands),
        out_specs=vmem,
        interpret=interpret,
    )(index, *operands)


def on_device(interpret, features, labels, w_first, w_second, block_rows, block_cols, block_vals):
    nodes_here = features.shape[0]
    classes = w_second.shape[1]
    ny, nq, nzh, nc = (lax.axis_size(a) for a in ("y", "q", "zh", "c"))
    nrep = nzh * nc
    nblk = ny * nq
    q_id = lax.axis_index("q")
    c_id = lax.axis_index("c")
    rep_id = lax.axis_index(REP)
    nodes = nodes_here * nblk
    tiles = block_vals[0, 0]
    steps = tiles.shape[0]
    half = nodes_here // nc
    skewed = [[((y + r) % ny) * nrep + r for r in range(nrep)] for y in range(ny)]
    yrep = ("y",) + REP
    core_swap = [(i, (i + 1) % nc) for i in range(nc)]

    def index_of(flag):
        tail = jnp.stack([q_id, flag]).astype(jnp.int32)
        return jnp.concatenate([block_rows[0, 0].reshape(-1), block_cols[0, 0].reshape(-1), tail])

    plain = index_of(jnp.int32(0))
    diagonal = index_of((rep_id == 0).astype(jnp.int32))
    from_same = (jnp.arange(nq, dtype=jnp.int32) >= q_id)[:, None, None]

    def to_all(value, count):
        return jnp.broadcast_to(value[None], (count,) + value.shape)

    def with_transpose(panel, index):
        parts = call(
            scatter_kernel, (steps, nodes_here, classes), BF, index, tiles, panel, interpret=interpret
        )
        parts = lax.all_to_all(parts, "q", 0, 0, tiled=True).astype(F32)
        before = jnp.sum(jnp.where(from_same, 0.0, parts), axis=0).astype(BF)
        moved = lax.ppermute(before, "y", [((i + 1) % ny, i) for i in range(ny)])
        total = jnp.sum(jnp.where(from_same, parts, 0.0), axis=0) + moved.astype(F32)
        pieces = total.astype(BF).reshape(nrep, nodes_here // nrep, classes)
        pieces = lax.all_to_all(pieces, yrep, 0, 0, axis_index_groups=skewed, tiled=True)
        return (1.0 - ALPHA) * jnp.sum(pieces.astype(F32), axis=0)

    def with_plain(piece, index):
        here = lax.all_to_all(
            to_all(piece, nrep), yrep, 0, 0, axis_index_groups=skewed, tiled=True
        ).reshape(nodes_here, classes)
        before = lax.ppermute(here, "y", [(i, (i + 1) % ny) for i in range(ny)])
        panels = jnp.where(from_same, here[None], before[None])
        panels = lax.all_to_all(panels, "q", 0, 0, tiled=True)
        part = call(
            gather_kernel, (nodes_here, classes), F32, index, tiles, panels, interpret=interpret
        )
        away = lax.dynamic_slice_in_dim(part, (nc - 1 - c_id) * half, half, 0).astype(BF)
        mine = lax.dynamic_slice_in_dim(part, c_id * half, half, 0)
        chip = (mine + lax.ppermute(away, "c", core_swap).astype(F32)).astype(BF)
        chips = lax.all_to_all(to_all(chip, nzh), "zh", 0, 0, tiled=True)
        return (1.0 - ALPHA) * jnp.sum(chips.astype(F32), axis=0)

    def whole(mine):
        other = lax.ppermute(mine, "c", core_swap)
        return jnp.where(
            c_id == 0,
            jnp.concatenate([mine, other], axis=-2),
            jnp.concatenate([other, mine], axis=-2),
        )

    hidden = jax.nn.relu(jnp.dot(features, w_first, preferred_element_type=F32)).astype(BF)
    base = jnp.dot(hidden, w_second, preferred_element_type=F32).astype(BF)
    base_half = lax.dynamic_slice_in_dim(base, c_id * half, half, 0)

    current = with_transpose(base, diagonal).astype(BF)
    mixed = with_plain(current, plain) + ALPHA * base_half.astype(F32)
    labels_half = lax.dynamic_slice_in_dim(labels, c_id * half, half, 0)
    onehot = (labels_half[:, None] == jnp.arange(classes, dtype=jnp.int32)[None, :]).astype(F32)
    top = jnp.max(mixed, axis=1, keepdims=True)
    grown = jnp.exp(mixed - top)
    mass = jnp.sum(grown, axis=1, keepdims=True)
    picked = jnp.sum(mixed * onehot, axis=1, keepdims=True)
    ce_sum = jnp.sum(jnp.log(mass) + top - picked)
    grad_out = (grown / mass - onehot) * (1.0 / math.sqrt(nodes))
    both = whole(jnp.stack([grad_out.astype(BF), mixed.astype(BF)]))
    moving, logits = both[0], both[1]

    moving = with_transpose(moving, plain).astype(BF)
    grad_half = with_plain(moving, diagonal) + ALPHA * grad_out
    grad_b = whole(grad_half.astype(BF))

    part = hidden.shape[1] // nrep
    hidden_part = lax.dynamic_slice_in_dim(hidden, rep_id * part, part, 1)
    second_part = lax.dynamic_slice_in_dim(w_second, rep_id * part, part, 0)
    back = lax.dot_general(grad_b, second_part, (((1,), (1,)), ((), ())), preferred_element_type=F32)
    grad_hidden = jnp.where(hidden_part > 0, back, 0.0).astype(BF)
    first_rows = lax.dot_general(
        grad_hidden, features, (((0,), (0,)), ((), ())), preferred_element_type=F32
    )
    second_rows = lax.dot_general(
        hidden_part, grad_b, (((0,), (0,)), ((), ())), preferred_element_type=F32
    )
    width = features.shape[1]
    count_first = part * width // classes
    used = count_first + part
    each = -(-(used + 1) // nblk)
    loss_part = jnp.where(lax.axis_index("zh") == 0, ce_sum, 0.0)
    tail = jnp.zeros((each * nblk - used, classes), F32).at[0, 0].set(loss_part)
    sums = jnp.concatenate([first_rows.reshape(count_first, classes), second_rows, tail])
    sums = lax.all_to_all(sums.reshape(nblk, each, classes), BLK, 0, 0, tiled=True)
    sums = jnp.sum(sums, axis=0)
    lanes = lax.broadcasted_iota(jnp.int32, (each, classes), 1)
    rows = lax.broadcasted_iota(jnp.int32, (each, classes), 0)
    is_loss = (lax.axis_index(BLK) * each + rows) == used
    value = sums[used % each, 0]
    high = value.astype(BF).astype(F32)
    middle = (value - high).astype(BF).astype(F32)
    low = value - high - middle
    terms = jnp.where(lanes == 0, high, jnp.where(lanes == 1, middle, jnp.where(lanes == 2, low, 0.0)))
    sums = jnp.where(is_loss, terms, sums).astype(BF)
    sums = lax.all_to_all(to_all(sums, nrep), REP, 0, 0, tiled=True)
    sums = lax.all_to_all(to_all(sums, nblk), BLK, 0, 0, tiled=True)
    sums = jnp.swapaxes(sums.astype(F32), 0, 1).reshape(nrep, nblk * each, classes)
    grad_first = sums[:, :count_first].reshape(nrep * part, width).T
    grad_second = sums[:, count_first:used].reshape(nrep * part, classes)
    loss = jnp.sum(sums[:, used, :3]) / nodes
    return (logits, grad_first, grad_second, loss)


def solution(mesh, interpret=False):
    nblk, nrep = mesh.devices.shape
    cores = 2
    fine = Mesh(
        mesh.devices.reshape(nrep, nblk // nrep, nrep // cores, cores), ("y", "q", "zh", "c")
    )
    in_specs = (
        P(BLK, None),
        P(BLK),
        P(),
        P(),
        P(BLK, REP, None, None),
        P(BLK, REP, None, None),
        P(BLK, REP, None, None, None, None),
    )
    out_specs = (P(BLK, None), P(), P(), P())
    return jax.shard_map(
        functools.partial(on_device, interpret),
        mesh=fine,
        in_specs=in_specs,
        out_specs=out_specs,
        check_vma=False,
    )
```

time: 1600 us -> 414 us (0.26)
  waiting for transfers between devices: 1030 us -> 85.7 us
  loops' own time: 115 us -> 0 us
  matrix products: 111 us -> 3.02 us
  blocking collectives: 110 us -> 201 us
  starting transfers between devices: 145 us -> 82.2 us
  local copies, waits for them, and re-layouts: 58.9 us -> 10.3 us
  Pallas kernels: 0 us -> 16.3 us
    psum x5 -> x0, waiting for transfers between devices: 836 us -> none  [the longest x4 466 us: reduce_rows(): return lax.psum(term, 'rep')]
    all_to_all x0 -> x8, blocking collectives: none -> 201 us  [the longest x2 60.3 us: with_transpose(): lax.all_to_all(pieces, yrep, 0, 0, axis_index_groups=skewed, tiled=True)]
    ppermute x56 -> x8, waiting for transfers between devices: 194 us -> 15.7 us  [the longest x2 7.28 us: with_transpose(): moved = lax.ppermute(before, 'y', [((i + 1) % ny, i) for i in range(ny)])]
    another operation x4 -> x0, loops' own time: 115 us -> none  [propagate(): total, near = lax.fori_loop(0, steps - 1, turn_one, (total, near))]
    psum x1 -> x0, blocking collectives: 110 us -> none  [on_device(): totals = lax.psum((grad_first, grad_second, ce_sum), ('blk', 'rep'))]
    dot_general x100 -> x4, matrix products: 111 us -> 3.02 us  [the longest x1 1.53 us: on_device(): jnp.dot(features, w_first, preferred_element_type=F32)]
    ppermute x56 -> x8, starting transfers between devices: 145 us -> 55.5 us  [the longest x2 16.5 us: with_transpose(): moved = lax.ppermute(before, 'y', [((i + 1) % ny, i) for i in range(ny)])]
    all_to_all x0 -> x5, waiting for transfers between devices: none -> 70 us  [the longest x2 22.4 us: with_plain(): chips = lax.all_to_all(to_all(chip, nzh), 'zh', 0, 0, tiled=True)]
  transfers between devices with their start and end apart: 61 -> 13, of which waited for: 59 -> 12; matrix products, arithmetic and copies ran while one was open for 9% -> 0% of each run, Pallas kernels for 0% -> 0%
where the time goes in v1:
time: 414 us; the launch traced here: 413 us
  blocking collectives  201 us (49%)
  waiting for transfers between devices  85.7 us (21%)
  starting transfers between devices  82.2 us (20%)
  Pallas kernels  16.3 us (4%)
  local copies, waits for them, and re-layouts  10.3 us (2%)
  other arithmetic  9.13 us (2%)
  between operations  4.78 us (1%)
    all_to_all x2, blocking collectives, with_transpose(): lax.all_to_all(pieces, yrep, 0, 0, axis_index_groups=skewed, tiled=True)  60.3 us
    all_to_all x2, blocking collectives, with_plain(): lax.all_to_all(to_all(piece, nrep), yrep, 0, 0, axis_index_groups=skewed,...  39.7 us
    all_to_all x1, blocking collectives, with_plain(): panels = lax.all_to_all(panels, 'q', 0, 0, tiled=True)  29.1 us
    all_to_all x1, blocking collectives, with_transpose(): parts = lax.all_to_all(parts, 'q', 0, 0, tiled=True).astype(F32)  28.2 us
    all_to_all x1, blocking collectives, on_device(): sums = lax.all_to_all(to_all(sums, nblk), BLK, 0, 0, tiled=True)  27.6 us
    all_to_all x2, waiting for transfers between devices, with_plain(): chips = lax.all_to_all(to_all(chip, nzh), 'zh', 0, 0, tiled=True)  22.4 us
    all_to_all x1, waiting for transfers between devices, with_plain(): panels = lax.all_to_all(panels, 'q', 0, 0, tiled=True)  19.6 us
    all_to_all x1, waiting for transfers between devices, with_transpose(): parts = lax.all_to_all(parts, 'q', 0, 0, tiled=True).astype(F32)  17.5 us
  transfers between devices with their start and end apart: 13, of which 12 were waited for; matrix products, arithmetic and copies ran while one was open for 0% of the time, Pallas kernels for 0%

profile of v1, /device:TPU:1, one launch (start us, length us, event | category | flops | bytes accessed | tf_op | source)
XLA Modules:
  0.0 412.9 jit_solution(12903140870455643049)
XLA Ops:
  0.7 0.8 copy.31
  1.6 0.8 copy.30
  2.5 1.5 fusion.4
  4.0 1.0 convolution_convert_fusion.panel_ref
  5.0 0.6 pad_add_fusion.2
  5.6 4.1 shard_map.102
  9.7 8.5 %all-to-all-start = ((bf16[12,512,128]{2,1,0:T(8,128)(2,1)}), bf16[12,512,128]{2,1,0:T(8,128)(2,1)S(1)}, u32[]{:S(2)}, u32[]{:S(2)}) async-start(bf16[12,512,128]{2,1,0:T(8,128)(2,1)} %shard_map.102), calls=%async_computation | async-start | bytes 3145728 | tf_op jit(solution)/shard_map/all_to_all | solution.py:103
  18.2 17.5 %all-to-all-done = bf16[12,512,128]{2,1,0:T(8,128)(2,1)S(1)} async-done(((bf16[12,512,128]{2,1,0:T(8,128)(2,1)}), bf16[12,512,128]{2,1,0:T(8,128)(2,1)S(1)}, u32[]{:S(2)}, u32[]{:S(2)}) %all-to-all-start) | async-done | bytes 1572896 | tf_op jit(solution)/shard_map/all_to_all | solution.py:103
  35.7 0.6 fusion.1
  36.4 14.2 %collective-permute-start = (bf16[512,128]{1,0:T(8,128)(2,1)S(1)}, bf16[512,128]{1,0:T(8,128)(2,1)S(1)}, u32[]{:S(2)}, u32[]{:S(2)}) collective-permute-start(bf16[512,128]{1,0:T(8,128)(2,1)S(1)} %get-tuple-element.38), channel_id=1, source_target_pairs={{96,0},{192,96},{288,192},{384,288},{480,384},{576,480},{672,576},... | collective-permute-start | bytes 393224 | tf_op jit(solution)/shard_map/ppermute | solution.py:105
  50.6 1.9 collective-permute-done
  52.5 34.4 %all_to_all.65 = bf16[8,64,128]{2,1,0:T(8,128)(2,1)S(1)} all-to-all(bf16[8,64,128]{2,1,0:T(8,128)(2,1)S(1)} %bitcast.36), channel_id=1, replica_groups={{0,97,194,291,388,485,582,679},{96,193,290,387,484,581,678,7},{192,289,..., dimensions={0} | all-to-all | bytes 262144 | tf_op jit(solution)/shard_map/all_to_all | solution.py:108
  87.0 19.9 %all_to_all.66 = bf16[8,64,128]{2,1,0:T(8,128)(2,1)S(1)} all-to-all(bf16[8,64,128]{2,1,0:T(8,128)(2,1)S(1)} %broadcast_in_dim.133), channel_id=1, replica_groups={{0,97,194,291,388,485,582,679},{96,193,290,387,484,581,678,7},{192,289,..., dimensions={0} | all-to-all | bytes 262144 | tf_op jit(solution)/shard_map/all_to_all | solution.py:112
  106.9 3.7 collective-permute-start.1
  110.7 3.2 collective-permute-done.1
  113.8 1.3 broadcast_select_fusion.1
  115.2 4.3 %all-to-all-start.3 = ((bf16[12,512,128]{2,1,0:T(8,128)(2,1)}), bf16[12,512,128]{2,1,0:T(8,128)(2,1)S(1)}, u32[]{:S(2)}, u32[]{:S(2)}) async-start(bf16[12,512,128]{2,1,0:T(8,128)(2,1)} %broadcast_select_fusion.1), calls=%async_computation.3 | async-start | bytes 3145728 | tf_op jit(solution)/shard_map/all_to_all | solution.py:117
  119.5 0.6 pad_add_fusion.index_ref
  120.1 19.6 %all-to-all-done.3.panels_ref = bf16[12,512,128]{2,1,0:T(8,128)(2,1)S(1)} async-done(((bf16[12,512,128]{2,1,0:T(8,128)(2,1)}), bf16[12,512,128]{2,1,0:T(8,128)(2,1)S(1)}, u32[]{:S(2)}, u32[]{:S(2)}) %all-to-all-start.3) | async-done | bytes 1572896 | tf_op jit(solution)/shard_map/all_to_all | solution.py:117
  139.7 1.2 copy-done.1
  140.8 4.1 shard_map.103
  144.9 0.9 dynamic-slice_convert_fusion.1
  145.9 10.3 %collective-permute-start.2 = (bf16[256,128]{1,0:T(8,128)(2,1)S(1)}, bf16[256,128]{1,0:T(8,128)(2,1)S(1)}, u32[]{:S(2)}, u32[]{:S(2)}) collective-permute-start(bf16[256,128]{1,0:T(8,128)(2,1)S(1)} %dynamic-slice_convert_fusion.1), channel_id=1, source_target_pairs={{0,1},{1,0},{2,3},{3,2},{4,5},{5,4},{6,7},{7,6},{8,9},{9,8},{10,11... | collective-permute-start | bytes 196616 | tf_op jit(solution)/shard_map/ppermute | solution.py:123
  156.2 0.9 collective-permute-done.2
  157.1 0.9 add_convert_fusion.4
  158.0 0.7 broadcast_in_dim.137
  158.7 3.8 all-to-all-start.4
  162.6 10.9 %all-to-all-done.4 = bf16[4,256,128]{2,1,0:T(8,128)(2,1)S(1)} async-done(((bf16[4,256,128]{2,1,0:T(8,128)(2,1)}), bf16[4,256,128]{2,1,0:T(8,128)(2,1)S(1)}, u32[]{:S(2)}, u32[]{:S(2)}) %all-to-all-start.4) | async-done | bytes 262176 | tf_op jit(solution)/shard_map/all_to_all | solution.py:124
  173.7 0.3 select_reduce_fusion
  174.1 6.6 %collective-permute-start.3 = (bf16[2,256,128]{2,1,0:T(8,128)(2,1)S(1)}, bf16[2,256,128]{2,1,0:T(8,128)(2,1)S(1)}, u32[]{:S(2)}, u32[]{:S(2)}) collective-permute-start(bf16[2,256,128]{2,1,0:T(8,128)(2,1)S(1)} %pad_maximum_fusion), channel_id=1, source_target_pairs={{0,1},{1,0},{2,3},{3,2},{4,5},{5,4},{6,7},{7,6},{8,9},{9,8},{10,11... | collective-permute-start | bytes 393224 | tf_op jit(solution)/shard_map/ppermute | solution.py:128
  180.7 1.0 collective-permute-done.3
  181.8 0.7 slice_bitcast_fusion
  182.5 4.1 shard_map.104
  186.6 28.2 %all_to_all.67 = bf16[12,512,128]{2,1,0:T(8,128)(2,1)S(1)} all-to-all(bf16[12,512,128]{2,1,0:T(8,128)(2,1)} %shard_map.104), channel_id=1, replica_groups=mesh['y'=8,'q'=12,'zh'=4,'c'=2] {'q'}, dimensions={0} | all-to-all | bytes 3145728 | tf_op jit(solution)/shard_map/all_to_all | solution.py:103
  214.8 0.6 fusion.3
  215.4 2.3 collective-permute-start.4
  217.7 5.4 %collective-permute-done.4 = bf16[512,128]{1,0:T(8,128)(2,1)S(1)} collective-permute-done((bf16[512,128]{1,0:T(8,128)(2,1)S(1)}, bf16[512,128]{1,0:T(8,128)(2,1)S(1)}, u32[]{:S(2)}, u32[]{:S(2)}) %collective-permute-start.4) | collective-permute-done | bytes 131104 | tf_op jit(solution)/shard_map/ppermute | solution.py:105
  223.1 25.8 %all_to_all.68 = bf16[8,64,128]{2,1,0:T(8,128)(2,1)S(1)} all-to-all(bf16[8,64,128]{2,1,0:T(8,128)(2,1)S(1)} %bitcast.37), channel_id=1, replica_groups={{0,97,194,291,388,485,582,679},{96,193,290,387,484,581,678,7},{192,289,..., dimensions={0} | all-to-all | bytes 262144 | tf_op jit(solution)/shard_map/all_to_all | solution.py:108
  249.0 19.8 %all_to_all.69 = bf16[8,64,128]{2,1,0:T(8,128)(2,1)S(1)} all-to-all(bf16[8,64,128]{2,1,0:T(8,128)(2,1)S(1)} %broadcast_in_dim.138), channel_id=1, replica_groups={{0,97,194,291,388,485,582,679},{96,193,290,387,484,581,678,7},{192,289,..., dimensions={0} | all-to-all | bytes 262144 | tf_op jit(solution)/shard_map/all_to_all | solution.py:112
  268.8 4.4 %collective-permute-start.5 = (bf16[512,128]{1,0:T(8,128)(2,1)S(1)}, bf16[512,128]{1,0:T(8,128)(2,1)S(1)}, u32[]{:S(2)}, u32[]{:S(2)}) collective-permute-start(bf16[512,128]{1,0:T(8,128)(2,1)S(1)} %bitcast.38), channel_id=1, source_target_pairs={{0,96},{96,192},{192,288},{288,384},{384,480},{480,576},{576,672},... | collective-permute-start | bytes 393224 | tf_op jit(solution)/shard_map/ppermute | solution.py:115
  273.2 2.5 collective-permute-done.5
  275.9 29.1 %all_to_all.70.panels_ref = bf16[12,512,128]{2,1,0:T(8,128)(2,1)} all-to-all(bf16[12,512,128]{2,1,0:T(8,128)(2,1)S(1)} %broadcast_select_fusion), channel_id=1, replica_groups=mesh['y'=8,'q'=12,'zh'=4,'c'=2] {'q'}, dimensions={0} | all-to-all | bytes 3145728 | tf_op jit(solution)/shard_map/all_to_all | solution.py:117
  305.0 4.1 shard_map.105
  309.1 0.9 dynamic-slice_convert_fusion
  310.0 6.0 %collective-permute-start.6 = (bf16[256,128]{1,0:T(8,128)(2,1)S(1)}, bf16[256,128]{1,0:T(8,128)(2,1)S(1)}, u32[]{:S(2)}, u32[]{:S(2)}) collective-permute-start(bf16[256,128]{1,0:T(8,128)(2,1)S(1)} %dynamic-slice_convert_fusion), channel_id=1, source_target_pairs={{0,1},{1,0},{2,3},{3,2},{4,5},{5,4},{6,7},{7,6},{8,9},{9,8},{10,11... | collective-permute-start | bytes 196616 | tf_op jit(solution)/shard_map/ppermute | solution.py:123
  316.0 0.9 collective-permute-done.6
  316.9 0.9 add_convert_fusion.3
  317.8 0.7 broadcast_in_dim.142
  318.6 3.4 all-to-all-start.9
  322.0 11.5 %all-to-all-done.9 = bf16[4,256,128]{2,1,0:T(8,128)(2,1)S(1)} async-done(((bf16[4,256,128]{2,1,0:T(8,128)(2,1)}), bf16[4,256,128]{2,1,0:T(8,128)(2,1)S(1)}, u32[]{:S(2)}, u32[]{:S(2)}) %all-to-all-start.9) | async-done | bytes 262176 | tf_op jit(solution)/shard_map/all_to_all | solution.py:124
  333.7 8.0 %collective-permute-start.7 = (bf16[256,128]{1,0:T(8,128)(2,1)S(1)}, bf16[256,128]{1,0:T(8,128)(2,1)S(1)}, u32[]{:S(2)}, u32[]{:S(2)}) collective-permute-start(bf16[256,128]{1,0:T(8,128)(2,1)S(1)} %add_convert_fusion.2), channel_id=1, source_target_pairs={{0,1},{1,0},{2,3},{3,2},{4,5},{5,4},{6,7},{7,6},{8,9},{9,8},{10,11... | collective-permute-start | bytes 196616 | tf_op jit(solution)/shard_map/ppermute | solution.py:128
  341.7 0.6 subtract_reduce_fusion
  343.0 0.3 fusion.6
  343.5 0.7 select_maximum_fusion
  344.2 6.7 %all-to-all-start.10 = ((f32[96,4,128]{2,1,0:T(4,128)}), f32[96,4,128]{2,1,0:T(4,128)S(1)}, u32[]{:S(2)}, u32[]{:S(2)}) async-start(f32[96,4,128]{2,1,0:T(4,128)} %bitcast.12), calls=%async_computation.10 | async-start | bytes 393216 | tf_op jit(solution)/shard_map/all_to_all | solution.py:174
  350.9 10.4 %all-to-all-done.10 = f32[96,4,128]{2,1,0:T(4,128)S(1)} async-done(((f32[96,4,128]{2,1,0:T(4,128)}), f32[96,4,128]{2,1,0:T(4,128)S(1)}, u32[]{:S(2)}, u32[]{:S(2)}) %all-to-all-start.10) | async-done | bytes 196640 | tf_op jit(solution)/shard_map/all_to_all | solution.py:174
  361.5 0.5 slice.36
  363.4 16.5 %all_to_all.71 = bf16[8,4,128]{2,1,0:T(4,128)(2,1)S(1)} all-to-all(bf16[8,4,128]{2,1,0:T(4,128)(2,1)S(1)} %broadcast_in_dim.148), channel_id=1, replica_groups=mesh['y'=8,'q'=12,'zh'=4,'c'=2] {'zh','c'}, dimensions={0} | all-to-all | bytes 16384 | tf_op jit(solution)/shard_map/all_to_all | solution.py:185
  379.9 0.2 broadcast_in_dim.149
  380.1 27.6 %all_to_all.72 = bf16[96,8,4,128]{3,2,1,0:T(4,128)(2,1)S(1)} all-to-all(bf16[96,8,4,128]{3,2,1,0:T(4,128)(2,1)S(1)} %broadcast_in_dim.149), channel_id=1, replica_groups=mesh['y'=8,'q'=12,'zh'=4,'c'=2] {'y','q'}, dimensions={0} | all-to-all | bytes 1572864 | tf_op jit(solution)/shard_map/all_to_all | solution.py:186
  407.8 0.2 copy_convert_fusion
  408.1 0.6 slice_reduce_fusion
  409.1 1.3 copy.35
  410.4 0.8 copy.34
  (42 shorter events, 2.1 us)
Async XLA Ops:
  0.6 1.8 copy-start
  0.6 3.3 copy-start.3
  9.7 26.0 %all-to-all-start = ((bf16[12,512,128]{2,1,0:T(8,128)(2,1)}), bf16[12,512,128]{2,1,0:T(8,128)(2,1)S(1)}, u32[]{:S(2)}, u32[]{:S(2)}) async-start(bf16[12,512,128]{2,1,0:T(8,128)(2,1)} %shard_map.102), calls=%async_computation | async-start | bytes 3145728 | tf_op jit(solution)/shard_map/all_to_all | solution.py:103
  36.4 16.1 %collective-permute-start = (bf16[512,128]{1,0:T(8,128)(2,1)S(1)}, bf16[512,128]{1,0:T(8,128)(2,1)S(1)}, u32[]{:S(2)}, u32[]{:S(2)}) collective-permute-start(bf16[512,128]{1,0:T(8,128)(2,1)S(1)} %get-tuple-element.38), channel_id=1, source_target_pairs={{96,0},{192,96},{288,192},{384,288},{480,384},{576,480},{672,576},... | collective-permute-start | bytes 393224 | tf_op jit(solution)/shard_map/ppermute | solution.py:105
  106.9 6.9 %collective-permute-start.1 = (bf16[512,128]{1,0:T(8,128)(2,1)S(1)}, bf16[512,128]{1,0:T(8,128)(2,1)S(1)}, u32[]{:S(2)}, u32[]{:S(2)}) collective-permute-start(bf16[512,128]{1,0:T(8,128)(2,1)S(1)} %bitcast.40), channel_id=1, source_target_pairs={{0,96},{96,192},{192,288},{288,384},{384,480},{480,576},{576,672},... | collective-permute-start | bytes 393224 | tf_op jit(solution)/shard_map/ppermute | solution.py:115
  115.2 24.5 %all-to-all-start.3 = ((bf16[12,512,128]{2,1,0:T(8,128)(2,1)}), bf16[12,512,128]{2,1,0:T(8,128)(2,1)S(1)}, u32[]{:S(2)}, u32[]{:S(2)}) async-start(bf16[12,512,128]{2,1,0:T(8,128)(2,1)} %broadcast_select_fusion.1), calls=%async_computation.3 | async-start | bytes 3145728 | tf_op jit(solution)/shard_map/all_to_all | solution.py:117
  120.1 42.5 %copy-start.4 = (s32[512]{0:T(512)S(1)}, s32[512]{0:T(512)}, u32[]{:S(2)}) copy-start(s32[512]{0:T(512)} %param.10) | copy-start | bytes 6148
  139.7 1.2 copy-start.1
  144.9 28.6 %copy-start.2 = (bf16[512,128]{1,0:T(8,128)(2,1)S(1)}, bf16[512,128]{1,0:T(8,128)(2,1)}, u32[]{:S(2)}) copy-start(bf16[512,128]{1,0:T(8,128)(2,1)} %convolution_convert_fusion.panel_ref) | copy-start | bytes 393220
  145.9 11.2 %collective-permute-start.2 = (bf16[256,128]{1,0:T(8,128)(2,1)S(1)}, bf16[256,128]{1,0:T(8,128)(2,1)S(1)}, u32[]{:S(2)}, u32[]{:S(2)}) collective-permute-start(bf16[256,128]{1,0:T(8,128)(2,1)S(1)} %dynamic-slice_convert_fusion.1), channel_id=1, source_target_pairs={{0,1},{1,0},{2,3},{3,2},{4,5},{5,4},{6,7},{7,6},{8,9},{9,8},{10,11... | collective-permute-start | bytes 196616 | tf_op jit(solution)/shard_map/ppermute | solution.py:123
  158.7 14.8 %all-to-all-start.4 = ((bf16[4,256,128]{2,1,0:T(8,128)(2,1)}), bf16[4,256,128]{2,1,0:T(8,128)(2,1)S(1)}, u32[]{:S(2)}, u32[]{:S(2)}) async-start(bf16[4,256,128]{2,1,0:T(8,128)(2,1)} %broadcast_in_dim.137), calls=%async_computation.4 | async-start | bytes 524288 | tf_op jit(solution)/shard_map/all_to_all | solution.py:124
  174.1 7.6 %collective-permute-start.3 = (bf16[2,256,128]{2,1,0:T(8,128)(2,1)S(1)}, bf16[2,256,128]{2,1,0:T(8,128)(2,1)S(1)}, u32[]{:S(2)}, u32[]{:S(2)}) collective-permute-start(bf16[2,256,128]{2,1,0:T(8,128)(2,1)S(1)} %pad_maximum_fusion), channel_id=1, source_target_pairs={{0,1},{1,0},{2,3},{3,2},{4,5},{5,4},{6,7},{7,6},{8,9},{9,8},{10,11... | collective-permute-start | bytes 393224 | tf_op jit(solution)/shard_map/ppermute | solution.py:128
  215.4 7.7 %collective-permute-start.4 = (bf16[512,128]{1,0:T(8,128)(2,1)S(1)}, bf16[512,128]{1,0:T(8,128)(2,1)S(1)}, u32[]{:S(2)}, u32[]{:S(2)}) collective-permute-start(bf16[512,128]{1,0:T(8,128)(2,1)S(1)} %get-tuple-element.36), channel_id=1, source_target_pairs={{96,0},{192,96},{288,192},{384,288},{480,384},{576,480},{672,576},... | collective-permute-start | bytes 393224 | tf_op jit(solution)/shard_map/ppermute | solution.py:105
  268.8 6.9 %collective-permute-start.5 = (bf16[512,128]{1,0:T(8,128)(2,1)S(1)}, bf16[512,128]{1,0:T(8,128)(2,1)S(1)}, u32[]{:S(2)}, u32[]{:S(2)}) collective-permute-start(bf16[512,128]{1,0:T(8,128)(2,1)S(1)} %bitcast.38), channel_id=1, source_target_pairs={{0,96},{96,192},{192,288},{288,384},{384,480},{480,576},{576,672},... | collective-permute-start | bytes 393224 | tf_op jit(solution)/shard_map/ppermute | solution.py:115
  310.0 6.9 %collective-permute-start.6 = (bf16[256,128]{1,0:T(8,128)(2,1)S(1)}, bf16[256,128]{1,0:T(8,128)(2,1)S(1)}, u32[]{:S(2)}, u32[]{:S(2)}) collective-permute-start(bf16[256,128]{1,0:T(8,128)(2,1)S(1)} %dynamic-slice_convert_fusion), channel_id=1, source_target_pairs={{0,1},{1,0},{2,3},{3,2},{4,5},{5,4},{6,7},{7,6},{8,9},{9,8},{10,11... | collective-permute-start | bytes 196616 | tf_op jit(solution)/shard_map/ppermute | solution.py:123
  318.6 14.9 %all-to-all-start.9 = ((bf16[4,256,128]{2,1,0:T(8,128)(2,1)}), bf16[4,256,128]{2,1,0:T(8,128)(2,1)S(1)}, u32[]{:S(2)}, u32[]{:S(2)}) async-start(bf16[4,256,128]{2,1,0:T(8,128)(2,1)} %broadcast_in_dim.142), calls=%async_computation.9 | async-start | bytes 524288 | tf_op jit(solution)/shard_map/all_to_all | solution.py:124
  333.7 9.3 %collective-permute-start.7 = (bf16[256,128]{1,0:T(8,128)(2,1)S(1)}, bf16[256,128]{1,0:T(8,128)(2,1)S(1)}, u32[]{:S(2)}, u32[]{:S(2)}) collective-permute-start(bf16[256,128]{1,0:T(8,128)(2,1)S(1)} %add_convert_fusion.2), channel_id=1, source_target_pairs={{0,1},{1,0},{2,3},{3,2},{4,5},{5,4},{6,7},{7,6},{8,9},{9,8},{10,11... | collective-permute-start | bytes 196616 | tf_op jit(solution)/shard_map/ppermute | solution.py:128
  344.2 17.1 %all-to-all-start.10 = ((f32[96,4,128]{2,1,0:T(4,128)}), f32[96,4,128]{2,1,0:T(4,128)S(1)}, u32[]{:S(2)}, u32[]{:S(2)}) async-start(f32[96,4,128]{2,1,0:T(4,128)} %bitcast.12), calls=%async_computation.10 | async-start | bytes 393216 | tf_op jit(solution)/shard_map/all_to_all | solution.py:174

commit v2 on v1

v2 whole, which is shorter than its diff:
```python
import functools
import math

import jax
import jax.numpy as jnp
from jax import lax
from jax.experimental import pallas as pl
from jax.experimental.pallas import tpu as pltpu
from jax.sharding import Mesh
from jax.sharding import PartitionSpec as P

ALPHA = 0.1
BF = jnp.bfloat16
F32 = jnp.float32
REP = ("zh", "c")
BLK = ("y", "q")


def scatter_kernel(place_ref, rows_ref, cols_ref, tiles_ref, panel_ref, out_ref):
    steps, slots, width, _ = tiles_ref.shape
    blocks = out_ref.shape[1] // width
    q = place_ref[0]
    share = jnp.where(place_ref[2] == 1, ALPHA / (1.0 - ALPHA), 0.0).astype(F32)
    for t in range(steps):
        place = lax.rem(q + (steps - t), steps)
        products = []
        for p in range(slots):
            rows = pl.ds(pl.multiple_of(rows_ref[p, t] * width, width), width)
            products.append(
                lax.dot_general(
                    tiles_ref[t, p],
                    panel_ref[rows, :],
                    (((0,), (0,)), ((), ())),
                    preferred_element_type=F32,
                )
            )
        for b in range(blocks):
            total = jnp.zeros(products[0].shape, F32)
            for p in range(slots):
                total = total + jnp.where(cols_ref[p, t] == b, products[p], 0.0)
            if t == 0:
                total = total + share * panel_ref[b * width : (b + 1) * width, :].astype(F32)
            out_ref[place, b * width : (b + 1) * width, :] = total.astype(BF)


def gather_kernel(
    place_ref, rows_ref, cols_ref, tiles_ref, panels_ref, mine_ref, away_ref, sum_ref
):
    steps, slots, width, _ = tiles_ref.shape
    half = mine_ref.shape[0]
    q = place_ref[0]
    c = place_ref[1]
    share = jnp.where(place_ref[2] == 1, ALPHA / (1.0 - ALPHA), 0.0).astype(F32)
    sum_ref[...] = share * panels_ref[q].astype(F32)
    for t in range(steps):
        place = lax.rem(q + (steps - t), steps)
        for p in range(slots):
            cols = pl.ds(pl.multiple_of(cols_ref[p, t] * width, width), width)
            rows = pl.ds(pl.multiple_of(rows_ref[p, t] * width, width), width)
            sum_ref[rows, :] += jnp.dot(
                tiles_ref[t, p], panels_ref[place, cols, :], preferred_element_type=F32
            )
    mine_ref[...] = sum_ref[pl.ds(pl.multiple_of(c * half, half), half), :]
    away_ref[...] = sum_ref[pl.ds(pl.multiple_of((1 - c) * half, half), half), :].astype(BF)


def call(kernel, outs, scalars, operands, scratch=(), interpret=False):
    vmem = pl.BlockSpec(memory_space=pltpu.VMEM)
    smem = pl.BlockSpec(memory_space=pltpu.SMEM)
    shapes = [jax.ShapeDtypeStruct(shape, dtype) for shape, dtype in outs]
    return pl.pallas_call(
        kernel,
        out_shape=shapes,
        in_specs=[smem] * len(scalars) + [vmem] * len(operands),
        out_specs=[vmem] * len(outs),
        scratch_shapes=list(scratch),
        interpret=interpret,
    )(*scalars, *operands)


def on_device(interpret, features, labels, w_first, w_second, block_rows, block_cols, block_vals):
    nodes_here = features.shape[0]
    classes = w_second.shape[1]
    ny, nq, nzh, nc = (lax.axis_size(a) for a in ("y", "q", "zh", "c"))
    nrep = nzh * nc
    nblk = ny * nq
    q_id = lax.axis_index("q")
    c_id = lax.axis_index("c")
    rep_id = lax.axis_index(REP)
    nodes = nodes_here * nblk
    tiles = block_vals[0, 0]
    steps = tiles.shape[0]
    half = nodes_here // nc
    yrep = ("y",) + REP
    fours = [
        [((y + zh * nc + c) % ny) * nrep + zh * nc + c for zh in range(nzh)]
        for y in range(ny)
        for c in range(nc)
    ]
    pairs = []
    for y in range(ny):
        for zh in range(nzh):
            here, there = y * nrep + zh * nc, ((y + 1) % ny) * nrep + zh * nc + 1
            pairs += [(here, there), (there, here)]
    cores = [(0, 1), (1, 0)]
    scalars = [block_rows[0, 0].T, block_cols[0, 0].T]

    def place(flag):
        return jnp.stack([q_id, c_id, flag]).astype(jnp.int32)

    plain = place(jnp.int32(0))
    diagonal = place((rep_id == 0).astype(jnp.int32))
    from_same = (jnp.arange(nq, dtype=jnp.int32) >= q_id)[:, None, None]

    def to_all(value, count):
        return jnp.broadcast_to(value[None], (count,) + value.shape)

    def halves(value):
        return [lax.dynamic_slice_in_dim(value, k * half, half, 0) for k in (c_id, 1 - c_id)]

    def whole(mine, other):
        return jnp.where(
            c_id == 0,
            jnp.concatenate([mine, other], axis=-2),
            jnp.concatenate([other, mine], axis=-2),
        )

    def with_transpose(panel, where):
        (parts,) = call(
            scatter_kernel,
            [((steps, nodes_here, classes), BF)],
            [where] + scalars,
            [tiles, panel],
            interpret=interpret,
        )
        parts = lax.all_to_all(parts, "q", 0, 0, tiled=True).astype(F32)
        before = jnp.sum(jnp.where(from_same, 0.0, parts), axis=0).astype(BF)
        moved = lax.ppermute(before, "y", [((i + 1) % ny, i) for i in range(ny)])
        total = jnp.sum(jnp.where(from_same, parts, 0.0), axis=0) + moved.astype(F32)
        mine, away = halves(total)
        pair = (mine + lax.ppermute(away.astype(BF), yrep, pairs).astype(F32)).astype(BF)
        group = lax.all_to_all(
            to_all(pair, nzh), yrep, 0, 0, axis_index_groups=fours, tiled=True
        )
        return ((1.0 - ALPHA) * jnp.sum(group.astype(F32), axis=0)).astype(BF)

    def with_plain(mine, where):
        here = whole(mine, lax.ppermute(mine, yrep, pairs))
        before = lax.ppermute(here, "y", [(i, (i + 1) % ny) for i in range(ny)])
        panels = jnp.where(from_same, here[None], before[None])
        panels = lax.all_to_all(panels, "q", 0, 0, tiled=True)
        mine, away = call(
            gather_kernel,
            [((half, classes), F32), ((half, classes), BF)],
            [where] + scalars,
            [tiles, panels],
            [pltpu.VMEM((nodes_here, classes), F32)],
            interpret=interpret,
        )
        chip = (mine + lax.ppermute(away, "c", cores).astype(F32)).astype(BF)
        chips = lax.all_to_all(to_all(chip, nzh), "zh", 0, 0, tiled=True)
        return (1.0 - ALPHA) * jnp.sum(chips.astype(F32), axis=0)

    hidden = jax.nn.relu(jnp.dot(features, w_first, preferred_element_type=F32)).astype(BF)
    base = jnp.dot(hidden, w_second, preferred_element_type=F32).astype(BF)
    base_half = lax.dynamic_slice_in_dim(base, c_id * half, half, 0)

    current = with_transpose(base, diagonal)
    mixed = with_plain(current, plain) + ALPHA * base_half.astype(F32)
    labels_half = lax.dynamic_slice_in_dim(labels, c_id * half, half, 0)
    onehot = (labels_half[:, None] == jnp.arange(classes, dtype=jnp.int32)[None, :]).astype(F32)
    top = jnp.max(mixed, axis=1, keepdims=True)
    grown = jnp.exp(mixed - top)
    mass = jnp.sum(grown, axis=1, keepdims=True)
    picked = jnp.sum(mixed * onehot, axis=1, keepdims=True)
    ce_sum = jnp.sum(jnp.log(mass) + top - picked)
    grad_out = (grown / mass - onehot) * (1.0 / math.sqrt(nodes))
    both = jnp.stack([grad_out.astype(BF), mixed.astype(BF)])
    both = whole(both, lax.ppermute(both, "c", cores))
    moving, logits = both[0], both[1]

    moving = with_transpose(moving, plain)
    grad_half = (with_plain(moving, diagonal) + ALPHA * grad_out).astype(BF)
    grad_b = whole(grad_half, lax.ppermute(grad_half, "c", cores))

    part = hidden.shape[1] // nc
    bands = part // classes
    hidden_part = lax.dynamic_slice_in_dim(hidden, c_id * part, part, 1)
    second_part = lax.dynamic_slice_in_dim(w_second, c_id * part, part, 0)
    back = lax.dot_general(grad_b, second_part, (((1,), (1,)), ((), ())), preferred_element_type=F32)
    grad_hidden = jnp.where(hidden_part > 0, back, 0.0).astype(BF)
    first = lax.dot_general(
        features, grad_hidden, (((0,), (0,)), ((), ())), preferred_element_type=F32
    ).astype(BF)
    second = lax.dot_general(
        hidden_part, grad_b, (((0,), (0,)), ((), ())), preferred_element_type=F32
    ).astype(BF)
    width = features.shape[1]
    used = bands * width + part
    each = -(-(used + 1) // nblk)
    each = -(-each // 16) * 16
    lanes = lax.broadcasted_iota(jnp.int32, (1, classes), 1)

    def in_terms(value):
        high = value.astype(BF)
        middle = (value - high.astype(F32)).astype(BF)
        low = (value - high.astype(F32) - middle.astype(F32)).astype(BF)
        zero = jnp.zeros((), BF)
        return jnp.where(
            lanes == 0, high, jnp.where(lanes == 1, middle, jnp.where(lanes == 2, low, zero))
        )

    sums = jnp.concatenate(
        [first[:, k * classes : (k + 1) * classes] for k in range(bands)]
        + [second, in_terms(ce_sum), jnp.zeros((each * nblk - used - 1, classes), BF)]
    )
    sums = lax.all_to_all(sums.reshape(nblk, each, classes), BLK, 0, 0, tiled=True)
    sums = jnp.sum(sums.astype(F32), axis=0)
    rows = lax.broadcasted_iota(jnp.int32, (each, classes), 0)
    is_loss = (lax.axis_index(BLK) * each + rows) == used
    loss_sum = jnp.sum(sums[used % each, :3])
    sums = jnp.where(is_loss, in_terms(loss_sum), sums.astype(BF))
    sums = lax.all_to_all(to_all(sums, nblk), BLK, 0, 0, tiled=True).reshape(nblk * each, classes)
    other = lax.ppermute(sums, "c", cores)
    first_core = jnp.where(c_id == 0, sums, other).astype(F32)
    second_core = jnp.where(c_id == 0, other, sums).astype(F32)
    grad_first = jnp.concatenate(
        [v[k * width : (k + 1) * width] for v in (first_core, second_core) for k in range(bands)],
        axis=1,
    )
    grad_second = jnp.concatenate([v[bands * width : used] for v in (first_core, second_core)])
    loss = (jnp.sum(first_core[used, :3]) + jnp.sum(second_core[used, :3])) / nodes
    return (logits, grad_first, grad_second, loss)


def solution(mesh, interpret=False):
    nblk, nrep = mesh.devices.shape
    cores = 2
    fine = Mesh(
        mesh.devices.reshape(nrep, nblk // nrep, nrep // cores, cores), ("y", "q", "zh", "c")
    )
    in_specs = (
        P(BLK, None),
        P(BLK),
        P(),
        P(),
        P(BLK, REP, None, None),
        P(BLK, REP, None, None),
        P(BLK, REP, None, None, None, None),
    )
    out_specs = (P(BLK, None), P(), P(), P())
    return jax.shard_map(
        functools.partial(on_device, interpret),
        mesh=fine,
        in_specs=in_specs,
        out_specs=out_specs,
        check_vma=False,
    )
```

time: 414 us -> 393 us (0.949)
  blocking collectives: 201 us -> 132 us
  waiting for transfers between devices: 85.7 us -> 112 us
  starting transfers between devices: 82.2 us -> 106 us
  local copies, waits for them, and re-layouts: 10.3 us -> 5.75 us
    all_to_all x6 -> x3, blocking collectives: 144 us -> 74.3 us  [the longest x2 54.4 us: with_transpose(): lax.all_to_all(to_all(pair, nzh), yrep, 0, 0, axis_index_groups=fours, ti...]
    ppermute x4 -> x9, starting transfers between devices: 30.9 us -> 58.1 us  [the longest x2 14.1 us: with_transpose(): lax.ppermute(away.astype(BF), yrep, pairs).astype(F32)]
    ppermute x4 -> x9, waiting for transfers between devices: 2.72 us -> 14.2 us  [the longest x2 4.99 us: with_plain(): here = whole(mine, lax.ppermute(mine, yrep, pairs))]
    all_to_all x1, waiting for transfers between devices: 19.6 us -> 26.6 us  [with_plain(): panels = lax.all_to_all(panels, 'q', 0, 0, tiled=True)]
    ppermute x2, waiting for transfers between devices: 5.71 us -> 12.5 us  [with_plain(): before = lax.ppermute(here, 'y', [(i, (i + 1) % ny) for i in range(ny)])]
    ppermute x2, starting transfers between devices: 8.1 us -> 3.84 us  [with_plain(): before = lax.ppermute(here, 'y', [(i, (i + 1) % ny) for i in range(ny)])]
  transfers between devices with their start and end apart: 13 -> 18, of which waited for: 12 -> 18; matrix products, arithmetic and copies ran while one was open for 0% -> 0% of each run, Pallas kernels for 0% -> 0%
where the time goes in v2:
time: 393 us; the launch traced here: 392 us
  blocking collectives  132 us (34%)
  waiting for transfers between devices  112 us (28%)
  starting transfers between devices  106 us (27%)
  Pallas kernels  16.3 us (4%)
  other arithmetic  10.9 us (3%)
  between operations  6.16 us (2%)
  local copies, waits for them, and re-layouts  5.75 us (1%)
    all_to_all x2, blocking collectives, with_transpose(): lax.all_to_all(to_all(pair, nzh), yrep, 0, 0, axis_index_groups=fours, ti...  54.4 us
    all_to_all x1, blocking collectives, with_plain(): panels = lax.all_to_all(panels, 'q', 0, 0, tiled=True)  29 us
    all_to_all x1, blocking collectives, with_transpose(): parts = lax.all_to_all(parts, 'q', 0, 0, tiled=True).astype(F32)  28.8 us
    all_to_all x1, waiting for transfers between devices, with_plain(): panels = lax.all_to_all(panels, 'q', 0, 0, tiled=True)  26.6 us
    all_to_all x2, waiting for transfers between devices, with_plain(): chips = lax.all_to_all(to_all(chip, nzh), 'zh', 0, 0, tiled=True)  21.2 us
    all_to_all x1, blocking collectives, on_device(): lax.all_to_all(to_all(sums, nblk), BLK, 0, 0, tiled=True)  19.9 us
    all_to_all x1, waiting for transfers between devices, with_transpose(): parts = lax.all_to_all(parts, 'q', 0, 0, tiled=True).astype(F32)  17.5 us
    pallas_call x4, Pallas kernels, call(): pl.pallas_call(kernel, out_shape=shapes, in_specs=[smem] * len(scalars) +...  16.3 us
  transfers between devices with their start and end apart: 18, of which 18 were waited for; matrix products, arithmetic and copies ran while one was open for 0% of the time, Pallas kernels for 0%

profile of v2, /device:TPU:1, one launch (start us, length us, event | category | flops | bytes accessed | tf_op | source)
XLA Modules:
  0.0 391.9 jit_solution(2642337214075116816)
XLA Ops:
  0.7 1.0 copy-done
  1.7 1.5 fusion.4
  3.2 1.0 convolution_convert_fusion.1.panel_ref
  4.1 0.7 pad_add_fusion.2.place_ref
  4.8 4.1 %shard_map.102 = bf16[12,512,128]{2,1,0:T(8,128)(2,1)} custom-call(s32[3]{0:T(128)} %pad_add_fusion.2.place_ref, s32[2,12]{1,0:T(2,128)} %bitcast.34, s32[2,12]{1,0:T(2,128)} %bitcast.38, bf16[12,2,256,256]{3,2,1,0:T(8,128)(2,1)} %bitcast.29, bf16[512,128]{1,0:T(8,128)(2,1)} %convolution_convert_fusion.1.panel_ref), custom_call_target="tpu_custom_call" | custom-call | tf_op jit(solution)/shard_map/pallas_call | solution.py:71
  8.9 8.5 %all-to-all-start = ((bf16[12,512,128]{2,1,0:T(8,128)(2,1)}), bf16[12,512,128]{2,1,0:T(8,128)(2,1)S(1)}, u32[]{:S(2)}, u32[]{:S(2)}) async-start(bf16[12,512,128]{2,1,0:T(8,128)(2,1)} %shard_map.102), calls=%async_computation | async-start | bytes 3145728 | tf_op jit(solution)/shard_map/all_to_all | solution.py:136
  17.4 17.5 %all-to-all-done = bf16[12,512,128]{2,1,0:T(8,128)(2,1)S(1)} async-done(((bf16[12,512,128]{2,1,0:T(8,128)(2,1)}), bf16[12,512,128]{2,1,0:T(8,128)(2,1)S(1)}, u32[]{:S(2)}, u32[]{:S(2)}) %all-to-all-start) | async-done | bytes 1572896 | tf_op jit(solution)/shard_map/all_to_all | solution.py:136
  34.9 0.6 fusion.1
  35.5 14.2 %collective-permute-start = (bf16[512,128]{1,0:T(8,128)(2,1)S(1)}, bf16[512,128]{1,0:T(8,128)(2,1)S(1)}, u32[]{:S(2)}, u32[]{:S(2)}) collective-permute-start(bf16[512,128]{1,0:T(8,128)(2,1)S(1)} %get-tuple-element.14), channel_id=1, source_target_pairs={{96,0},{192,96},{288,192},{384,288},{480,384},{576,480},{672,576},... | collective-permute-start | bytes 393224 | tf_op jit(solution)/shard_map/ppermute | solution.py:138
  49.7 1.9 collective-permute-done
  51.7 8.2 %collective-permute-start.1 = (bf16[256,128]{1,0:T(8,128)(2,1)S(1)}, bf16[256,128]{1,0:T(8,128)(2,1)S(1)}, u32[]{:S(2)}, u32[]{:S(2)}) collective-permute-start(bf16[256,128]{1,0:T(8,128)(2,1)S(1)} %dynamic-slice_convert_fusion.1), channel_id=1, source_target_pairs={{0,97},{97,0},{2,99},{99,2},{4,101},{101,4},{6,103},{103,6},{96,19... | collective-permute-start | bytes 196616 | tf_op jit(solution)/shard_map/ppermute | solution.py:141
  59.9 1.9 collective-permute-done.1
  61.9 34.6 %all_to_all.50 = bf16[4,256,128]{2,1,0:T(8,128)(2,1)S(1)} all-to-all(bf16[4,256,128]{2,1,0:T(8,128)(2,1)S(1)} %broadcast_in_dim.147), channel_id=1, replica_groups={{0,194,388,582},{97,291,485,679},{96,290,484,678},{193,387,581,7},{192,..., dimensions={0} | all-to-all | bytes 524288 | tf_op jit(solution)/shard_map/all_to_all | solution.py:142
  96.6 3.7 collective-permute-start.2
  100.4 3.1 collective-permute-done.2
  103.5 1.9 collective-permute-start.3
  105.4 6.4 %collective-permute-done.3 = bf16[512,128]{1,0:T(8,128)(2,1)S(1)} collective-permute-done((bf16[512,128]{1,0:T(8,128)(2,1)S(1)}, bf16[512,128]{1,0:T(8,128)(2,1)S(1)}, u32[]{:S(2)}, u32[]{:S(2)}) %collective-permute-start.3) | collective-permute-done | bytes 131104 | tf_op jit(solution)/shard_map/ppermute | solution.py:149
  111.8 1.3 broadcast_select_fusion.1
  113.1 5.7 %all-to-all-start.2 = ((bf16[12,512,128]{2,1,0:T(8,128)(2,1)}), bf16[12,512,128]{2,1,0:T(8,128)(2,1)S(1)}, u32[]{:S(2)}, u32[]{:S(2)}) async-start(bf16[12,512,128]{2,1,0:T(8,128)(2,1)} %broadcast_select_fusion.1), calls=%async_computation.2 | async-start | bytes 3145728 | tf_op jit(solution)/shard_map/all_to_all | solution.py:151
  118.8 0.6 pad_add_fusion.place_ref
  119.4 26.6 %all-to-all-done.2.panels_ref = bf16[12,512,128]{2,1,0:T(8,128)(2,1)S(1)} async-done(((bf16[12,512,128]{2,1,0:T(8,128)(2,1)}), bf16[12,512,128]{2,1,0:T(8,128)(2,1)S(1)}, u32[]{:S(2)}, u32[]{:S(2)}) %all-to-all-start.2) | async-done | bytes 1572896 | tf_op jit(solution)/shard_map/all_to_all | solution.py:151
  146.1 1.2 copy-done.1
  147.2 4.0 %shard_map.103 = (f32[256,128]{1,0:T(8,128)}, bf16[256,128]{1,0:T(8,128)(2,1)}) custom-call(s32[3]{0:T(128)} %pad_add_fusion.place_ref, s32[2,12]{1,0:T(2,128)} %bitcast.35, s32[2,12]{1,0:T(2,128)} %bitcast.39, bf16[12,2,256,256]{3,2,1,0:T(8,128)(2,1)} %bitcast.30, bf16[12,512,128]{2,1,0:T(8,128)(2,1)} %copy-done.1), custom_call_target="tpu_custom_call" | custom-call | tf_op jit(solution)/shard_map/pallas_call | solution.py:71
  151.3 3.6 collective-permute-start.4
  154.8 1.1 collective-permute-done.4
  155.9 0.9 add_convert_fusion.3
  156.8 0.7 broadcast_in_dim.150
  157.6 3.4 all-to-all-start.3
  161.1 11.6 %all-to-all-done.3 = bf16[4,256,128]{2,1,0:T(8,128)(2,1)S(1)} async-done(((bf16[4,256,128]{2,1,0:T(8,128)(2,1)}), bf16[4,256,128]{2,1,0:T(8,128)(2,1)S(1)}, u32[]{:S(2)}, u32[]{:S(2)}) %all-to-all-start.3) | async-done | bytes 262176 | tf_op jit(solution)/shard_map/all_to_all | solution.py:161
  173.3 6.8 %collective-permute-start.5 = (bf16[2,256,128]{2,1,0:T(8,128)(2,1)S(1)}, bf16[2,256,128]{2,1,0:T(8,128)(2,1)S(1)}, u32[]{:S(2)}, u32[]{:S(2)}) collective-permute-start(bf16[2,256,128]{2,1,0:T(8,128)(2,1)S(1)} %pad_maximum_fusion.2), channel_id=1, source_target_pairs={{0,1},{1,0},{2,3},{3,2},{4,5},{5,4},{6,7},{7,6},{8,9},{9,8},{10,11... | collective-permute-start | bytes 393224 | tf_op jit(solution)/shard_map/ppermute | solution.py:179
  180.1 1.0 collective-permute-done.5
  181.2 0.7 slice_bitcast_fusion
  181.9 4.1 %shard_map.104 = bf16[12,512,128]{2,1,0:T(8,128)(2,1)} custom-call(s32[3]{0:T(128)} %pad_add_fusion.place_ref, s32[2,12]{1,0:T(2,128)} %bitcast.36, s32[2,12]{1,0:T(2,128)} %bitcast.40, bf16[12,2,256,256]{3,2,1,0:T(8,128)(2,1)} %bitcast.31, bf16[512,128]{1,0:T(8,128)(2,1)} %get-tuple-element.28.panel_ref), custom_call_target="tpu_custom_call" | custom-call | tf_op jit(solution)/shard_map/pallas_call | solution.py:71
  186.0 28.8 %all_to_all.51 = bf16[12,512,128]{2,1,0:T(8,128)(2,1)S(1)} all-to-all(bf16[12,512,128]{2,1,0:T(8,128)(2,1)} %shard_map.104), channel_id=1, replica_groups=mesh['y'=8,'q'=12,'zh'=4,'c'=2] {'q'}, dimensions={0} | all-to-all | bytes 3145728 | tf_op jit(solution)/shard_map/all_to_all | solution.py:136
  214.8 0.6 fusion.3
  215.4 1.9 collective-permute-start.6
  217.3 3.8 collective-permute-done.6
  221.2 5.9 %collective-permute-start.7 = (bf16[256,128]{1,0:T(8,128)(2,1)S(1)}, bf16[256,128]{1,0:T(8,128)(2,1)S(1)}, u32[]{:S(2)}, u32[]{:S(2)}) collective-permute-start(bf16[256,128]{1,0:T(8,128)(2,1)S(1)} %dynamic-slice_convert_fusion), channel_id=1, source_target_pairs={{0,97},{97,0},{2,99},{99,2},{4,101},{101,4},{6,103},{103,6},{96,19... | collective-permute-start | bytes 196616 | tf_op jit(solution)/shard_map/ppermute | solution.py:141
  227.1 1.9 collective-permute-done.7
  229.1 19.8 %all_to_all.52 = bf16[4,256,128]{2,1,0:T(8,128)(2,1)S(1)} all-to-all(bf16[4,256,128]{2,1,0:T(8,128)(2,1)S(1)} %broadcast_in_dim.151), channel_id=1, replica_groups={{0,194,388,582},{97,291,485,679},{96,290,484,678},{193,387,581,7},{192,..., dimensions={0} | all-to-all | bytes 524288 | tf_op jit(solution)/shard_map/all_to_all | solution.py:142
  248.9 9.9 %collective-permute-start.8 = (bf16[256,128]{1,0:T(8,128)(2,1)S(1)}, bf16[256,128]{1,0:T(8,128)(2,1)S(1)}, u32[]{:S(2)}, u32[]{:S(2)}) collective-permute-start(bf16[256,128]{1,0:T(8,128)(2,1)S(1)} %multiply_convert_fusion), channel_id=1, source_target_pairs={{0,97},{97,0},{2,99},{99,2},{4,101},{101,4},{6,103},{103,6},{96,19... | collective-permute-start | bytes 196616 | tf_op jit(solution)/shard_map/ppermute | solution.py:148
  258.9 1.9 collective-permute-done.8
  260.8 1.9 collective-permute-start.9
  262.8 6.2 %collective-permute-done.9 = bf16[512,128]{1,0:T(8,128)(2,1)S(1)} collective-permute-done((bf16[512,128]{1,0:T(8,128)(2,1)S(1)}, bf16[512,128]{1,0:T(8,128)(2,1)S(1)}, u32[]{:S(2)}, u32[]{:S(2)}) %collective-permute-start.9) | collective-permute-done | bytes 131104 | tf_op jit(solution)/shard_map/ppermute | solution.py:149
  269.1 29.0 %all_to_all.53.panels_ref = bf16[12,512,128]{2,1,0:T(8,128)(2,1)} all-to-all(bf16[12,512,128]{2,1,0:T(8,128)(2,1)S(1)} %broadcast_select_fusion), channel_id=1, replica_groups=mesh['y'=8,'q'=12,'zh'=4,'c'=2] {'q'}, dimensions={0} | all-to-all | bytes 3145728 | tf_op jit(solution)/shard_map/all_to_all | solution.py:151
  298.1 4.0 %shard_map.105 = (f32[256,128]{1,0:T(8,128)}, bf16[256,128]{1,0:T(8,128)(2,1)}) custom-call(s32[3]{0:T(128)} %pad_add_fusion.2.place_ref, s32[2,12]{1,0:T(2,128)} %bitcast.37, s32[2,12]{1,0:T(2,128)} %bitcast.41, bf16[12,2,256,256]{3,2,1,0:T(8,128)(2,1)} %bitcast.32, bf16[12,512,128]{2,1,0:T(8,128)(2,1)} %all_to_all.53.panels_ref), custom_call_target="tpu_custom_call" | custom-call | tf_op jit(solution)/shard_map/pallas_call | solution.py:71
  302.1 5.6 %collective-permute-start.10 = (bf16[256,128]{1,0:T(8,128)(2,1)}, bf16[256,128]{1,0:T(8,128)(2,1)S(1)}, u32[]{:S(2)}, u32[]{:S(2)}) collective-permute-start(bf16[256,128]{1,0:T(8,128)(2,1)} %get-tuple-element.11), channel_id=1, source_target_pairs={{0,1},{1,0},{2,3},{3,2},{4,5},{5,4},{6,7},{7,6},{8,9},{9,8},{10,11... | collective-permute-start | bytes 196616 | tf_op jit(solution)/shard_map/ppermute | solution.py:160
  307.8 1.1 collective-permute-done.10
  308.9 0.9 add_convert_fusion.1
  309.8 0.7 broadcast_in_dim.154
  310.5 3.4 all-to-all-start.7
  313.9 0.6 subtract_reduce_fusion
  315.9 9.6 %all-to-all-done.7 = bf16[4,256,128]{2,1,0:T(8,128)(2,1)S(1)} async-done(((bf16[4,256,128]{2,1,0:T(8,128)(2,1)}), bf16[4,256,128]{2,1,0:T(8,128)(2,1)S(1)}, u32[]{:S(2)}, u32[]{:S(2)}) %all-to-all-start.7) | async-done | bytes 262176 | tf_op jit(solution)/shard_map/all_to_all | solution.py:161
  325.7 8.0 %collective-permute-start.11 = (bf16[256,128]{1,0:T(8,128)(2,1)S(1)}, bf16[256,128]{1,0:T(8,128)(2,1)S(1)}, u32[]{:S(2)}, u32[]{:S(2)}) collective-permute-start(bf16[256,128]{1,0:T(8,128)(2,1)S(1)} %add_convert_fusion), channel_id=1, source_target_pairs={{0,1},{1,0},{2,3},{3,2},{4,5},{5,4},{6,7},{7,6},{8,9},{9,8},{10,11... | collective-permute-start | bytes 196616 | tf_op jit(solution)/shard_map/ppermute | solution.py:184
  333.7 0.9 collective-permute-done.11
  335.6 0.9 copy.15
  336.5 6.7 %all-to-all-start.8 = ((bf16[96,16,128]{2,1,0:T(8,128)(2,1)}), bf16[96,16,128]{2,1,0:T(8,128)(2,1)S(1)}, u32[]{:S(2)}, u32[]{:S(2)}) async-start(bf16[96,16,128]{2,1,0:T(8,128)(2,1)} %bitcast.15), calls=%async_computation.8 | async-start | bytes 786432 | tf_op jit(solution)/shard_map/all_to_all | solution.py:217
  343.3 13.8 %all-to-all-done.8 = bf16[96,16,128]{2,1,0:T(8,128)(2,1)S(1)} async-done(((bf16[96,16,128]{2,1,0:T(8,128)(2,1)}), bf16[96,16,128]{2,1,0:T(8,128)(2,1)S(1)}, u32[]{:S(2)}, u32[]{:S(2)}) %all-to-all-start.8) | async-done | bytes 393248 | tf_op jit(solution)/shard_map/all_to_all | solution.py:217
  359.3 19.9 %all_to_all.54 = bf16[96,16,128]{2,1,0:T(8,128)(2,1)S(1)} all-to-all(bf16[96,16,128]{2,1,0:T(8,128)(2,1)S(1)} %broadcast_in_dim.166), channel_id=1, replica_groups=mesh['y'=8,'q'=12,'zh'=4,'c'=2] {'y','q'}, dimensions={0} | all-to-all | bytes 786432 | tf_op jit(solution)/shard_map/all_to_all | solution.py:223
  379.2 6.4 %collective-permute-start.12 = (bf16[1536,128]{1,0:T(8,128)(2,1)S(1)}, bf16[1536,128]{1,0:T(8,128)(2,1)S(1)}, u32[]{:S(2)}, u32[]{:S(2)}) collective-permute-start(bf16[1536,128]{1,0:T(8,128)(2,1)S(1)} %bitcast.33), channel_id=1, source_target_pairs={{0,1},{1,0},{2,3},{3,2},{4,5},{5,4},{6,7},{7,6},{8,9},{9,8},{10,11... | collective-permute-start | bytes 1179656 | tf_op jit(solution)/shard_map/ppermute | solution.py:224
  385.5 1.3 collective-permute-done.12
  387.1 0.6 slice_reduce_fusion
  387.7 0.7 pad_maximum_fusion.1
  389.7 1.0 pad_maximum_fusion
  (49 shorter events, 3.6 us)
Async XLA Ops:
  0.6 1.0 copy-start
  0.6 2.5 copy-start.3
  8.9 26.0 %all-to-all-start = ((bf16[12,512,128]{2,1,0:T(8,128)(2,1)}), bf16[12,512,128]{2,1,0:T(8,128)(2,1)S(1)}, u32[]{:S(2)}, u32[]{:S(2)}) async-start(bf16[12,512,128]{2,1,0:T(8,128)(2,1)} %shard_map.102), calls=%async_computation | async-start | bytes 3145728 | tf_op jit(solution)/shard_map/all_to_all | solution.py:136
  35.5 16.1 %collective-permute-start = (bf16[512,128]{1,0:T(8,128)(2,1)S(1)}, bf16[512,128]{1,0:T(8,128)(2,1)S(1)}, u32[]{:S(2)}, u32[]{:S(2)}) collective-permute-start(bf16[512,128]{1,0:T(8,128)(2,1)S(1)} %get-tuple-element.14), channel_id=1, source_target_pairs={{96,0},{192,96},{288,192},{384,288},{480,384},{576,480},{672,576},... | collective-permute-start | bytes 393224 | tf_op jit(solution)/shard_map/ppermute | solution.py:138
  51.7 10.2 %collective-permute-start.1 = (bf16[256,128]{1,0:T(8,128)(2,1)S(1)}, bf16[256,128]{1,0:T(8,128)(2,1)S(1)}, u32[]{:S(2)}, u32[]{:S(2)}) collective-permute-start(bf16[256,128]{1,0:T(8,128)(2,1)S(1)} %dynamic-slice_convert_fusion.1), channel_id=1, source_target_pairs={{0,97},{97,0},{2,99},{99,2},{4,101},{101,4},{6,103},{103,6},{96,19... | collective-permute-start | bytes 196616 | tf_op jit(solution)/shard_map/ppermute | solution.py:141
  96.6 6.8 %collective-permute-start.2 = (bf16[256,128]{1,0:T(8,128)(2,1)S(1)}, bf16[256,128]{1,0:T(8,128)(2,1)S(1)}, u32[]{:S(2)}, u32[]{:S(2)}) collective-permute-start(bf16[256,128]{1,0:T(8,128)(2,1)S(1)} %multiply_convert_fusion.2), channel_id=1, source_target_pairs={{0,97},{97,0},{2,99},{99,2},{4,101},{101,4},{6,103},{103,6},{96,19... | collective-permute-start | bytes 196616 | tf_op jit(solution)/shard_map/ppermute | solution.py:148
  103.5 8.3 %collective-permute-start.3 = (bf16[512,128]{1,0:T(8,128)(2,1)S(1)}, bf16[512,128]{1,0:T(8,128)(2,1)S(1)}, u32[]{:S(2)}, u32[]{:S(2)}) collective-permute-start(bf16[512,128]{1,0:T(8,128)(2,1)S(1)} %maximum_select_fusion.1), channel_id=1, source_target_pairs={{0,96},{96,192},{192,288},{288,384},{384,480},{480,576},{576,672},... | collective-permute-start | bytes 393224 | tf_op jit(solution)/shard_map/ppermute | solution.py:149
  113.1 33.0 %all-to-all-start.2 = ((bf16[12,512,128]{2,1,0:T(8,128)(2,1)}), bf16[12,512,128]{2,1,0:T(8,128)(2,1)S(1)}, u32[]{:S(2)}, u32[]{:S(2)}) async-start(bf16[12,512,128]{2,1,0:T(8,128)(2,1)} %broadcast_select_fusion.1), calls=%async_computation.2 | async-start | bytes 3145728 | tf_op jit(solution)/shard_map/all_to_all | solution.py:151
  119.4 41.6 %copy-start.4 = (s32[512]{0:T(512)S(1)}, s32[512]{0:T(512)}, u32[]{:S(2)}) copy-start(s32[512]{0:T(512)} %param.8) | copy-start | bytes 6148
  119.4 53.2 %copy-start.2 = (bf16[512,128]{1,0:T(8,128)(2,1)S(1)}, bf16[512,128]{1,0:T(8,128)(2,1)}, u32[]{:S(2)}) copy-start(bf16[512,128]{1,0:T(8,128)(2,1)} %convolution_convert_fusion.1.panel_ref) | copy-start | bytes 393220
  146.1 1.2 copy-start.1
  151.3 4.6 %collective-permute-start.4 = (bf16[256,128]{1,0:T(8,128)(2,1)}, bf16[256,128]{1,0:T(8,128)(2,1)S(1)}, u32[]{:S(2)}, u32[]{:S(2)}) collective-permute-start(bf16[256,128]{1,0:T(8,128)(2,1)} %get-tuple-element.9), channel_id=1, source_target_pairs={{0,1},{1,0},{2,3},{3,2},{4,5},{5,4},{6,7},{7,6},{8,9},{9,8},{10,11... | collective-permute-start | bytes 196616 | tf_op jit(solution)/shard_map/ppermute | solution.py:160
  157.6 15.1 %all-to-all-start.3 = ((bf16[4,256,128]{2,1,0:T(8,128)(2,1)}), bf16[4,256,128]{2,1,0:T(8,128)(2,1)S(1)}, u32[]{:S(2)}, u32[]{:S(2)}) async-start(bf16[4,256,128]{2,1,0:T(8,128)(2,1)} %broadcast_in_dim.150), calls=%async_computation.3 | async-start | bytes 524288 | tf_op jit(solution)/shard_map/all_to_all | solution.py:161
  173.3 7.8 %collective-permute-start.5 = (bf16[2,256,128]{2,1,0:T(8,128)(2,1)S(1)}, bf16[2,256,128]{2,1,0:T(8,128)(2,1)S(1)}, u32[]{:S(2)}, u32[]{:S(2)}) collective-permute-start(bf16[2,256,128]{2,1,0:T(8,128)(2,1)S(1)} %pad_maximum_fusion.2), channel_id=1, source_target_pairs={{0,1},{1,0},{2,3},{3,2},{4,5},{5,4},{6,7},{7,6},{8,9},{9,8},{10,11... | collective-permute-start | bytes 393224 | tf_op jit(solution)/shard_map/ppermute | solution.py:179
  215.4 5.7 %collective-permute-start.6 = (bf16[512,128]{1,0:T(8,128)(2,1)S(1)}, bf16[512,128]{1,0:T(8,128)(2,1)S(1)}, u32[]{:S(2)}, u32[]{:S(2)}) collective-permute-start(bf16[512,128]{1,0:T(8,128)(2,1)S(1)} %get-tuple-element.12), channel_id=1, source_target_pairs={{96,0},{192,96},{288,192},{384,288},{480,384},{576,480},{672,576},... | collective-permute-start | bytes 393224 | tf_op jit(solution)/shard_map/ppermute | solution.py:138
  221.2 7.8 %collective-permute-start.7 = (bf16[256,128]{1,0:T(8,128)(2,1)S(1)}, bf16[256,128]{1,0:T(8,128)(2,1)S(1)}, u32[]{:S(2)}, u32[]{:S(2)}) collective-permute-start(bf16[256,128]{1,0:T(8,128)(2,1)S(1)} %dynamic-slice_convert_fusion), channel_id=1, source_target_pairs={{0,97},{97,0},{2,99},{99,2},{4,101},{101,4},{6,103},{103,6},{96,19... | collective-permute-start | bytes 196616 | tf_op jit(solution)/shard_map/ppermute | solution.py:141
  248.9 11.9 %collective-permute-start.8 = (bf16[256,128]{1,0:T(8,128)(2,1)S(1)}, bf16[256,128]{1,0:T(8,128)(2,1)S(1)}, u32[]{:S(2)}, u32[]{:S(2)}) collective-permute-start(bf16[256,128]{1,0:T(8,128)(2,1)S(1)} %multiply_convert_fusion), channel_id=1, source_target_pairs={{0,97},{97,0},{2,99},{99,2},{4,101},{101,4},{6,103},{103,6},{96,19... | collective-permute-start | bytes 196616 | tf_op jit(solution)/shard_map/ppermute | solution.py:148
  260.8 8.1 %collective-permute-start.9 = (bf16[512,128]{1,0:T(8,128)(2,1)S(1)}, bf16[512,128]{1,0:T(8,128)(2,1)S(1)}, u32[]{:S(2)}, u32[]{:S(2)}) collective-permute-start(bf16[512,128]{1,0:T(8,128)(2,1)S(1)} %maximum_select_fusion.2), channel_id=1, source_target_pairs={{0,96},{96,192},{192,288},{288,384},{384,480},{480,576},{576,672},... | collective-permute-start | bytes 393224 | tf_op jit(solution)/shard_map/ppermute | solution.py:149
  302.1 6.7 %collective-permute-start.10 = (bf16[256,128]{1,0:T(8,128)(2,1)}, bf16[256,128]{1,0:T(8,128)(2,1)S(1)}, u32[]{:S(2)}, u32[]{:S(2)}) collective-permute-start(bf16[256,128]{1,0:T(8,128)(2,1)} %get-tuple-element.11), channel_id=1, source_target_pairs={{0,1},{1,0},{2,3},{3,2},{4,5},{5,4},{6,7},{7,6},{8,9},{9,8},{10,11... | collective-permute-start | bytes 196616 | tf_op jit(solution)/shard_map/ppermute | solution.py:160
  310.5 15.0 %all-to-all-start.7 = ((bf16[4,256,128]{2,1,0:T(8,128)(2,1)}), bf16[4,256,128]{2,1,0:T(8,128)(2,1)S(1)}, u32[]{:S(2)}, u32[]{:S(2)}) async-start(bf16[4,256,128]{2,1,0:T(8,128)(2,1)} %broadcast_in_dim.154), calls=%async_computation.7 | async-start | bytes 524288 | tf_op jit(solution)/shard_map/all_to_all | solution.py:161
  325.7 8.9 %collective-permute-start.11 = (bf16[256,128]{1,0:T(8,128)(2,1)S(1)}, bf16[256,128]{1,0:T(8,128)(2,1)S(1)}, u32[]{:S(2)}, u32[]{:S(2)}) collective-permute-start(bf16[256,128]{1,0:T(8,128)(2,1)S(1)} %add_convert_fusion), channel_id=1, source_target_pairs={{0,1},{1,0},{2,3},{3,2},{4,5},{5,4},{6,7},{7,6},{8,9},{9,8},{10,11... | collective-permute-start | bytes 196616 | tf_op jit(solution)/shard_map/ppermute | solution.py:184
  336.5 20.6 %all-to-all-start.8 = ((bf16[96,16,128]{2,1,0:T(8,128)(2,1)}), bf16[96,16,128]{2,1,0:T(8,128)(2,1)S(1)}, u32[]{:S(2)}, u32[]{:S(2)}) async-start(bf16[96,16,128]{2,1,0:T(8,128)(2,1)} %bitcast.15), calls=%async_computation.8 | async-start | bytes 786432 | tf_op jit(solution)/shard_map/all_to_all | solution.py:217
  379.2 7.7 %collective-permute-start.12 = (bf16[1536,128]{1,0:T(8,128)(2,1)S(1)}, bf16[1536,128]{1,0:T(8,128)(2,1)S(1)}, u32[]{:S(2)}, u32[]{:S(2)}) collective-permute-start(bf16[1536,128]{1,0:T(8,128)(2,1)S(1)} %bitcast.33), channel_id=1, source_target_pairs={{0,1},{1,0},{2,3},{3,2},{4,5},{5,4},{6,7},{7,6},{8,9},{9,8},{10,11... | collective-permute-start | bytes 1179656 | tf_op jit(solution)/shard_map/ppermute | solution.py:224

commit v3 on v2

--- a/solution.py
+++ b/solution.py
@@ -16,10 +16,10 @@
 BLK = ("y", "q")
 
 
-def scatter_kernel(place_ref, rows_ref, cols_ref, tiles_ref, panel_ref, out_ref):
+def scatter_kernel(place_ref, rows_ref, cols_ref, tiles_ref, panel_ref, mine_ref, away_ref):
     steps, slots, width, _ = tiles_ref.shape
-    blocks = out_ref.shape[1] // width
     q = place_ref[0]
+    c = place_ref[1]
     share = jnp.where(place_ref[2] == 1, ALPHA / (1.0 - ALPHA), 0.0).astype(F32)
     for t in range(steps):
         place = lax.rem(q + (steps - t), steps)
@@ -34,34 +34,35 @@
                     preferred_element_type=F32,
                 )
             )
-        for b in range(blocks):
+        for block, out_ref in ((c, mine_ref), (1 - c, away_ref)):
             total = jnp.zeros(products[0].shape, F32)
             for p in range(slots):
-                total = total + jnp.where(cols_ref[p, t] == b, products[p], 0.0)
+                total = total + jnp.where(cols_ref[p, t] == block, products[p], 0.0)
             if t == 0:
-                total = total + share * panel_ref[b * width : (b + 1) * width, :].astype(F32)
-            out_ref[place, b * width : (b + 1) * width, :] = total.astype(BF)
+                rows = pl.ds(pl.multiple_of(block * width, width), width)
+                total = total + share * panel_ref[rows, :].astype(F32)
+            out_ref[place] = total.astype(out_ref.dtype)
 
 
 def gather_kernel(
-    place_ref, rows_ref, cols_ref, tiles_ref, panels_ref, mine_ref, away_ref, sum_ref
+    place_ref, rows_ref, cols_ref, tiles_ref, near_ref, far_ref, mine_ref, away_ref, sum_ref
 ):
     steps, slots, width, _ = tiles_ref.shape
-    half = mine_ref.shape[0]
     q = place_ref[0]
     c = place_ref[1]
     share = jnp.where(place_ref[2] == 1, ALPHA / (1.0 - ALPHA), 0.0).astype(F32)
-    sum_ref[...] = share * panels_ref[q].astype(F32)
+    mine = pl.ds(pl.multiple_of(c * width, width), width)
+    away = pl.ds(pl.multiple_of((1 - c) * width, width), width)
+    sum_ref[mine, :] = share * near_ref[q].astype(F32)
+    sum_ref[away, :] = share * far_ref[q].astype(F32)
     for t in range(steps):
         place = lax.rem(q + (steps - t), steps)
         for p in range(slots):
-            cols = pl.ds(pl.multiple_of(cols_ref[p, t] * width, width), width)
+            piece = jnp.where(cols_ref[p, t] == c, near_ref[place], far_ref[place])
             rows = pl.ds(pl.multiple_of(rows_ref[p, t] * width, width), width)
-            sum_ref[rows, :] += jnp.dot(
-                tiles_ref[t, p], panels_ref[place, cols, :], preferred_element_type=F32
-            )
-    mine_ref[...] = sum_ref[pl.ds(pl.multiple_of(c * half, half), half), :]
-    away_ref[...] = sum_ref[pl.ds(pl.multiple_of((1 - c) * half, half), half), :].astype(BF)
+            sum_ref[rows, :] += jnp.dot(tiles_ref[t, p], piece, preferred_element_type=F32)
+    mine_ref[...] = sum_ref[mine, :]
+    away_ref[...] = sum_ref[away, :].astype(BF)
 
 
 def call(kernel, outs, scalars, operands, scratch=(), interpret=False):
@@ -74,6 +75,7 @@
         in_specs=[smem] * len(scalars) + [vmem] * len(operands),
         out_specs=[vmem] * len(outs),
         scratch_shapes=list(scratch),
+        compiler_params=pltpu.CompilerParams(vmem_limit_bytes=16 << 20),
         interpret=interpret,
     )(*scalars, *operands)
 
@@ -115,9 +117,6 @@
     def to_all(value, count):
         return jnp.broadcast_to(value[None], (count,) + value.shape)
 
-    def halves(value):
-        return [lax.dynamic_slice_in_dim(value, k * half, half, 0) for k in (c_id, 1 - c_id)]
-
     def whole(mine, other):
         return jnp.where(
             c_id == 0,
@@ -126,34 +125,33 @@
         )
 
     def with_transpose(panel, where):
-        (parts,) = call(
+        mine, away = call(
             scatter_kernel,
-            [((steps, nodes_here, classes), BF)],
+            [((steps, half, classes), F32), ((steps, half, classes), BF)],
             [where] + scalars,
             [tiles, panel],
             interpret=interpret,
         )
+        parts = (mine + lax.ppermute(away, yrep, pairs).astype(F32)).astype(BF)
         parts = lax.all_to_all(parts, "q", 0, 0, tiled=True).astype(F32)
         before = jnp.sum(jnp.where(from_same, 0.0, parts), axis=0).astype(BF)
         moved = lax.ppermute(before, "y", [((i + 1) % ny, i) for i in range(ny)])
         total = jnp.sum(jnp.where(from_same, parts, 0.0), axis=0) + moved.astype(F32)
-        mine, away = halves(total)
-        pair = (mine + lax.ppermute(away.astype(BF), yrep, pairs).astype(F32)).astype(BF)
         group = lax.all_to_all(
-            to_all(pair, nzh), yrep, 0, 0, axis_index_groups=fours, tiled=True
+            to_all(total.astype(BF), nzh), yrep, 0, 0, axis_index_groups=fours, tiled=True
         )
         return ((1.0 - ALPHA) * jnp.sum(group.astype(F32), axis=0)).astype(BF)
 
-    def with_plain(mine, where):
-        here = whole(mine, lax.ppermute(mine, yrep, pairs))
+    def with_plain(here, where):
         before = lax.ppermute(here, "y", [(i, (i + 1) % ny) for i in range(ny)])
-        panels = jnp.where(from_same, here[None], before[None])
-        panels = lax.all_to_all(panels, "q", 0, 0, tiled=True)
+        near = jnp.where(from_same, here[None], before[None])
+        near = lax.all_to_all(near, "q", 0, 0, tiled=True)
+        far = lax.ppermute(near, yrep, pairs)
         mine, away = call(
             gather_kernel,
             [((half, classes), F32), ((half, classes), BF)],
             [where] + scalars,
-            [tiles, panels],
+            [tiles, near, far],
             [pltpu.VMEM((nodes_here, classes), F32)],
             interpret=interpret,
         )

time: 393 us -> 357 us (0.908)
  starting transfers between devices: 106 us -> 87 us
  Pallas kernels: 16.3 us -> 6.54 us
  waiting for transfers between devices: 112 us -> 106 us
    ppermute x4, waiting for transfers between devices: 8.85 us -> 40.3 us  [the longest x2 21.1 us: with_transpose(): parts = (mine + lax.ppermute(away, yrep, pairs).astype(F32)).astype(BF)]
    all_to_all x1 -> x0, waiting for transfers between devices: 26.6 us -> none  [with_plain(): panels = lax.all_to_all(panels, 'q', 0, 0, tiled=True)]
    all_to_all x1, blocking collectives: 28.8 us -> 16.9 us  [with_transpose(): parts = lax.all_to_all(parts, 'q', 0, 0, tiled=True).astype(F32)]
    all_to_all x3 -> x4, blocking collectives: 83.4 us -> 94.5 us  [the longest x2 62.6 us: with_transpose(): lax.all_to_all(to_all(total.astype(BF), nzh), yrep, 0, 0, axis_index_grou...]
    ppermute x2, starting transfers between devices: 16.1 us -> 5.94 us  [with_transpose(): moved = lax.ppermute(before, 'y', [((i + 1) % ny, i) for i in range(ny)])]
    pallas_call x4, Pallas kernels: 16.3 us -> 6.54 us  [call(): pl.pallas_call(kernel, out_shape=shapes, in_specs=[smem] * len(scalars) +...]
    all_to_all x1, waiting for transfers between devices: 17.5 us -> 9.34 us  [with_transpose(): parts = lax.all_to_all(parts, 'q', 0, 0, tiled=True).astype(F32)]
    all_to_all x1 -> x0, starting transfers between devices: 5.71 us -> none  [with_plain(): panels = lax.all_to_all(panels, 'q', 0, 0, tiled=True)]
  transfers between devices with their start and end apart: 18 -> 17, of which waited for: 18 -> 17; matrix products, arithmetic and copies ran while one was open for 0% -> 0% of each run, Pallas kernels for 0% -> 0%
where the time goes in v3:
time: 357 us; the launch traced here: 356 us
  blocking collectives  131 us (37%)
  waiting for transfers between devices  106 us (30%)
  starting transfers between devices  87 us (24%)
  local copies, waits for them, and re-layouts  8.29 us (2%)
  other arithmetic  7.35 us (2%)
  Pallas kernels  6.54 us (2%)
  between operations  6.19 us (2%)
    all_to_all x2, blocking collectives, with_transpose(): lax.all_to_all(to_all(total.astype(BF), nzh), yrep, 0, 0, axis_index_grou...  62.6 us
    all_to_all x2, blocking collectives, with_plain(): near = lax.all_to_all(near, 'q', 0, 0, tiled=True)  31.9 us
    ppermute x2, waiting for transfers between devices, with_transpose(): parts = (mine + lax.ppermute(away, yrep, pairs).astype(F32)).astype(BF)  21.1 us
    all_to_all x2, waiting for transfers between devices, with_plain(): chips = lax.all_to_all(to_all(chip, nzh), 'zh', 0, 0, tiled=True)  20.9 us
    all_to_all x1, blocking collectives, on_device(): lax.all_to_all(to_all(sums, nblk), BLK, 0, 0, tiled=True)  19.9 us
    ppermute x2, waiting for transfers between devices, with_plain(): far = lax.ppermute(near, yrep, pairs)  19.2 us
    all_to_all x1, blocking collectives, with_transpose(): parts = lax.all_to_all(parts, 'q', 0, 0, tiled=True).astype(F32)  16.9 us
    ppermute x2, starting transfers between devices, with_plain(): far = lax.ppermute(near, yrep, pairs)  14.7 us
  transfers between devices with their start and end apart: 17, of which 17 were waited for; matrix products, arithmetic and copies ran while one was open for 0% of the time, Pallas kernels for 0%

profile of v3, /device:TPU:1, one launch (start us, length us, event | category | flops | bytes accessed | tf_op | source)
XLA Modules:
  0.0 355.6 jit_solution(466037652513993480)
XLA Ops:
  0.7 1.0 copy-done
  1.7 1.5 fusion.4
  3.2 0.3 convolution_convert_fusion.1.panel_ref
  3.6 1.9 copy-done.1
  5.4 1.6 shard_map.102
  7.1 6.5 %collective-permute-start = (bf16[12,256,128]{2,1,0:T(8,128)(2,1)S(1)}, bf16[12,256,128]{2,1,0:T(8,128)(2,1)S(1)}, u32[]{:S(2)}, u32[]{:S(2)}) collective-permute-start(bf16[12,256,128]{2,1,0:T(8,128)(2,1)S(1)} %get-tuple-element.13), channel_id=1, source_target_pairs={{0,97},{97,0},{2,99},{99,2},{4,101},{101,4},{6,103},{103,6},{96,19... | collective-permute-start | bytes 2359304 | tf_op jit(solution)/shard_map/ppermute | solution.py:135
  13.6 9.7 %collective-permute-done = bf16[12,256,128]{2,1,0:T(8,128)(2,1)S(1)} collective-permute-done((bf16[12,256,128]{2,1,0:T(8,128)(2,1)S(1)}, bf16[12,256,128]{2,1,0:T(8,128)(2,1)S(1)}, u32[]{:S(2)}, u32[]{:S(2)}) %collective-permute-start) | collective-permute-done | bytes 786464 | tf_op jit(solution)/shard_map/ppermute | solution.py:135
  23.2 1.1 add_convert_fusion.1
  24.3 7.7 %all-to-all-start = ((bf16[12,256,128]{2,1,0:T(8,128)(2,1)}), bf16[12,256,128]{2,1,0:T(8,128)(2,1)S(1)}, u32[]{:S(2)}, u32[]{:S(2)}) async-start(bf16[12,256,128]{2,1,0:T(8,128)(2,1)} %add_convert_fusion.1), calls=%async_computation | async-start | bytes 1572864 | tf_op jit(solution)/shard_map/all_to_all | solution.py:136
  32.0 9.3 %all-to-all-done = bf16[12,256,128]{2,1,0:T(8,128)(2,1)S(1)} async-done(((bf16[12,256,128]{2,1,0:T(8,128)(2,1)}), bf16[12,256,128]{2,1,0:T(8,128)(2,1)S(1)}, u32[]{:S(2)}, u32[]{:S(2)}) %all-to-all-start) | async-done | bytes 786464 | tf_op jit(solution)/shard_map/all_to_all | solution.py:136
  41.4 0.3 fusion.1
  41.7 4.0 %collective-permute-start.1 = (bf16[256,128]{1,0:T(8,128)(2,1)S(1)}, bf16[256,128]{1,0:T(8,128)(2,1)S(1)}, u32[]{:S(2)}, u32[]{:S(2)}) collective-permute-start(bf16[256,128]{1,0:T(8,128)(2,1)S(1)} %get-tuple-element.22), channel_id=1, source_target_pairs={{96,0},{192,96},{288,192},{384,288},{480,384},{576,480},{672,576},... | collective-permute-start | bytes 196616 | tf_op jit(solution)/shard_map/ppermute | solution.py:138
  45.7 5.4 %collective-permute-done.1 = bf16[256,128]{1,0:T(8,128)(2,1)S(1)} collective-permute-done((bf16[256,128]{1,0:T(8,128)(2,1)S(1)}, bf16[256,128]{1,0:T(8,128)(2,1)S(1)}, u32[]{:S(2)}, u32[]{:S(2)}) %collective-permute-start.1) | collective-permute-done | bytes 65568 | tf_op jit(solution)/shard_map/ppermute | solution.py:138
  51.2 37.7 %all_to_all.50 = bf16[4,256,128]{2,1,0:T(8,128)(2,1)S(1)} all-to-all(bf16[4,256,128]{2,1,0:T(8,128)(2,1)S(1)} %broadcast_in_dim.147), channel_id=1, replica_groups={{0,194,388,582},{97,291,485,679},{96,290,484,678},{193,387,581,7},{192,..., dimensions={0} | all-to-all | bytes 524288 | tf_op jit(solution)/shard_map/all_to_all | solution.py:140
  89.0 1.9 collective-permute-start.2
  90.9 4.3 %collective-permute-done.2 = bf16[256,128]{1,0:T(8,128)(2,1)S(1)} collective-permute-done((bf16[256,128]{1,0:T(8,128)(2,1)S(1)}, bf16[256,128]{1,0:T(8,128)(2,1)S(1)}, u32[]{:S(2)}, u32[]{:S(2)}) %collective-permute-start.2) | collective-permute-done | bytes 65568 | tf_op jit(solution)/shard_map/ppermute | solution.py:146
  95.3 15.2 %all_to_all.51.near_ref = bf16[12,256,128]{2,1,0:T(8,128)(2,1)S(1)} all-to-all(bf16[12,256,128]{2,1,0:T(8,128)(2,1)S(1)} %broadcast_select_fusion.1), channel_id=1, replica_groups=mesh['y'=8,'q'=12,'zh'=4,'c'=2] {'q'}, dimensions={0} | all-to-all | bytes 1572864 | tf_op jit(solution)/shard_map/all_to_all | solution.py:148
  110.5 7.7 %collective-permute-start.3 = (bf16[12,256,128]{2,1,0:T(8,128)(2,1)S(1)}, bf16[12,256,128]{2,1,0:T(8,128)(2,1)S(1)}, u32[]{:S(2)}, u32[]{:S(2)}) collective-permute-start(bf16[12,256,128]{2,1,0:T(8,128)(2,1)S(1)} %all_to_all.51.near_ref), channel_id=1, source_target_pairs={{0,97},{97,0},{2,99},{99,2},{4,101},{101,4},{6,103},{103,6},{96,19... | collective-permute-start | bytes 2359304 | tf_op jit(solution)/shard_map/ppermute | solution.py:149
  118.3 9.6 %collective-permute-done.3.far_ref = bf16[12,256,128]{2,1,0:T(8,128)(2,1)S(1)} collective-permute-done((bf16[12,256,128]{2,1,0:T(8,128)(2,1)S(1)}, bf16[12,256,128]{2,1,0:T(8,128)(2,1)S(1)}, u32[]{:S(2)}, u32[]{:S(2)}) %collective-permute-start.3) | collective-permute-done | bytes 786464 | tf_op jit(solution)/shard_map/ppermute | solution.py:149
  127.9 1.7 shard_map.103
  129.6 4.1 %collective-permute-start.4 = (bf16[256,128]{1,0:T(8,128)(2,1)S(1)}, bf16[256,128]{1,0:T(8,128)(2,1)S(1)}, u32[]{:S(2)}, u32[]{:S(2)}) collective-permute-start(bf16[256,128]{1,0:T(8,128)(2,1)S(1)} %get-tuple-element.15), channel_id=1, source_target_pairs={{0,1},{1,0},{2,3},{3,2},{4,5},{5,4},{6,7},{7,6},{8,9},{9,8},{10,11... | collective-permute-start | bytes 196616 | tf_op jit(solution)/shard_map/ppermute | solution.py:158
  133.7 0.9 collective-permute-done.4
  134.6 0.7 broadcast_in_dim.150
  135.3 3.4 all-to-all-start.3
  138.8 11.5 %all-to-all-done.3 = bf16[4,256,128]{2,1,0:T(8,128)(2,1)S(1)} async-done(((bf16[4,256,128]{2,1,0:T(8,128)(2,1)}), bf16[4,256,128]{2,1,0:T(8,128)(2,1)S(1)}, u32[]{:S(2)}, u32[]{:S(2)}) %all-to-all-start.3) | async-done | bytes 262176 | tf_op jit(solution)/shard_map/all_to_all | solution.py:159
  150.5 0.3 select_reduce_fusion
  151.0 7.8 %collective-permute-start.5 = (bf16[2,256,128]{2,1,0:T(8,128)(2,1)S(1)}, bf16[2,256,128]{2,1,0:T(8,128)(2,1)S(1)}, u32[]{:S(2)}, u32[]{:S(2)}) collective-permute-start(bf16[2,256,128]{2,1,0:T(8,128)(2,1)S(1)} %pad_maximum_fusion.2), channel_id=1, source_target_pairs={{0,1},{1,0},{2,3},{3,2},{4,5},{5,4},{6,7},{7,6},{8,9},{9,8},{10,11... | collective-permute-start | bytes 393224 | tf_op jit(solution)/shard_map/ppermute | solution.py:177
  158.8 1.0 collective-permute-done.5
  159.9 0.7 slice_bitcast_fusion
  160.6 1.9 copy-done.3
  162.5 1.6 shard_map.104
  164.1 3.1 collective-permute-start.6
  167.2 11.4 %collective-permute-done.6 = bf16[12,256,128]{2,1,0:T(8,128)(2,1)S(1)} collective-permute-done((bf16[12,256,128]{2,1,0:T(8,128)(2,1)S(1)}, bf16[12,256,128]{2,1,0:T(8,128)(2,1)S(1)}, u32[]{:S(2)}, u32[]{:S(2)}) %collective-permute-start.6) | collective-permute-done | bytes 786464 | tf_op jit(solution)/shard_map/ppermute | solution.py:135
  178.8 16.9 %all_to_all.52 = bf16[12,256,128]{2,1,0:T(8,128)(2,1)S(1)} all-to-all(bf16[12,256,128]{2,1,0:T(8,128)(2,1)S(1)} %add_convert_fusion), channel_id=1, replica_groups=mesh['y'=8,'q'=12,'zh'=4,'c'=2] {'q'}, dimensions={0} | all-to-all | bytes 1572864 | tf_op jit(solution)/shard_map/all_to_all | solution.py:136
  195.7 0.3 fusion.3
  196.1 1.9 collective-permute-start.7
  198.0 3.1 collective-permute-done.7
  201.2 24.8 %all_to_all.53 = bf16[4,256,128]{2,1,0:T(8,128)(2,1)S(1)} all-to-all(bf16[4,256,128]{2,1,0:T(8,128)(2,1)S(1)} %broadcast_in_dim.151), channel_id=1, replica_groups={{0,194,388,582},{97,291,485,679},{96,290,484,678},{193,387,581,7},{192,..., dimensions={0} | all-to-all | bytes 524288 | tf_op jit(solution)/shard_map/all_to_all | solution.py:140
  226.1 1.9 collective-permute-start.8
  228.0 4.3 %collective-permute-done.8 = bf16[256,128]{1,0:T(8,128)(2,1)S(1)} collective-permute-done((bf16[256,128]{1,0:T(8,128)(2,1)S(1)}, bf16[256,128]{1,0:T(8,128)(2,1)S(1)}, u32[]{:S(2)}, u32[]{:S(2)}) %collective-permute-start.8) | collective-permute-done | bytes 65568 | tf_op jit(solution)/shard_map/ppermute | solution.py:146
  232.4 16.7 %all_to_all.54.near_ref = bf16[12,256,128]{2,1,0:T(8,128)(2,1)S(1)} all-to-all(bf16[12,256,128]{2,1,0:T(8,128)(2,1)S(1)} %broadcast_select_fusion), channel_id=1, replica_groups=mesh['y'=8,'q'=12,'zh'=4,'c'=2] {'q'}, dimensions={0} | all-to-all | bytes 1572864 | tf_op jit(solution)/shard_map/all_to_all | solution.py:148
  249.2 7.0 %collective-permute-start.9 = (bf16[12,256,128]{2,1,0:T(8,128)(2,1)S(1)}, bf16[12,256,128]{2,1,0:T(8,128)(2,1)S(1)}, u32[]{:S(2)}, u32[]{:S(2)}) collective-permute-start(bf16[12,256,128]{2,1,0:T(8,128)(2,1)S(1)} %all_to_all.54.near_ref), channel_id=1, source_target_pairs={{0,97},{97,0},{2,99},{99,2},{4,101},{101,4},{6,103},{103,6},{96,19... | collective-permute-start | bytes 2359304 | tf_op jit(solution)/shard_map/ppermute | solution.py:149
  256.1 9.7 %collective-permute-done.9.far_ref = bf16[12,256,128]{2,1,0:T(8,128)(2,1)S(1)} collective-permute-done((bf16[12,256,128]{2,1,0:T(8,128)(2,1)S(1)}, bf16[12,256,128]{2,1,0:T(8,128)(2,1)S(1)}, u32[]{:S(2)}, u32[]{:S(2)}) %collective-permute-start.9) | collective-permute-done | bytes 786464 | tf_op jit(solution)/shard_map/ppermute | solution.py:149
  265.8 1.6 shard_map.105
  267.4 3.7 %collective-permute-start.10 = (bf16[256,128]{1,0:T(8,128)(2,1)S(1)}, bf16[256,128]{1,0:T(8,128)(2,1)S(1)}, u32[]{:S(2)}, u32[]{:S(2)}) collective-permute-start(bf16[256,128]{1,0:T(8,128)(2,1)S(1)} %get-tuple-element.19), channel_id=1, source_target_pairs={{0,1},{1,0},{2,3},{3,2},{4,5},{5,4},{6,7},{7,6},{8,9},{9,8},{10,11... | collective-permute-start | bytes 196616 | tf_op jit(solution)/shard_map/ppermute | solution.py:158
  271.2 0.9 collective-permute-done.10
  272.1 0.7 broadcast_in_dim.154
  272.8 3.9 %all-to-all-start.7 = ((bf16[4,256,128]{2,1,0:T(8,128)(2,1)}), bf16[4,256,128]{2,1,0:T(8,128)(2,1)S(1)}, u32[]{:S(2)}, u32[]{:S(2)}) async-start(bf16[4,256,128]{2,1,0:T(8,128)(2,1)} %broadcast_in_dim.154), calls=%async_computation.7 | async-start | bytes 524288 | tf_op jit(solution)/shard_map/all_to_all | solution.py:159
  276.7 0.6 subtract_reduce_fusion
  278.7 9.3 %all-to-all-done.7 = bf16[4,256,128]{2,1,0:T(8,128)(2,1)S(1)} async-done(((bf16[4,256,128]{2,1,0:T(8,128)(2,1)}), bf16[4,256,128]{2,1,0:T(8,128)(2,1)S(1)}, u32[]{:S(2)}, u32[]{:S(2)}) %all-to-all-start.7) | async-done | bytes 262176 | tf_op jit(solution)/shard_map/all_to_all | solution.py:159
  288.2 7.9 %collective-permute-start.11 = (bf16[256,128]{1,0:T(8,128)(2,1)S(1)}, bf16[256,128]{1,0:T(8,128)(2,1)S(1)}, u32[]{:S(2)}, u32[]{:S(2)}) collective-permute-start(bf16[256,128]{1,0:T(8,128)(2,1)S(1)} %add_convert_fusion.2), channel_id=1, source_target_pairs={{0,1},{1,0},{2,3},{3,2},{4,5},{5,4},{6,7},{7,6},{8,9},{9,8},{10,11... | collective-permute-start | bytes 196616 | tf_op jit(solution)/shard_map/ppermute | solution.py:182
  296.1 0.9 collective-permute-done.11
  297.0 0.6 fusion.6
  297.6 0.2 convolution_convert_fusion.2
  298.0 0.9 copy.15
  298.9 8.1 %all-to-all-start.8 = ((bf16[96,16,128]{2,1,0:T(8,128)(2,1)}), bf16[96,16,128]{2,1,0:T(8,128)(2,1)S(1)}, u32[]{:S(2)}, u32[]{:S(2)}) async-start(bf16[96,16,128]{2,1,0:T(8,128)(2,1)} %bitcast.15), calls=%async_computation.8 | async-start | bytes 786432 | tf_op jit(solution)/shard_map/all_to_all | solution.py:215
  307.0 13.8 %all-to-all-done.8 = bf16[96,16,128]{2,1,0:T(8,128)(2,1)S(1)} async-done(((bf16[96,16,128]{2,1,0:T(8,128)(2,1)}), bf16[96,16,128]{2,1,0:T(8,128)(2,1)S(1)}, u32[]{:S(2)}, u32[]{:S(2)}) %all-to-all-start.8) | async-done | bytes 393248 | tf_op jit(solution)/shard_map/all_to_all | solution.py:215
  320.9 0.6 slice_reduce_fusion.2
  323.0 19.9 %all_to_all.55 = bf16[96,16,128]{2,1,0:T(8,128)(2,1)S(1)} all-to-all(bf16[96,16,128]{2,1,0:T(8,128)(2,1)S(1)} %broadcast_in_dim.166), channel_id=1, replica_groups=mesh['y'=8,'q'=12,'zh'=4,'c'=2] {'y','q'}, dimensions={0} | all-to-all | bytes 786432 | tf_op jit(solution)/shard_map/all_to_all | solution.py:221
  342.9 6.4 %collective-permute-start.12 = (bf16[1536,128]{1,0:T(8,128)(2,1)S(1)}, bf16[1536,128]{1,0:T(8,128)(2,1)S(1)}, u32[]{:S(2)}, u32[]{:S(2)}) collective-permute-start(bf16[1536,128]{1,0:T(8,128)(2,1)S(1)} %bitcast.41), channel_id=1, source_target_pairs={{0,1},{1,0},{2,3},{3,2},{4,5},{5,4},{6,7},{7,6},{8,9},{9,8},{10,11... | collective-permute-start | bytes 1179656 | tf_op jit(solution)/shard_map/ppermute | solution.py:222
  349.2 1.3 collective-permute-done.12
  350.8 0.6 slice_reduce_fusion
  351.4 0.7 pad_maximum_fusion.1
  353.5 1.0 pad_maximum_fusion
  (52 shorter events, 2.2 us)
Async XLA Ops:
  0.6 1.0 copy-start
  0.6 2.5 copy-start.7
  0.7 2.9 copy-start.5
  0.7 2.9 copy-start.6
  3.6 1.9 copy-start.1
  7.1 16.2 %collective-permute-start = (bf16[12,256,128]{2,1,0:T(8,128)(2,1)S(1)}, bf16[12,256,128]{2,1,0:T(8,128)(2,1)S(1)}, u32[]{:S(2)}, u32[]{:S(2)}) collective-permute-start(bf16[12,256,128]{2,1,0:T(8,128)(2,1)S(1)} %get-tuple-element.13), channel_id=1, source_target_pairs={{0,97},{97,0},{2,99},{99,2},{4,101},{101,4},{6,103},{103,6},{96,19... | collective-permute-start | bytes 2359304 | tf_op jit(solution)/shard_map/ppermute | solution.py:135
  24.3 17.0 %all-to-all-start = ((bf16[12,256,128]{2,1,0:T(8,128)(2,1)}), bf16[12,256,128]{2,1,0:T(8,128)(2,1)S(1)}, u32[]{:S(2)}, u32[]{:S(2)}) async-start(bf16[12,256,128]{2,1,0:T(8,128)(2,1)} %add_convert_fusion.1), calls=%async_computation | async-start | bytes 1572864 | tf_op jit(solution)/shard_map/all_to_all | solution.py:136
  41.7 9.4 %collective-permute-start.1 = (bf16[256,128]{1,0:T(8,128)(2,1)S(1)}, bf16[256,128]{1,0:T(8,128)(2,1)S(1)}, u32[]{:S(2)}, u32[]{:S(2)}) collective-permute-start(bf16[256,128]{1,0:T(8,128)(2,1)S(1)} %get-tuple-element.22), channel_id=1, source_target_pairs={{96,0},{192,96},{288,192},{384,288},{480,384},{576,480},{672,576},... | collective-permute-start | bytes 196616 | tf_op jit(solution)/shard_map/ppermute | solution.py:138
  51.2 76.7 %copy-start.2 = (bf16[1,1,12,2,256,256]{5,4,3,2,1,0:T(8,128)(2,1)S(1)}, bf16[1,1,12,2,256,256]{5,4,3,2,1,0:T(8,128)(2,1)}, u32[]{:S(2)}) copy-start(bf16[1,1,12,2,256,256]{5,4,3,2,1,0:T(8,128)(2,1)} %param.13) | copy-start | bytes 9437188
  89.0 6.2 %collective-permute-start.2 = (bf16[256,128]{1,0:T(8,128)(2,1)S(1)}, bf16[256,128]{1,0:T(8,128)(2,1)S(1)}, u32[]{:S(2)}, u32[]{:S(2)}) collective-permute-start(bf16[256,128]{1,0:T(8,128)(2,1)S(1)} %multiply_convert_fusion.2), channel_id=1, source_target_pairs={{0,96},{96,192},{192,288},{288,384},{384,480},{480,576},{576,672},... | collective-permute-start | bytes 196616 | tf_op jit(solution)/shard_map/ppermute | solution.py:146
  110.5 17.4 %collective-permute-start.3 = (bf16[12,256,128]{2,1,0:T(8,128)(2,1)S(1)}, bf16[12,256,128]{2,1,0:T(8,128)(2,1)S(1)}, u32[]{:S(2)}, u32[]{:S(2)}) collective-permute-start(bf16[12,256,128]{2,1,0:T(8,128)(2,1)S(1)} %all_to_all.51.near_ref), channel_id=1, source_target_pairs={{0,97},{97,0},{2,99},{99,2},{4,101},{101,4},{6,103},{103,6},{96,19... | collective-permute-start | bytes 2359304 | tf_op jit(solution)/shard_map/ppermute | solution.py:149
  118.3 20.4 %copy-start.8 = (s32[512]{0:T(512)S(1)}, s32[512]{0:T(512)}, u32[]{:S(2)}) copy-start(s32[512]{0:T(512)} %param.8) | copy-start | bytes 6148
  129.6 5.0 %collective-permute-start.4 = (bf16[256,128]{1,0:T(8,128)(2,1)S(1)}, bf16[256,128]{1,0:T(8,128)(2,1)S(1)}, u32[]{:S(2)}, u32[]{:S(2)}) collective-permute-start(bf16[256,128]{1,0:T(8,128)(2,1)S(1)} %get-tuple-element.15), channel_id=1, source_target_pairs={{0,1},{1,0},{2,3},{3,2},{4,5},{5,4},{6,7},{7,6},{8,9},{9,8},{10,11... | collective-permute-start | bytes 196616 | tf_op jit(solution)/shard_map/ppermute | solution.py:158
  135.3 15.0 %all-to-all-start.3 = ((bf16[4,256,128]{2,1,0:T(8,128)(2,1)}), bf16[4,256,128]{2,1,0:T(8,128)(2,1)S(1)}, u32[]{:S(2)}, u32[]{:S(2)}) async-start(bf16[4,256,128]{2,1,0:T(8,128)(2,1)} %broadcast_in_dim.150), calls=%async_computation.3 | async-start | bytes 524288 | tf_op jit(solution)/shard_map/all_to_all | solution.py:159
  151.0 8.8 %collective-permute-start.5 = (bf16[2,256,128]{2,1,0:T(8,128)(2,1)S(1)}, bf16[2,256,128]{2,1,0:T(8,128)(2,1)S(1)}, u32[]{:S(2)}, u32[]{:S(2)}) collective-permute-start(bf16[2,256,128]{2,1,0:T(8,128)(2,1)S(1)} %pad_maximum_fusion.2), channel_id=1, source_target_pairs={{0,1},{1,0},{2,3},{3,2},{4,5},{5,4},{6,7},{7,6},{8,9},{9,8},{10,11... | collective-permute-start | bytes 393224 | tf_op jit(solution)/shard_map/ppermute | solution.py:177
  160.6 1.9 copy-start.3
  164.1 14.5 %collective-permute-start.6 = (bf16[12,256,128]{2,1,0:T(8,128)(2,1)S(1)}, bf16[12,256,128]{2,1,0:T(8,128)(2,1)S(1)}, u32[]{:S(2)}, u32[]{:S(2)}) collective-permute-start(bf16[12,256,128]{2,1,0:T(8,128)(2,1)S(1)} %get-tuple-element.17), channel_id=1, source_target_pairs={{0,97},{97,0},{2,99},{99,2},{4,101},{101,4},{6,103},{103,6},{96,19... | collective-permute-start | bytes 2359304 | tf_op jit(solution)/shard_map/ppermute | solution.py:135
  196.1 5.0 %collective-permute-start.7 = (bf16[256,128]{1,0:T(8,128)(2,1)S(1)}, bf16[256,128]{1,0:T(8,128)(2,1)S(1)}, u32[]{:S(2)}, u32[]{:S(2)}) collective-permute-start(bf16[256,128]{1,0:T(8,128)(2,1)S(1)} %get-tuple-element.20), channel_id=1, source_target_pairs={{96,0},{192,96},{288,192},{384,288},{480,384},{576,480},{672,576},... | collective-permute-start | bytes 196616 | tf_op jit(solution)/shard_map/ppermute | solution.py:138
  201.2 64.7 %copy-start.4 = (bf16[1,1,12,2,256,256]{5,4,3,2,1,0:T(8,128)(2,1)S(1)}, bf16[1,1,12,2,256,256]{5,4,3,2,1,0:T(8,128)(2,1)}, u32[]{:S(2)}) copy-start(bf16[1,1,12,2,256,256]{5,4,3,2,1,0:T(8,128)(2,1)} %param.13) | copy-start | bytes 9437188
  226.1 6.2 %collective-permute-start.8 = (bf16[256,128]{1,0:T(8,128)(2,1)S(1)}, bf16[256,128]{1,0:T(8,128)(2,1)S(1)}, u32[]{:S(2)}, u32[]{:S(2)}) collective-permute-start(bf16[256,128]{1,0:T(8,128)(2,1)S(1)} %multiply_convert_fusion), channel_id=1, source_target_pairs={{0,96},{96,192},{192,288},{288,384},{384,480},{480,576},{576,672},... | collective-permute-start | bytes 196616 | tf_op jit(solution)/shard_map/ppermute | solution.py:146
  249.2 16.6 %collective-permute-start.9 = (bf16[12,256,128]{2,1,0:T(8,128)(2,1)S(1)}, bf16[12,256,128]{2,1,0:T(8,128)(2,1)S(1)}, u32[]{:S(2)}, u32[]{:S(2)}) collective-permute-start(bf16[12,256,128]{2,1,0:T(8,128)(2,1)S(1)} %all_to_all.54.near_ref), channel_id=1, source_target_pairs={{0,97},{97,0},{2,99},{99,2},{4,101},{101,4},{6,103},{103,6},{96,19... | collective-permute-start | bytes 2359304 | tf_op jit(solution)/shard_map/ppermute | solution.py:149
  267.4 4.6 %collective-permute-start.10 = (bf16[256,128]{1,0:T(8,128)(2,1)S(1)}, bf16[256,128]{1,0:T(8,128)(2,1)S(1)}, u32[]{:S(2)}, u32[]{:S(2)}) collective-permute-start(bf16[256,128]{1,0:T(8,128)(2,1)S(1)} %get-tuple-element.19), channel_id=1, source_target_pairs={{0,1},{1,0},{2,3},{3,2},{4,5},{5,4},{6,7},{7,6},{8,9},{9,8},{10,11... | collective-permute-start | bytes 196616 | tf_op jit(solution)/shard_map/ppermute | solution.py:158
  272.8 15.2 %all-to-all-start.7 = ((bf16[4,256,128]{2,1,0:T(8,128)(2,1)}), bf16[4,256,128]{2,1,0:T(8,128)(2,1)S(1)}, u32[]{:S(2)}, u32[]{:S(2)}) async-start(bf16[4,256,128]{2,1,0:T(8,128)(2,1)} %broadcast_in_dim.154), calls=%async_computation.7 | async-start | bytes 524288 | tf_op jit(solution)/shard_map/all_to_all | solution.py:159
  288.2 8.8 %collective-permute-start.11 = (bf16[256,128]{1,0:T(8,128)(2,1)S(1)}, bf16[256,128]{1,0:T(8,128)(2,1)S(1)}, u32[]{:S(2)}, u32[]{:S(2)}) collective-permute-start(bf16[256,128]{1,0:T(8,128)(2,1)S(1)} %add_convert_fusion.2), channel_id=1, source_target_pairs={{0,1},{1,0},{2,3},{3,2},{4,5},{5,4},{6,7},{7,6},{8,9},{9,8},{10,11... | collective-permute-start | bytes 196616 | tf_op jit(solution)/shard_map/ppermute | solution.py:182
  298.9 21.9 %all-to-all-start.8 = ((bf16[96,16,128]{2,1,0:T(8,128)(2,1)}), bf16[96,16,128]{2,1,0:T(8,128)(2,1)S(1)}, u32[]{:S(2)}, u32[]{:S(2)}) async-start(bf16[96,16,128]{2,1,0:T(8,128)(2,1)} %bitcast.15), calls=%async_computation.8 | async-start | bytes 786432 | tf_op jit(solution)/shard_map/all_to_all | solution.py:215
  342.9 7.7 %collective-permute-start.12 = (bf16[1536,128]{1,0:T(8,128)(2,1)S(1)}, bf16[1536,128]{1,0:T(8,128)(2,1)S(1)}, u32[]{:S(2)}, u32[]{:S(2)}) collective-permute-start(bf16[1536,128]{1,0:T(8,128)(2,1)S(1)} %bitcast.41), channel_id=1, source_target_pairs={{0,1},{1,0},{2,3},{3,2},{4,5},{5,4},{6,7},{7,6},{8,9},{9,8},{10,11... | collective-permute-start | bytes 1179656 | tf_op jit(solution)/shard_map/ppermute | solution.py:222

commit v4 on v3

--- a/solution.py
+++ b/solution.py
@@ -16,12 +16,21 @@
 BLK = ("y", "q")
 
 
-def scatter_kernel(place_ref, rows_ref, cols_ref, tiles_ref, panel_ref, mine_ref, away_ref):
+def scatter_kernel(
+    place_ref, rows_ref, cols_ref, far_tiles_ref, panel_ref, mine_ref, away_ref, tiles_ref, arrived
+):
     steps, slots, width, _ = tiles_ref.shape
     q = place_ref[0]
     c = place_ref[1]
     share = jnp.where(place_ref[2] == 1, ALPHA / (1.0 - ALPHA), 0.0).astype(F32)
+    copies = [
+        pltpu.make_async_copy(far_tiles_ref.at[t], tiles_ref.at[t], arrived.at[t])
+        for t in range(steps)
+    ]
+    for copy in copies:
+        copy.start()
     for t in range(steps):
+        copies[t].wait()
         place = lax.rem(q + (steps - t), steps)
         products = []
         for p in range(slots):
@@ -65,19 +74,21 @@
     away_ref[...] = sum_ref[away, :].astype(BF)
 
 
-def call(kernel, outs, scalars, operands, scratch=(), interpret=False):
+def call(kernel, outs, scalars, tiles, operands, scratch, tiles_space, interpret):
     vmem = pl.BlockSpec(memory_space=pltpu.VMEM)
     smem = pl.BlockSpec(memory_space=pltpu.SMEM)
     shapes = [jax.ShapeDtypeStruct(shape, dtype) for shape, dtype in outs]
     return pl.pallas_call(
         kernel,
         out_shape=shapes,
-        in_specs=[smem] * len(scalars) + [vmem] * len(operands),
+        in_specs=[smem] * len(scalars)
+        + [pl.BlockSpec(memory_space=tiles_space)]
+        + [vmem] * len(operands),
         out_specs=[vmem] * len(outs),
         scratch_shapes=list(scratch),
         compiler_params=pltpu.CompilerParams(vmem_limit_bytes=16 << 20),
         interpret=interpret,
-    )(*scalars, *operands)
+    )(*scalars, tiles, *operands)
 
 
 def on_device(interpret, features, labels, w_first, w_second, block_rows, block_cols, block_vals):
@@ -91,6 +102,7 @@
     rep_id = lax.axis_index(REP)
     nodes = nodes_here * nblk
     tiles = block_vals[0, 0]
+    far_tiles = pltpu.with_memory_space_constraint(tiles, pltpu.HBM)
     steps = tiles.shape[0]
     half = nodes_here // nc
     yrep = ("y",) + REP
@@ -110,9 +122,33 @@
     def place(flag):
         return jnp.stack([q_id, c_id, flag]).astype(jnp.int32)
 
+    width = features.shape[1]
+    part = w_first.shape[1] // nc
+    bands = part // classes
+    used = bands * width + part
+    each = -(-(used + 3) // nq)
+    each = -(-each // 16) * 16
     plain = place(jnp.int32(0))
     diagonal = place((rep_id == 0).astype(jnp.int32))
-    from_same = (jnp.arange(nq, dtype=jnp.int32) >= q_id)[:, None, None]
+    from_same = lax.broadcasted_iota(jnp.int32, (nq, 1, classes), 0) >= q_id
+    loss_row = lax.broadcasted_iota(jnp.int32, (each, classes), 0) - (used - q_id * each)
+    labels_half = lax.dynamic_slice_in_dim(labels, c_id * half, half, 0)
+
+    def in_terms(value):
+        high = value.astype(BF)
+        middle = (value - high.astype(F32)).astype(BF)
+        low = (value - high.astype(F32) - middle.astype(F32)).astype(BF)
+        return high, middle, low
+
+    def summed(parts):
+        sums = jnp.sum(parts.astype(F32), axis=0)
+        at = used % each
+        terms = in_terms(jnp.sum(sums[at : at + 3], axis=0, keepdims=True))
+        sums = sums.astype(BF)
+        for k, term in enumerate(terms):
+            sums = jnp.where(loss_row == k, term, sums)
+        return sums
+
 
     def to_all(value, count):
         return jnp.broadcast_to(value[None], (count,) + value.shape)
@@ -129,8 +165,11 @@
             scatter_kernel,
             [((steps, half, classes), F32), ((steps, half, classes), BF)],
             [where] + scalars,
-            [tiles, panel],
-            interpret=interpret,
+            far_tiles,
+            [panel],
+            [pltpu.VMEM(tiles.shape, BF), pltpu.SemaphoreType.DMA((steps,))],
+            pltpu.HBM,
+            interpret,
         )
         parts = (mine + lax.ppermute(away, yrep, pairs).astype(F32)).astype(BF)
         parts = lax.all_to_all(parts, "q", 0, 0, tiled=True).astype(F32)
@@ -151,9 +190,11 @@
             gather_kernel,
             [((half, classes), F32), ((half, classes), BF)],
             [where] + scalars,
-            [tiles, near, far],
+            tiles,
+            [near, far],
             [pltpu.VMEM((nodes_here, classes), F32)],
-            interpret=interpret,
+            pltpu.VMEM,
+            interpret,
         )
         chip = (mine + lax.ppermute(away, "c", cores).astype(F32)).astype(BF)
         chips = lax.all_to_all(to_all(chip, nzh), "zh", 0, 0, tiled=True)
@@ -162,18 +203,23 @@
     hidden = jax.nn.relu(jnp.dot(features, w_first, preferred_element_type=F32)).astype(BF)
     base = jnp.dot(hidden, w_second, preferred_element_type=F32).astype(BF)
     base_half = lax.dynamic_slice_in_dim(base, c_id * half, half, 0)
+    base, base_half, labels_half, plain, diagonal, from_same, loss_row = lax.optimization_barrier(
+        (base, base_half, labels_half, plain, diagonal, from_same, loss_row)
+    )
 
     current = with_transpose(base, diagonal)
     mixed = with_plain(current, plain) + ALPHA * base_half.astype(F32)
-    labels_half = lax.dynamic_slice_in_dim(labels, c_id * half, half, 0)
     onehot = (labels_half[:, None] == jnp.arange(classes, dtype=jnp.int32)[None, :]).astype(F32)
     top = jnp.max(mixed, axis=1, keepdims=True)
     grown = jnp.exp(mixed - top)
     mass = jnp.sum(grown, axis=1, keepdims=True)
-    picked = jnp.sum(mixed * onehot, axis=1, keepdims=True)
-    ce_sum = jnp.sum(jnp.log(mass) + top - picked)
+    lanes = lax.broadcasted_iota(jnp.int32, (1, classes), 1)
+    ce_rows = jnp.where(lanes == 0, jnp.log(mass) + top, 0.0) - mixed * onehot
+    ce_terms = in_terms(jnp.sum(ce_rows, axis=0, keepdims=True))
     grad_out = (grown / mass - onehot) * (1.0 / math.sqrt(nodes))
-    both = jnp.stack([grad_out.astype(BF), mixed.astype(BF)])
+    both, ce_terms, grad_out = lax.optimization_barrier(
+        (jnp.stack([grad_out.astype(BF), mixed.astype(BF)]), ce_terms, grad_out)
+    )
     both = whole(both, lax.ppermute(both, "c", cores))
     moving, logits = both[0], both[1]
 
@@ -181,8 +227,6 @@
     grad_half = (with_plain(moving, diagonal) + ALPHA * grad_out).astype(BF)
     grad_b = whole(grad_half, lax.ppermute(grad_half, "c", cores))
 
-    part = hidden.shape[1] // nc
-    bands = part // classes
     hidden_part = lax.dynamic_slice_in_dim(hidden, c_id * part, part, 1)
     second_part = lax.dynamic_slice_in_dim(w_second, c_id * part, part, 0)
     back = lax.dot_general(grad_b, second_part, (((1,), (1,)), ((), ())), preferred_element_type=F32)
@@ -193,32 +237,14 @@
     second = lax.dot_general(
         hidden_part, grad_b, (((0,), (0,)), ((), ())), preferred_element_type=F32
     ).astype(BF)
-    width = features.shape[1]
-    used = bands * width + part
-    each = -(-(used + 1) // nblk)
-    each = -(-each // 16) * 16
-    lanes = lax.broadcasted_iota(jnp.int32, (1, classes), 1)
-
-    def in_terms(value):
-        high = value.astype(BF)
-        middle = (value - high.astype(F32)).astype(BF)
-        low = (value - high.astype(F32) - middle.astype(F32)).astype(BF)
-        zero = jnp.zeros((), BF)
-        return jnp.where(
-            lanes == 0, high, jnp.where(lanes == 1, middle, jnp.where(lanes == 2, low, zero))
-        )
 
     sums = jnp.concatenate(
         [first[:, k * classes : (k + 1) * classes] for k in range(bands)]
-        + [second, in_terms(ce_sum), jnp.zeros((each * nblk - used - 1, classes), BF)]
-    )
-    sums = lax.all_to_all(sums.reshape(nblk, each, classes), BLK, 0, 0, tiled=True)
-    sums = jnp.sum(sums.astype(F32), axis=0)
-    rows = lax.broadcasted_iota(jnp.int32, (each, classes), 0)
-    is_loss = (lax.axis_index(BLK) * each + rows) == used
-    loss_sum = jnp.sum(sums[used % each, :3])
-    sums = jnp.where(is_loss, in_terms(loss_sum), sums.astype(BF))
-    sums = lax.all_to_all(to_all(sums, nblk), BLK, 0, 0, tiled=True).reshape(nblk * each, classes)
+        + [second, *ce_terms, jnp.zeros((each * nq - used - 3, classes), BF)]
+    ).reshape(nq, each, classes)
+    sums = summed(lax.all_to_all(sums, "q", 0, 0, tiled=True))
+    sums = summed(lax.all_to_all(to_all(sums, ny), "y", 0, 0, tiled=True))
+    sums = lax.all_to_all(to_all(sums, nq), "q", 0, 0, tiled=True).reshape(nq * each, classes)
     other = lax.ppermute(sums, "c", cores)
     first_core = jnp.where(c_id == 0, sums, other).astype(F32)
     second_core = jnp.where(c_id == 0, other, sums).astype(F32)
@@ -227,7 +253,7 @@
         axis=1,
     )
     grad_second = jnp.concatenate([v[bands * width : used] for v in (first_core, second_core)])
-    loss = (jnp.sum(first_core[used, :3]) + jnp.sum(second_core[used, :3])) / nodes
+    loss = jnp.sum(first_core[used : used + 3] + second_core[used : used + 3]) / nodes
     return (logits, grad_first, grad_second, loss)
 
 

time: 357 us -> 348 us (0.975)
  blocking collectives: 131 us -> 181 us
  waiting for transfers between devices: 106 us -> 70 us
  starting transfers between devices: 87 us -> 69.4 us
  Pallas kernels: 6.54 us -> 13.2 us
  local copies, waits for them, and re-layouts: 8.29 us -> 3.73 us
    all_to_all x1 -> x4, blocking collectives: 19.9 us -> 52.2 us  [the longest x1 15 us: with_plain(): chips = lax.all_to_all(to_all(chip, nzh), 'zh', 0, 0, tiled=True)]
    all_to_all x2 -> x0, waiting for transfers between devices: 23.1 us -> none  [the longest x1 13.8 us: on_device(): lax.all_to_all(sums.reshape(nblk, each, classes), BLK, 0, 0, tiled=True)]
    all_to_all x1 -> x2, blocking collectives: 16.9 us -> 35.7 us  [with_transpose(): parts = lax.all_to_all(parts, 'q', 0, 0, tiled=True).astype(F32)]
    all_to_all x2 -> x0, starting transfers between devices: 15.7 us -> none  [the longest x1 8.07 us: on_device(): lax.all_to_all(sums.reshape(nblk, each, classes), BLK, 0, 0, tiled=True)]
    all_to_all x2 -> x1, waiting for transfers between devices: 20.9 us -> 11.6 us  [with_plain(): chips = lax.all_to_all(to_all(chip, nzh), 'zh', 0, 0, tiled=True)]
    pallas_call x4, Pallas kernels: 6.54 us -> 13.2 us  [call(): pl.pallas_call(kernel, out_shape=shapes, in_specs=[smem] * len(scalars) +...]
    all_to_all x2 -> x1, starting transfers between devices: 7.32 us -> 3.41 us  [with_plain(): chips = lax.all_to_all(to_all(chip, nzh), 'zh', 0, 0, tiled=True)]
    unnamed x18 -> x14, local copies, waits for them, and re-layouts: 4.8 us -> 1.02 us
  transfers between devices with their start and end apart: 17 -> 14, of which waited for: 17 -> 14; matrix products, arithmetic and copies ran while one was open for 0% -> 0% of each run, Pallas kernels for 0% -> 0%
where the time goes in v4:
time: 348 us; the launch traced here: 347 us
  blocking collectives  181 us (52%)
  waiting for transfers between devices  70 us (20%)
  starting transfers between devices  69.4 us (20%)
  Pallas kernels  13.2 us (4%)
  other arithmetic  4.68 us (1%)
  local copies, waits for them, and re-layouts  3.73 us (1%)
    all_to_all x2, blocking collectives, with_transpose(): lax.all_to_all(to_all(total.astype(BF), nzh), yrep, 0, 0, axis_index_grou...  63.8 us
    all_to_all x2, blocking collectives, with_transpose(): parts = lax.all_to_all(parts, 'q', 0, 0, tiled=True).astype(F32)  35.7 us
    all_to_all x2, blocking collectives, with_plain(): near = lax.all_to_all(near, 'q', 0, 0, tiled=True)  29 us
    ppermute x2, waiting for transfers between devices, with_transpose(): parts = (mine + lax.ppermute(away, yrep, pairs).astype(F32)).astype(BF)  19.3 us
    ppermute x2, waiting for transfers between devices, with_plain(): far = lax.ppermute(near, yrep, pairs)  19.3 us
    ppermute x2, starting transfers between devices, with_plain(): far = lax.ppermute(near, yrep, pairs)  16.9 us
    all_to_all x1, blocking collectives, with_plain(): chips = lax.all_to_all(to_all(chip, nzh), 'zh', 0, 0, tiled=True)  15 us
    all_to_all x1, blocking collectives, on_device(): lax.all_to_all(to_all(sums, nq), 'q', 0, 0, tiled=True)  13.8 us
  transfers between devices with their start and end apart: 14, of which 14 were waited for; matrix products, arithmetic and copies ran while one was open for 0% of the time, Pallas kernels for 0%

profile of v4, /device:TPU:1, one launch (start us, length us, event | category | flops | bytes accessed | tf_op | source)
XLA Modules:
  0.0 347.3 jit_solution(8726330629216961967)
XLA Ops:
  0.7 1.0 copy-done
  1.7 1.5 fusion.4
  3.2 0.3 convolution_convert_fusion.1.panel_ref
  3.8 5.0 %shard_map.102 = (f32[12,256,128]{2,1,0:T(8,128)S(1)}, bf16[12,256,128]{2,1,0:T(8,128)(2,1)S(1)}) custom-call(s32[3]{0:T(128)S(1)} %get-tuple-element.26.place_ref, s32[2,12]{1,0:T(2,128)S(1)} %bitcast.47, s32[2,12]{1,0:T(2,128)S(1)} %bitcast.51, bf16[12,2,256,256]{3,2,1,0:T(8,128)(2,1)} %bitcast.43, bf16[512,128]{1,0:T(8,128)(2,1)S(1)} %convolution_convert_fusion.1.panel_ref), custom_call_target="tpu_custom_call" | custom-call | tf_op jit(solution)/shard_map/pallas_call | solution.py:81
  8.8 6.5 %collective-permute-start = (bf16[12,256,128]{2,1,0:T(8,128)(2,1)S(1)}, bf16[12,256,128]{2,1,0:T(8,128)(2,1)S(1)}, u32[]{:S(2)}, u32[]{:S(2)}) collective-permute-start(bf16[12,256,128]{2,1,0:T(8,128)(2,1)S(1)} %get-tuple-element.29), channel_id=1, source_target_pairs={{0,97},{97,0},{2,99},{99,2},{4,101},{101,4},{6,103},{103,6},{96,19... | collective-permute-start | bytes 2359304 | tf_op jit(solution)/shard_map/ppermute | solution.py:174
  15.3 9.7 %collective-permute-done = bf16[12,256,128]{2,1,0:T(8,128)(2,1)S(1)} collective-permute-done((bf16[12,256,128]{2,1,0:T(8,128)(2,1)S(1)}, bf16[12,256,128]{2,1,0:T(8,128)(2,1)S(1)}, u32[]{:S(2)}, u32[]{:S(2)}) %collective-permute-start) | collective-permute-done | bytes 786464 | tf_op jit(solution)/shard_map/ppermute | solution.py:174
  25.0 0.2 add_convert_fusion.1
  25.2 18.9 %all_to_all.55 = bf16[12,256,128]{2,1,0:T(8,128)(2,1)S(1)} all-to-all(bf16[12,256,128]{2,1,0:T(8,128)(2,1)S(1)} %add_convert_fusion.1), channel_id=1, replica_groups=mesh['y'=8,'q'=12,'zh'=4,'c'=2] {'q'}, dimensions={0} | all-to-all | bytes 1572864 | tf_op jit(solution)/shard_map/all_to_all | solution.py:175
  44.0 0.3 fusion.1
  44.3 4.1 %collective-permute-start.1 = (bf16[256,128]{1,0:T(8,128)(2,1)S(1)}, bf16[256,128]{1,0:T(8,128)(2,1)S(1)}, u32[]{:S(2)}, u32[]{:S(2)}) collective-permute-start(bf16[256,128]{1,0:T(8,128)(2,1)S(1)} %get-tuple-element.46), channel_id=1, source_target_pairs={{96,0},{192,96},{288,192},{384,288},{480,384},{576,480},{672,576},... | collective-permute-start | bytes 196616 | tf_op jit(solution)/shard_map/ppermute | solution.py:177
  48.4 4.5 %collective-permute-done.1 = bf16[256,128]{1,0:T(8,128)(2,1)S(1)} collective-permute-done((bf16[256,128]{1,0:T(8,128)(2,1)S(1)}, bf16[256,128]{1,0:T(8,128)(2,1)S(1)}, u32[]{:S(2)}, u32[]{:S(2)}) %collective-permute-start.1) | collective-permute-done | bytes 65568 | tf_op jit(solution)/shard_map/ppermute | solution.py:177
  52.9 37.6 %all_to_all.56 = bf16[4,256,128]{2,1,0:T(8,128)(2,1)S(1)} all-to-all(bf16[4,256,128]{2,1,0:T(8,128)(2,1)S(1)} %broadcast_in_dim.175), channel_id=1, replica_groups={{0,194,388,582},{97,291,485,679},{96,290,484,678},{193,387,581,7},{192,..., dimensions={0} | all-to-all | bytes 524288 | tf_op jit(solution)/shard_map/all_to_all | solution.py:179
  90.6 2.7 collective-permute-start.2
  93.4 3.5 %collective-permute-done.2 = bf16[256,128]{1,0:T(8,128)(2,1)S(1)} collective-permute-done((bf16[256,128]{1,0:T(8,128)(2,1)S(1)}, bf16[256,128]{1,0:T(8,128)(2,1)S(1)}, u32[]{:S(2)}, u32[]{:S(2)}) %collective-permute-start.2) | collective-permute-done | bytes 65568 | tf_op jit(solution)/shard_map/ppermute | solution.py:185
  96.9 14.5 %all_to_all.57.near_ref = bf16[12,256,128]{2,1,0:T(8,128)(2,1)S(1)} all-to-all(bf16[12,256,128]{2,1,0:T(8,128)(2,1)S(1)} %broadcast_select_fusion.1), channel_id=1, replica_groups=mesh['y'=8,'q'=12,'zh'=4,'c'=2] {'q'}, dimensions={0} | all-to-all | bytes 1572864 | tf_op jit(solution)/shard_map/all_to_all | solution.py:187
  111.4 9.4 %collective-permute-start.3 = (bf16[12,256,128]{2,1,0:T(8,128)(2,1)S(1)}, bf16[12,256,128]{2,1,0:T(8,128)(2,1)S(1)}, u32[]{:S(2)}, u32[]{:S(2)}) collective-permute-start(bf16[12,256,128]{2,1,0:T(8,128)(2,1)S(1)} %all_to_all.57.near_ref), channel_id=1, source_target_pairs={{0,97},{97,0},{2,99},{99,2},{4,101},{101,4},{6,103},{103,6},{96,19... | collective-permute-start | bytes 2359304 | tf_op jit(solution)/shard_map/ppermute | solution.py:188
  120.9 9.7 %collective-permute-done.3.far_ref = bf16[12,256,128]{2,1,0:T(8,128)(2,1)S(1)} collective-permute-done((bf16[12,256,128]{2,1,0:T(8,128)(2,1)S(1)}, bf16[12,256,128]{2,1,0:T(8,128)(2,1)S(1)}, u32[]{:S(2)}, u32[]{:S(2)}) %collective-permute-start.3) | collective-permute-done | bytes 786464 | tf_op jit(solution)/shard_map/ppermute | solution.py:188
  130.5 1.7 shard_map.103
  132.2 2.3 collective-permute-start.4
  134.5 0.9 collective-permute-done.4
  135.4 0.7 broadcast_in_dim.178
  136.1 3.4 all-to-all-start.3
  139.5 11.6 %all-to-all-done.3 = bf16[4,256,128]{2,1,0:T(8,128)(2,1)S(1)} async-done(((bf16[4,256,128]{2,1,0:T(8,128)(2,1)}), bf16[4,256,128]{2,1,0:T(8,128)(2,1)S(1)}, u32[]{:S(2)}, u32[]{:S(2)}) %all-to-all-start.3) | async-done | bytes 262176 | tf_op jit(solution)/shard_map/all_to_all | solution.py:200
  151.2 0.1 fusion.27
  151.3 0.2 fusion.12
  151.5 0.2 convert_bitcast_fusion.1
  151.8 7.9 %collective-permute-start.5 = (bf16[2,256,128]{2,1,0:T(8,128)(2,1)S(1)}, bf16[2,256,128]{2,1,0:T(8,128)(2,1)S(1)}, u32[]{:S(2)}, u32[]{:S(2)}) collective-permute-start(bf16[2,256,128]{2,1,0:T(8,128)(2,1)S(1)} %pad_maximum_fusion.2), channel_id=1, source_target_pairs={{0,1},{1,0},{2,3},{3,2},{4,5},{5,4},{6,7},{7,6},{8,9},{9,8},{10,11... | collective-permute-start | bytes 393224 | tf_op jit(solution)/shard_map/ppermute | solution.py:223
  159.7 1.0 collective-permute-done.5
  160.8 0.7 slice_bitcast_fusion
  161.4 5.0 %shard_map.104 = (f32[12,256,128]{2,1,0:T(8,128)S(1)}, bf16[12,256,128]{2,1,0:T(8,128)(2,1)S(1)}) custom-call(s32[3]{0:T(128)S(1)} %get-tuple-element.24.place_ref, s32[2,12]{1,0:T(2,128)S(1)} %bitcast.49, s32[2,12]{1,0:T(2,128)S(1)} %bitcast.53, bf16[12,2,256,256]{3,2,1,0:T(8,128)(2,1)} %bitcast.44, bf16[512,128]{1,0:T(8,128)(2,1)S(1)} %get-tuple-element.62.panel_ref), custom_call_target="tpu_custom_call" | custom-call | tf_op jit(solution)/shard_map/pallas_call | solution.py:81
  166.4 4.8 %collective-permute-start.6 = (bf16[12,256,128]{2,1,0:T(8,128)(2,1)S(1)}, bf16[12,256,128]{2,1,0:T(8,128)(2,1)S(1)}, u32[]{:S(2)}, u32[]{:S(2)}) collective-permute-start(bf16[12,256,128]{2,1,0:T(8,128)(2,1)S(1)} %get-tuple-element.37), channel_id=1, source_target_pairs={{0,97},{97,0},{2,99},{99,2},{4,101},{101,4},{6,103},{103,6},{96,19... | collective-permute-start | bytes 2359304 | tf_op jit(solution)/shard_map/ppermute | solution.py:174
  171.3 9.7 %collective-permute-done.6 = bf16[12,256,128]{2,1,0:T(8,128)(2,1)S(1)} collective-permute-done((bf16[12,256,128]{2,1,0:T(8,128)(2,1)S(1)}, bf16[12,256,128]{2,1,0:T(8,128)(2,1)S(1)}, u32[]{:S(2)}, u32[]{:S(2)}) %collective-permute-start.6) | collective-permute-done | bytes 786464 | tf_op jit(solution)/shard_map/ppermute | solution.py:174
  181.0 0.2 add_convert_fusion
  181.2 16.8 %all_to_all.58 = bf16[12,256,128]{2,1,0:T(8,128)(2,1)S(1)} all-to-all(bf16[12,256,128]{2,1,0:T(8,128)(2,1)S(1)} %add_convert_fusion), channel_id=1, replica_groups=mesh['y'=8,'q'=12,'zh'=4,'c'=2] {'q'}, dimensions={0} | all-to-all | bytes 1572864 | tf_op jit(solution)/shard_map/all_to_all | solution.py:175
  198.0 0.3 fusion.3
  198.3 1.9 collective-permute-start.7
  200.2 3.1 collective-permute-done.7
  203.4 26.2 %all_to_all.59 = bf16[4,256,128]{2,1,0:T(8,128)(2,1)S(1)} all-to-all(bf16[4,256,128]{2,1,0:T(8,128)(2,1)S(1)} %broadcast_in_dim.182), channel_id=1, replica_groups={{0,194,388,582},{97,291,485,679},{96,290,484,678},{193,387,581,7},{192,..., dimensions={0} | all-to-all | bytes 524288 | tf_op jit(solution)/shard_map/all_to_all | solution.py:179
  229.6 1.9 collective-permute-start.8
  231.5 4.3 %collective-permute-done.8 = bf16[256,128]{1,0:T(8,128)(2,1)S(1)} collective-permute-done((bf16[256,128]{1,0:T(8,128)(2,1)S(1)}, bf16[256,128]{1,0:T(8,128)(2,1)S(1)}, u32[]{:S(2)}, u32[]{:S(2)}) %collective-permute-start.8) | collective-permute-done | bytes 65568 | tf_op jit(solution)/shard_map/ppermute | solution.py:185
  235.9 14.5 %all_to_all.60.near_ref = bf16[12,256,128]{2,1,0:T(8,128)(2,1)S(1)} all-to-all(bf16[12,256,128]{2,1,0:T(8,128)(2,1)S(1)} %broadcast_select_fusion), channel_id=1, replica_groups=mesh['y'=8,'q'=12,'zh'=4,'c'=2] {'q'}, dimensions={0} | all-to-all | bytes 1572864 | tf_op jit(solution)/shard_map/all_to_all | solution.py:187
  250.3 7.5 %collective-permute-start.9 = (bf16[12,256,128]{2,1,0:T(8,128)(2,1)S(1)}, bf16[12,256,128]{2,1,0:T(8,128)(2,1)S(1)}, u32[]{:S(2)}, u32[]{:S(2)}) collective-permute-start(bf16[12,256,128]{2,1,0:T(8,128)(2,1)S(1)} %all_to_all.60.near_ref), channel_id=1, source_target_pairs={{0,97},{97,0},{2,99},{99,2},{4,101},{101,4},{6,103},{103,6},{96,19... | collective-permute-start | bytes 2359304 | tf_op jit(solution)/shard_map/ppermute | solution.py:188
  257.8 9.7 %collective-permute-done.9.far_ref = bf16[12,256,128]{2,1,0:T(8,128)(2,1)S(1)} collective-permute-done((bf16[12,256,128]{2,1,0:T(8,128)(2,1)S(1)}, bf16[12,256,128]{2,1,0:T(8,128)(2,1)S(1)}, u32[]{:S(2)}, u32[]{:S(2)}) %collective-permute-start.9) | collective-permute-done | bytes 786464 | tf_op jit(solution)/shard_map/ppermute | solution.py:188
  267.5 1.6 shard_map.105
  269.1 4.1 %collective-permute-start.10 = (bf16[256,128]{1,0:T(8,128)(2,1)S(1)}, bf16[256,128]{1,0:T(8,128)(2,1)S(1)}, u32[]{:S(2)}, u32[]{:S(2)}) collective-permute-start(bf16[256,128]{1,0:T(8,128)(2,1)S(1)} %get-tuple-element.39), channel_id=1, source_target_pairs={{0,1},{1,0},{2,3},{3,2},{4,5},{5,4},{6,7},{7,6},{8,9},{9,8},{10,11... | collective-permute-start | bytes 196616 | tf_op jit(solution)/shard_map/ppermute | solution.py:199
  273.2 0.9 collective-permute-done.10
  274.2 15.0 %all_to_all.61 = bf16[4,256,128]{2,1,0:T(8,128)(2,1)S(1)} all-to-all(bf16[4,256,128]{2,1,0:T(8,128)(2,1)S(1)} %broadcast_in_dim.185), channel_id=1, replica_groups=mesh['y'=8,'q'=12,'zh'=4,'c'=2] {'zh'}, dimensions={0} | all-to-all | bytes 524288 | tf_op jit(solution)/shard_map/all_to_all | solution.py:200
  289.3 7.4 %collective-permute-start.11 = (bf16[256,128]{1,0:T(8,128)(2,1)S(1)}, bf16[256,128]{1,0:T(8,128)(2,1)S(1)}, u32[]{:S(2)}, u32[]{:S(2)}) collective-permute-start(bf16[256,128]{1,0:T(8,128)(2,1)S(1)} %add_convert_fusion.2), channel_id=1, source_target_pairs={{0,1},{1,0},{2,3},{3,2},{4,5},{5,4},{6,7},{7,6},{8,9},{9,8},{10,11... | collective-permute-start | bytes 196616 | tf_op jit(solution)/shard_map/ppermute | solution.py:228
  296.6 0.1 copy.23
  296.8 0.1 copy.24
  296.9 0.1 copy.25
  297.0 0.5 collective-permute-done.11
  297.5 0.6 fusion.6
  298.1 0.2 convolution_convert_fusion.2
  298.4 0.1 concatenate.25
  298.5 0.2 copy.26
  298.7 10.5 %all_to_all.62 = bf16[12,112,128]{2,1,0:T(8,128)(2,1)S(1)} all-to-all(bf16[12,112,128]{2,1,0:T(8,128)(2,1)S(1)} %bitcast.55), channel_id=1, replica_groups=mesh['y'=8,'q'=12,'zh'=4,'c'=2] {'q'}, dimensions={0} | all-to-all | bytes 688128 | tf_op jit(solution)/shard_map/all_to_all | solution.py:245
  309.4 12.9 %all_to_all.63 = bf16[8,112,128]{2,1,0:T(8,128)(2,1)S(1)} all-to-all(bf16[8,112,128]{2,1,0:T(8,128)(2,1)S(1)} %broadcast_in_dim.191), channel_id=1, replica_groups=mesh['y'=8,'q'=12,'zh'=4,'c'=2] {'y'}, dimensions={0} | all-to-all | bytes 458752 | tf_op jit(solution)/shard_map/all_to_all | solution.py:246
  322.4 13.8 %all_to_all.64 = bf16[12,112,128]{2,1,0:T(8,128)(2,1)S(1)} all-to-all(bf16[12,112,128]{2,1,0:T(8,128)(2,1)S(1)} %broadcast_in_dim.195), channel_id=1, replica_groups=mesh['y'=8,'q'=12,'zh'=4,'c'=2] {'q'}, dimensions={0} | all-to-all | bytes 688128 | tf_op jit(solution)/shard_map/all_to_all | solution.py:247
  336.2 5.4 %collective-permute-start.12 = (bf16[1344,128]{1,0:T(8,128)(2,1)S(1)}, bf16[1344,128]{1,0:T(8,128)(2,1)S(1)}, u32[]{:S(2)}, u32[]{:S(2)}) collective-permute-start(bf16[1344,128]{1,0:T(8,128)(2,1)S(1)} %bitcast.56), channel_id=1, source_target_pairs={{0,1},{1,0},{2,3},{3,2},{4,5},{5,4},{6,7},{7,6},{8,9},{9,8},{10,11... | collective-permute-start | bytes 1032200 | tf_op jit(solution)/shard_map/ppermute | solution.py:248
  341.7 1.3 collective-permute-done.12
  343.2 0.6 fusion.15
  343.8 0.7 pad_maximum_fusion.1
  345.1 1.0 pad_maximum_fusion
  (59 shorter events, 1.5 us)
Async XLA Ops:
  0.6 1.0 copy-start
  0.6 2.5 copy-start.5
  0.7 2.8 copy-start.6
  0.7 3.1 copy-start.3
  0.7 3.1 copy-start.4
  8.8 16.2 %collective-permute-start = (bf16[12,256,128]{2,1,0:T(8,128)(2,1)S(1)}, bf16[12,256,128]{2,1,0:T(8,128)(2,1)S(1)}, u32[]{:S(2)}, u32[]{:S(2)}) collective-permute-start(bf16[12,256,128]{2,1,0:T(8,128)(2,1)S(1)} %get-tuple-element.29), channel_id=1, source_target_pairs={{0,97},{97,0},{2,99},{99,2},{4,101},{101,4},{6,103},{103,6},{96,19... | collective-permute-start | bytes 2359304 | tf_op jit(solution)/shard_map/ppermute | solution.py:174
  44.3 8.5 %collective-permute-start.1 = (bf16[256,128]{1,0:T(8,128)(2,1)S(1)}, bf16[256,128]{1,0:T(8,128)(2,1)S(1)}, u32[]{:S(2)}, u32[]{:S(2)}) collective-permute-start(bf16[256,128]{1,0:T(8,128)(2,1)S(1)} %get-tuple-element.46), channel_id=1, source_target_pairs={{96,0},{192,96},{288,192},{384,288},{480,384},{576,480},{672,576},... | collective-permute-start | bytes 196616 | tf_op jit(solution)/shard_map/ppermute | solution.py:177
  52.9 77.6 %copy-start.1 = (bf16[1,1,12,2,256,256]{5,4,3,2,1,0:T(8,128)(2,1)S(1)}, bf16[1,1,12,2,256,256]{5,4,3,2,1,0:T(8,128)(2,1)}, u32[]{:S(2)}) copy-start(bf16[1,1,12,2,256,256]{5,4,3,2,1,0:T(8,128)(2,1)} %param.13) | copy-start | bytes 9437188
  90.6 6.2 %collective-permute-start.2 = (bf16[256,128]{1,0:T(8,128)(2,1)S(1)}, bf16[256,128]{1,0:T(8,128)(2,1)S(1)}, u32[]{:S(2)}, u32[]{:S(2)}) collective-permute-start(bf16[256,128]{1,0:T(8,128)(2,1)S(1)} %multiply_convert_fusion.1), channel_id=1, source_target_pairs={{0,96},{96,192},{192,288},{288,384},{384,480},{480,576},{576,672},... | collective-permute-start | bytes 196616 | tf_op jit(solution)/shard_map/ppermute | solution.py:185
  111.4 19.1 %collective-permute-start.3 = (bf16[12,256,128]{2,1,0:T(8,128)(2,1)S(1)}, bf16[12,256,128]{2,1,0:T(8,128)(2,1)S(1)}, u32[]{:S(2)}, u32[]{:S(2)}) collective-permute-start(bf16[12,256,128]{2,1,0:T(8,128)(2,1)S(1)} %all_to_all.57.near_ref), channel_id=1, source_target_pairs={{0,97},{97,0},{2,99},{99,2},{4,101},{101,4},{6,103},{103,6},{96,19... | collective-permute-start | bytes 2359304 | tf_op jit(solution)/shard_map/ppermute | solution.py:188
  132.2 3.1 collective-permute-start.4
  136.1 15.1 %all-to-all-start.3 = ((bf16[4,256,128]{2,1,0:T(8,128)(2,1)}), bf16[4,256,128]{2,1,0:T(8,128)(2,1)S(1)}, u32[]{:S(2)}, u32[]{:S(2)}) async-start(bf16[4,256,128]{2,1,0:T(8,128)(2,1)} %broadcast_in_dim.178), calls=%async_computation.3 | async-start | bytes 524288 | tf_op jit(solution)/shard_map/all_to_all | solution.py:200
  151.8 8.9 %collective-permute-start.5 = (bf16[2,256,128]{2,1,0:T(8,128)(2,1)S(1)}, bf16[2,256,128]{2,1,0:T(8,128)(2,1)S(1)}, u32[]{:S(2)}, u32[]{:S(2)}) collective-permute-start(bf16[2,256,128]{2,1,0:T(8,128)(2,1)S(1)} %pad_maximum_fusion.2), channel_id=1, source_target_pairs={{0,1},{1,0},{2,3},{3,2},{4,5},{5,4},{6,7},{7,6},{8,9},{9,8},{10,11... | collective-permute-start | bytes 393224 | tf_op jit(solution)/shard_map/ppermute | solution.py:223
  166.4 14.5 %collective-permute-start.6 = (bf16[12,256,128]{2,1,0:T(8,128)(2,1)S(1)}, bf16[12,256,128]{2,1,0:T(8,128)(2,1)S(1)}, u32[]{:S(2)}, u32[]{:S(2)}) collective-permute-start(bf16[12,256,128]{2,1,0:T(8,128)(2,1)S(1)} %get-tuple-element.37), channel_id=1, source_target_pairs={{0,97},{97,0},{2,99},{99,2},{4,101},{101,4},{6,103},{103,6},{96,19... | collective-permute-start | bytes 2359304 | tf_op jit(solution)/shard_map/ppermute | solution.py:174
  198.3 5.0 %collective-permute-start.7 = (bf16[256,128]{1,0:T(8,128)(2,1)S(1)}, bf16[256,128]{1,0:T(8,128)(2,1)S(1)}, u32[]{:S(2)}, u32[]{:S(2)}) collective-permute-start(bf16[256,128]{1,0:T(8,128)(2,1)S(1)} %get-tuple-element.44), channel_id=1, source_target_pairs={{96,0},{192,96},{288,192},{384,288},{480,384},{576,480},{672,576},... | collective-permute-start | bytes 196616 | tf_op jit(solution)/shard_map/ppermute | solution.py:177
  203.3 64.2 %copy-start.2 = (bf16[1,1,12,2,256,256]{5,4,3,2,1,0:T(8,128)(2,1)S(1)}, bf16[1,1,12,2,256,256]{5,4,3,2,1,0:T(8,128)(2,1)}, u32[]{:S(2)}) copy-start(bf16[1,1,12,2,256,256]{5,4,3,2,1,0:T(8,128)(2,1)} %param.13) | copy-start | bytes 9437188
  229.6 6.2 %collective-permute-start.8 = (bf16[256,128]{1,0:T(8,128)(2,1)S(1)}, bf16[256,128]{1,0:T(8,128)(2,1)S(1)}, u32[]{:S(2)}, u32[]{:S(2)}) collective-permute-start(bf16[256,128]{1,0:T(8,128)(2,1)S(1)} %multiply_convert_fusion), channel_id=1, source_target_pairs={{0,96},{96,192},{192,288},{288,384},{384,480},{480,576},{576,672},... | collective-permute-start | bytes 196616 | tf_op jit(solution)/shard_map/ppermute | solution.py:185
  250.3 17.2 %collective-permute-start.9 = (bf16[12,256,128]{2,1,0:T(8,128)(2,1)S(1)}, bf16[12,256,128]{2,1,0:T(8,128)(2,1)S(1)}, u32[]{:S(2)}, u32[]{:S(2)}) collective-permute-start(bf16[12,256,128]{2,1,0:T(8,128)(2,1)S(1)} %all_to_all.60.near_ref), channel_id=1, source_target_pairs={{0,97},{97,0},{2,99},{99,2},{4,101},{101,4},{6,103},{103,6},{96,19... | collective-permute-start | bytes 2359304 | tf_op jit(solution)/shard_map/ppermute | solution.py:188
  269.1 5.0 %collective-permute-start.10 = (bf16[256,128]{1,0:T(8,128)(2,1)S(1)}, bf16[256,128]{1,0:T(8,128)(2,1)S(1)}, u32[]{:S(2)}, u32[]{:S(2)}) collective-permute-start(bf16[256,128]{1,0:T(8,128)(2,1)S(1)} %get-tuple-element.39), channel_id=1, source_target_pairs={{0,1},{1,0},{2,3},{3,2},{4,5},{5,4},{6,7},{7,6},{8,9},{9,8},{10,11... | collective-permute-start | bytes 196616 | tf_op jit(solution)/shard_map/ppermute | solution.py:199
  289.3 8.3 %collective-permute-start.11 = (bf16[256,128]{1,0:T(8,128)(2,1)S(1)}, bf16[256,128]{1,0:T(8,128)(2,1)S(1)}, u32[]{:S(2)}, u32[]{:S(2)}) collective-permute-start(bf16[256,128]{1,0:T(8,128)(2,1)S(1)} %add_convert_fusion.2), channel_id=1, source_target_pairs={{0,1},{1,0},{2,3},{3,2},{4,5},{5,4},{6,7},{7,6},{8,9},{9,8},{10,11... | collective-permute-start | bytes 196616 | tf_op jit(solution)/shard_map/ppermute | solution.py:228
  336.2 6.7 %collective-permute-start.12 = (bf16[1344,128]{1,0:T(8,128)(2,1)S(1)}, bf16[1344,128]{1,0:T(8,128)(2,1)S(1)}, u32[]{:S(2)}, u32[]{:S(2)}) collective-permute-start(bf16[1344,128]{1,0:T(8,128)(2,1)S(1)} %bitcast.56), channel_id=1, source_target_pairs={{0,1},{1,0},{2,3},{3,2},{4,5},{5,4},{6,7},{7,6},{8,9},{9,8},{10,11... | collective-permute-start | bytes 1032200 | tf_op jit(solution)/shard_map/ppermute | solution.py:248

commit v5 on v4

--- a/solution.py
+++ b/solution.py
@@ -16,21 +16,16 @@
 BLK = ("y", "q")
 
 
-def scatter_kernel(
-    place_ref, rows_ref, cols_ref, far_tiles_ref, panel_ref, mine_ref, away_ref, tiles_ref, arrived
-):
+def share_of(flag):
+    return jnp.where(flag == 1, ALPHA / (1.0 - ALPHA), 0.0).astype(F32)
+
+
+def scatter_kernel(place_ref, rows_ref, cols_ref, tiles_ref, panel_ref, mine_ref, away_ref):
     steps, slots, width, _ = tiles_ref.shape
     q = place_ref[0]
     c = place_ref[1]
-    share = jnp.where(place_ref[2] == 1, ALPHA / (1.0 - ALPHA), 0.0).astype(F32)
-    copies = [
-        pltpu.make_async_copy(far_tiles_ref.at[t], tiles_ref.at[t], arrived.at[t])
-        for t in range(steps)
-    ]
-    for copy in copies:
-        copy.start()
+    share = share_of(place_ref[2])
     for t in range(steps):
-        copies[t].wait()
         place = lax.rem(q + (steps - t), steps)
         products = []
         for p in range(slots):
@@ -53,42 +48,102 @@
             out_ref[place] = total.astype(out_ref.dtype)
 
 
-def gather_kernel(
-    place_ref, rows_ref, cols_ref, tiles_ref, near_ref, far_ref, mine_ref, away_ref, sum_ref
+def first_kernel(
+    place_ref,
+    rows_ref,
+    cols_ref,
+    far_tiles_ref,
+    far_features_ref,
+    far_first_ref,
+    far_second_ref,
+    mine_ref,
+    away_ref,
+    tiles_ref,
+    hidden_ref,
+    base_ref,
+    features_ref,
+    first_ref,
+    second_ref,
+    arrived,
 ):
+    copies = [
+        pltpu.make_async_copy(source, target, arrived.at[k])
+        for k, (source, target) in enumerate(
+            (
+                (far_features_ref, features_ref),
+                (far_first_ref, first_ref),
+                (far_second_ref, second_ref),
+                (far_tiles_ref, tiles_ref),
+            )
+        )
+    ]
+    for copy in copies:
+        copy.start()
+    copies[0].wait()
+    copies[1].wait()
+    hidden = jnp.dot(features_ref[...], first_ref[...], preferred_element_type=F32)
+    hidden_ref[...] = jnp.maximum(hidden, 0.0).astype(BF)
+    copies[2].wait()
+    base = jnp.dot(hidden_ref[...], second_ref[...], preferred_element_type=F32)
+    base_ref[...] = base.astype(BF)
+    copies[3].wait()
+    scatter_kernel(place_ref, rows_ref, cols_ref, tiles_ref, base_ref, mine_ref, away_ref)
+
+
+def add_gathered(place_ref, rows_ref, cols_ref, tiles_ref, near_ref, far_ref, sum_ref):
     steps, slots, width, _ = tiles_ref.shape
     q = place_ref[0]
     c = place_ref[1]
-    share = jnp.where(place_ref[2] == 1, ALPHA / (1.0 - ALPHA), 0.0).astype(F32)
-    mine = pl.ds(pl.multiple_of(c * width, width), width)
-    away = pl.ds(pl.multiple_of((1 - c) * width, width), width)
-    sum_ref[mine, :] = share * near_ref[q].astype(F32)
-    sum_ref[away, :] = share * far_ref[q].astype(F32)
     for t in range(steps):
         place = lax.rem(q + (steps - t), steps)
         for p in range(slots):
             piece = jnp.where(cols_ref[p, t] == c, near_ref[place], far_ref[place])
             rows = pl.ds(pl.multiple_of(rows_ref[p, t] * width, width), width)
             sum_ref[rows, :] += jnp.dot(tiles_ref[t, p], piece, preferred_element_type=F32)
+
+
+def core_rows(place_ref, width):
+    c = place_ref[1]
+    return [pl.ds(pl.multiple_of(k * width, width), width) for k in (c, 1 - c)]
+
+
+def gather_kernel(
+    place_ref, rows_ref, cols_ref, tiles_ref, near_ref, far_ref, mine_ref, away_ref, sum_ref
+):
+    mine, away = core_rows(place_ref, tiles_ref.shape[2])
+    sum_ref[...] = jnp.zeros(sum_ref.shape, F32)
+    add_gathered(place_ref, rows_ref, cols_ref, tiles_ref, near_ref, far_ref, sum_ref)
     mine_ref[...] = sum_ref[mine, :]
     away_ref[...] = sum_ref[away, :].astype(BF)
 
 
-def call(kernel, outs, scalars, tiles, operands, scratch, tiles_space, interpret):
+def last_kernel(
+    place_ref, rows_ref, cols_ref, tiles_ref, near_ref, far_ref, grad_ref, out_ref, sum_ref
+):
+    mine, away = core_rows(place_ref, tiles_ref.shape[2])
+    q = place_ref[0]
+    share = share_of(place_ref[2])
+    sum_ref[mine, :] = share * (near_ref[q].astype(F32) + grad_ref[mine, :].astype(F32))
+    sum_ref[away, :] = share * (far_ref[q].astype(F32) + grad_ref[away, :].astype(F32))
+    add_gathered(place_ref, rows_ref, cols_ref, tiles_ref, near_ref, far_ref, sum_ref)
+    out_ref[...] = ((1.0 - ALPHA) * sum_ref[...]).astype(BF)
+
+
+def call(kernel, outs, scalars, operands, scratch=(), space=pltpu.VMEM, interpret=False):
     vmem = pl.BlockSpec(memory_space=pltpu.VMEM)
     smem = pl.BlockSpec(memory_space=pltpu.SMEM)
     shapes = [jax.ShapeDtypeStruct(shape, dtype) for shape, dtype in outs]
+    if not interpret:
+        operands = [pltpu.with_memory_space_constraint(v, space) for v in operands]
     return pl.pallas_call(
         kernel,
         out_shape=shapes,
-        in_specs=[smem] * len(scalars)
-        + [pl.BlockSpec(memory_space=tiles_space)]
-        + [vmem] * len(operands),
+        in_specs=[smem] * len(scalars) + [pl.BlockSpec(memory_space=space)] * len(operands),
         out_specs=[vmem] * len(outs),
         scratch_shapes=list(scratch),
         compiler_params=pltpu.CompilerParams(vmem_limit_bytes=16 << 20),
         interpret=interpret,
-    )(*scalars, tiles, *operands)
+    )(*scalars, *operands)
 
 
 def on_device(interpret, features, labels, w_first, w_second, block_rows, block_cols, block_vals):
@@ -102,7 +157,6 @@
     rep_id = lax.axis_index(REP)
     nodes = nodes_here * nblk
     tiles = block_vals[0, 0]
-    far_tiles = pltpu.with_memory_space_constraint(tiles, pltpu.HBM)
     steps = tiles.shape[0]
     half = nodes_here // nc
     yrep = ("y",) + REP
@@ -160,17 +214,7 @@
             jnp.concatenate([other, mine], axis=-2),
         )
 
-    def with_transpose(panel, where):
-        mine, away = call(
-            scatter_kernel,
-            [((steps, half, classes), F32), ((steps, half, classes), BF)],
-            [where] + scalars,
-            far_tiles,
-            [panel],
-            [pltpu.VMEM(tiles.shape, BF), pltpu.SemaphoreType.DMA((steps,))],
-            pltpu.HBM,
-            interpret,
-        )
+    def reduced(mine, away):
         parts = (mine + lax.ppermute(away, yrep, pairs).astype(F32)).astype(BF)
         parts = lax.all_to_all(parts, "q", 0, 0, tiled=True).astype(F32)
         before = jnp.sum(jnp.where(from_same, 0.0, parts), axis=0).astype(BF)
@@ -181,68 +225,91 @@
         )
         return ((1.0 - ALPHA) * jnp.sum(group.astype(F32), axis=0)).astype(BF)
 
-    def with_plain(here, where):
+    def gathered(here):
         before = lax.ppermute(here, "y", [(i, (i + 1) % ny) for i in range(ny)])
         near = jnp.where(from_same, here[None], before[None])
         near = lax.all_to_all(near, "q", 0, 0, tiled=True)
-        far = lax.ppermute(near, yrep, pairs)
-        mine, away = call(
-            gather_kernel,
-            [((half, classes), F32), ((half, classes), BF)],
-            [where] + scalars,
-            tiles,
-            [near, far],
-            [pltpu.VMEM((nodes_here, classes), F32)],
-            pltpu.VMEM,
-            interpret,
-        )
-        chip = (mine + lax.ppermute(away, "c", cores).astype(F32)).astype(BF)
-        chips = lax.all_to_all(to_all(chip, nzh), "zh", 0, 0, tiled=True)
-        return (1.0 - ALPHA) * jnp.sum(chips.astype(F32), axis=0)
-
-    hidden = jax.nn.relu(jnp.dot(features, w_first, preferred_element_type=F32)).astype(BF)
-    base = jnp.dot(hidden, w_second, preferred_element_type=F32).astype(BF)
+        return near, lax.ppermute(near, yrep, pairs)
+
+    slots_here = [((steps, half, classes), F32), ((steps, half, classes), BF)]
+    sum_here = pltpu.VMEM((nodes_here, classes), F32)
+    labels_half, plain, diagonal, from_same, loss_row = lax.optimization_barrier(
+        (labels_half, plain, diagonal, from_same, loss_row)
+    )
+    operands = (tiles, features, w_first, w_second)
+    mine, away, tiles, hidden, base = call(
+        first_kernel,
+        slots_here
+        + [(tiles.shape, BF), ((nodes_here, w_first.shape[1]), BF), ((nodes_here, classes), BF)],
+        [diagonal] + scalars,
+        operands,
+        [pltpu.VMEM(v.shape, BF) for v in operands[1:]] + [pltpu.SemaphoreType.DMA((4,))],
+        pltpu.HBM,
+        interpret=interpret,
+    )
     base_half = lax.dynamic_slice_in_dim(base, c_id * half, half, 0)
-    base, base_half, labels_half, plain, diagonal, from_same, loss_row = lax.optimization_barrier(
-        (base, base_half, labels_half, plain, diagonal, from_same, loss_row)
-    )
-
-    current = with_transpose(base, diagonal)
-    mixed = with_plain(current, plain) + ALPHA * base_half.astype(F32)
-    onehot = (labels_half[:, None] == jnp.arange(classes, dtype=jnp.int32)[None, :]).astype(F32)
+    near, far = gathered(reduced(mine, away))
+    mine, away = call(
+        gather_kernel,
+        [((half, classes), F32), ((half, classes), BF)],
+        [plain] + scalars,
+        [tiles, near, far],
+        [sum_here],
+        interpret=interpret,
+    )
+    chip = (mine + lax.ppermute(away, "c", cores).astype(F32)).astype(BF)
+    chips = lax.all_to_all(to_all(chip, nzh), "zh", 0, 0, tiled=True)
+    mixed = (1.0 - ALPHA) * jnp.sum(chips.astype(F32), axis=0) + ALPHA * base_half.astype(F32)
+    chosen = labels_half[:, None] == jnp.arange(classes, dtype=jnp.int32)[None, :]
     top = jnp.max(mixed, axis=1, keepdims=True)
     grown = jnp.exp(mixed - top)
     mass = jnp.sum(grown, axis=1, keepdims=True)
-    lanes = lax.broadcasted_iota(jnp.int32, (1, classes), 1)
-    ce_rows = jnp.where(lanes == 0, jnp.log(mass) + top, 0.0) - mixed * onehot
-    ce_terms = in_terms(jnp.sum(ce_rows, axis=0, keepdims=True))
-    grad_out = (grown / mass - onehot) * (1.0 / math.sqrt(nodes))
-    both, ce_terms, grad_out = lax.optimization_barrier(
-        (jnp.stack([grad_out.astype(BF), mixed.astype(BF)]), ce_terms, grad_out)
+    ce_rows = jnp.where(chosen, jnp.log(mass) + top - mixed, 0.0)
+    ce_sum = jnp.sum(ce_rows, axis=0, keepdims=True)
+    ce_terms = in_terms(jnp.where(lax.axis_index("zh") == 0, ce_sum, 0.0))
+    grad_out = (grown / mass - chosen.astype(F32)) * (1.0 / math.sqrt(nodes))
+    both, ce_terms = lax.optimization_barrier(
+        (jnp.stack([grad_out.astype(BF), mixed.astype(BF)]), ce_terms)
     )
     both = whole(both, lax.ppermute(both, "c", cores))
     moving, logits = both[0], both[1]
 
-    moving = with_transpose(moving, plain)
-    grad_half = (with_plain(moving, diagonal) + ALPHA * grad_out).astype(BF)
-    grad_b = whole(grad_half, lax.ppermute(grad_half, "c", cores))
-
-    hidden_part = lax.dynamic_slice_in_dim(hidden, c_id * part, part, 1)
-    second_part = lax.dynamic_slice_in_dim(w_second, c_id * part, part, 0)
-    back = lax.dot_general(grad_b, second_part, (((1,), (1,)), ((), ())), preferred_element_type=F32)
-    grad_hidden = jnp.where(hidden_part > 0, back, 0.0).astype(BF)
-    first = lax.dot_general(
-        features, grad_hidden, (((0,), (0,)), ((), ())), preferred_element_type=F32
-    ).astype(BF)
-    second = lax.dot_general(
-        hidden_part, grad_b, (((0,), (0,)), ((), ())), preferred_element_type=F32
-    ).astype(BF)
-
+    mine, away = call(
+        scatter_kernel, slots_here, [plain] + scalars, [tiles, moving], interpret=interpret
+    )
+    near, far = gathered(reduced(mine, away))
+    (grad_b,) = call(
+        last_kernel,
+        [((nodes_here, classes), BF)],
+        [diagonal] + scalars,
+        [tiles, near, far, moving],
+        [sum_here],
+        interpret=interpret,
+    )
+
+    def weight_rows(core):
+        hidden_part = lax.dynamic_slice_in_dim(hidden, core * part, part, 1)
+        second_part = lax.dynamic_slice_in_dim(w_second, core * part, part, 0)
+        back = lax.dot_general(
+            grad_b, second_part, (((1,), (1,)), ((), ())), preferred_element_type=F32
+        )
+        grad_hidden = jnp.where(hidden_part > 0, back, 0.0).astype(BF)
+        first = lax.dot_general(
+            features, grad_hidden, (((0,), (0,)), ((), ())), preferred_element_type=F32
+        )
+        second = lax.dot_general(
+            hidden_part, grad_b, (((0,), (0,)), ((), ())), preferred_element_type=F32
+        )
+        bands_here = [first[:, k * classes : (k + 1) * classes] for k in range(bands)]
+        return jnp.concatenate(bands_here + [second])
+
+    away = lax.ppermute(weight_rows(1 - c_id).astype(BF), "c", cores)
+    sums = (weight_rows(c_id) + away.astype(F32)).astype(BF)
     sums = jnp.concatenate(
-        [first[:, k * classes : (k + 1) * classes] for k in range(bands)]
-        + [second, *ce_terms, jnp.zeros((each * nq - used - 3, classes), BF)]
+        [sums, *ce_terms, jnp.zeros((each * nq - used - 3, classes), BF)]
     ).reshape(nq, each, classes)
     sums = summed(lax.all_to_all(sums, "q", 0, 0, tiled=True))
+    sums = summed(lax.all_to_all(to_all(sums, nzh), "zh", 0, 0, tiled=True))
     sums = summed(lax.all_to_all(to_all(sums, ny), "y", 0, 0, tiled=True))
     sums = lax.all_to_all(to_all(sums, nq), "q", 0, 0, tiled=True).reshape(nq * each, classes)
     other = lax.ppermute(sums, "c", cores)

time: 348 us -> 340 us (0.977)
  starting transfers between devices: 69.4 us -> 63 us
  local copies, waits for them, and re-layouts: 3.73 us -> 8.55 us
    ppermute x11 -> x10, starting transfers between devices: 52.6 us -> 45.3 us  [the longest x2 16.9 us: gathered(): return (near, lax.ppermute(near, yrep, pairs))]
    pallas_call x4, Pallas kernels: 13.2 us -> 9.72 us  [call(): pl.pallas_call(kernel, out_shape=shapes, in_specs=[smem] * len(scalars) +...]
    ppermute x11 -> x10, waiting for transfers between devices: 56.2 us -> 54 us  [the longest x2 19.4 us: reduced(): parts = (mine + lax.ppermute(away, yrep, pairs).astype(F32)).astype(BF)]
  transfers between devices with their start and end apart: 14 -> 13, of which waited for: 14 -> 13; matrix products, arithmetic and copies ran while one was open for 0% -> 1% of each run, Pallas kernels for 0% -> 0%
where the time goes in v5:
time: 340 us; the launch traced here: 339 us
  blocking collectives  178 us (52%)
  waiting for transfers between devices  67.8 us (20%)
  starting transfers between devices  63 us (19%)
  Pallas kernels  9.72 us (3%)
  local copies, waits for them, and re-layouts  8.55 us (3%)
  other arithmetic  5.42 us (2%)
    all_to_all x2, blocking collectives, reduced(): lax.all_to_all(to_all(total.astype(BF), nzh), yrep, 0, 0, axis_index_grou...  63.3 us
    all_to_all x2, blocking collectives, reduced(): parts = lax.all_to_all(parts, 'q', 0, 0, tiled=True).astype(F32)  35.7 us
    all_to_all x2, blocking collectives, gathered(): near = lax.all_to_all(near, 'q', 0, 0, tiled=True)  29.1 us
    ppermute x2, waiting for transfers between devices, reduced(): parts = (mine + lax.ppermute(away, yrep, pairs).astype(F32)).astype(BF)  19.4 us
    ppermute x2, waiting for transfers between devices, gathered(): return (near, lax.ppermute(near, yrep, pairs))  17.4 us
    ppermute x2, starting transfers between devices, gathered(): return (near, lax.ppermute(near, yrep, pairs))  16.9 us
    all_to_all x1, blocking collectives, on_device(): sums = summed(lax.all_to_all(to_all(sums, nzh), 'zh', 0, 0, tiled=True))  14.8 us
    all_to_all x1, blocking collectives, on_device(): lax.all_to_all(to_all(sums, nq), 'q', 0, 0, tiled=True)  13.5 us
  transfers between devices with their start and end apart: 13, of which 13 were waited for; matrix products, arithmetic and copies ran while one was open for 1% of the time, Pallas kernels for 0%

profile of v5, /device:TPU:1, one launch (start us, length us, event | category | flops | bytes accessed | tf_op | source)
XLA Modules:
  0.0 338.9 jit_solution(12216016513339876663)
XLA Ops:
  0.7 1.3 dynamic_slice.18
  2.2 0.7 iota.19
  2.9 0.7 copy-done.2
  3.5 0.7 copy-done.4
  4.2 4.0 %shard_map.102 = (f32[12,256,128]{2,1,0:T(8,128)S(1)}, bf16[12,256,128]{2,1,0:T(8,128)(2,1)S(1)}, bf16[12,2,256,256]{3,2,1,0:T(8,128)(2,1)S(1)}, bf16[512,512]{1,0:T(8,128)(2,1)S(1)}, bf16[512,128]{1,0:T(8,128)(2,1)S(1)}) custom-call(s32[3]{0:T(128)S(1)} %get-tuple-element.23.place_ref, s32[2,12]{1,0:T(2,128)S(1)} %bitcast.41, s32[2,12]{1,0:T(2,128)S(1)} %bitcast.45, ...), custom_call_target="tpu_custom_call" | custom-call | tf_op jit(solution)/shard_map/pallas_call | solution.py:138
  8.3 0.8 copy-done
  9.0 6.5 %collective-permute-start = (bf16[12,256,128]{2,1,0:T(8,128)(2,1)S(1)}, bf16[12,256,128]{2,1,0:T(8,128)(2,1)S(1)}, u32[]{:S(2)}, u32[]{:S(2)}) collective-permute-start(bf16[12,256,128]{2,1,0:T(8,128)(2,1)S(1)} %get-tuple-element.27), channel_id=1, source_target_pairs={{0,97},{97,0},{2,99},{99,2},{4,101},{101,4},{6,103},{103,6},{96,19... | collective-permute-start | bytes 2359304 | tf_op jit(solution)/shard_map/ppermute | solution.py:218
  15.5 9.7 %collective-permute-done = bf16[12,256,128]{2,1,0:T(8,128)(2,1)S(1)} collective-permute-done((bf16[12,256,128]{2,1,0:T(8,128)(2,1)S(1)}, bf16[12,256,128]{2,1,0:T(8,128)(2,1)S(1)}, u32[]{:S(2)}, u32[]{:S(2)}) %collective-permute-start) | collective-permute-done | bytes 786464 | tf_op jit(solution)/shard_map/ppermute | solution.py:218
  25.2 0.2 add_convert_fusion.1
  25.4 18.9 %all_to_all.55 = bf16[12,256,128]{2,1,0:T(8,128)(2,1)S(1)} all-to-all(bf16[12,256,128]{2,1,0:T(8,128)(2,1)S(1)} %add_convert_fusion.1), channel_id=1, replica_groups=mesh['y'=8,'q'=12,'zh'=4,'c'=2] {'q'}, dimensions={0} | all-to-all | bytes 1572864 | tf_op jit(solution)/shard_map/all_to_all | solution.py:219
  44.3 0.3 fusion.1
  44.5 4.1 %collective-permute-start.1 = (bf16[256,128]{1,0:T(8,128)(2,1)S(1)}, bf16[256,128]{1,0:T(8,128)(2,1)S(1)}, u32[]{:S(2)}, u32[]{:S(2)}) collective-permute-start(bf16[256,128]{1,0:T(8,128)(2,1)S(1)} %get-tuple-element.42), channel_id=1, source_target_pairs={{96,0},{192,96},{288,192},{384,288},{480,384},{576,480},{672,576},... | collective-permute-start | bytes 196616 | tf_op jit(solution)/shard_map/ppermute | solution.py:221
  48.6 4.5 %collective-permute-done.1 = bf16[256,128]{1,0:T(8,128)(2,1)S(1)} collective-permute-done((bf16[256,128]{1,0:T(8,128)(2,1)S(1)}, bf16[256,128]{1,0:T(8,128)(2,1)S(1)}, u32[]{:S(2)}, u32[]{:S(2)}) %collective-permute-start.1) | collective-permute-done | bytes 65568 | tf_op jit(solution)/shard_map/ppermute | solution.py:221
  53.2 37.4 %all_to_all.56 = bf16[4,256,128]{2,1,0:T(8,128)(2,1)S(1)} all-to-all(bf16[4,256,128]{2,1,0:T(8,128)(2,1)S(1)} %broadcast_in_dim.180), channel_id=1, replica_groups={{0,194,388,582},{97,291,485,679},{96,290,484,678},{193,387,581,7},{192,..., dimensions={0} | all-to-all | bytes 524288 | tf_op jit(solution)/shard_map/all_to_all | solution.py:223
  90.6 2.7 collective-permute-start.2
  93.3 3.5 %collective-permute-done.2 = bf16[256,128]{1,0:T(8,128)(2,1)S(1)} collective-permute-done((bf16[256,128]{1,0:T(8,128)(2,1)S(1)}, bf16[256,128]{1,0:T(8,128)(2,1)S(1)}, u32[]{:S(2)}, u32[]{:S(2)}) %collective-permute-start.2) | collective-permute-done | bytes 65568 | tf_op jit(solution)/shard_map/ppermute | solution.py:229
  96.9 14.5 %all_to_all.57.near_ref = bf16[12,256,128]{2,1,0:T(8,128)(2,1)S(1)} all-to-all(bf16[12,256,128]{2,1,0:T(8,128)(2,1)S(1)} %broadcast_select_fusion.1), channel_id=1, replica_groups=mesh['y'=8,'q'=12,'zh'=4,'c'=2] {'q'}, dimensions={0} | all-to-all | bytes 1572864 | tf_op jit(solution)/shard_map/all_to_all | solution.py:231
  111.4 9.4 %collective-permute-start.3 = (bf16[12,256,128]{2,1,0:T(8,128)(2,1)S(1)}, bf16[12,256,128]{2,1,0:T(8,128)(2,1)S(1)}, u32[]{:S(2)}, u32[]{:S(2)}) collective-permute-start(bf16[12,256,128]{2,1,0:T(8,128)(2,1)S(1)} %all_to_all.57.near_ref), channel_id=1, source_target_pairs={{0,97},{97,0},{2,99},{99,2},{4,101},{101,4},{6,103},{103,6},{96,19... | collective-permute-start | bytes 2359304 | tf_op jit(solution)/shard_map/ppermute | solution.py:232
  120.8 9.7 %collective-permute-done.3.far_ref = bf16[12,256,128]{2,1,0:T(8,128)(2,1)S(1)} collective-permute-done((bf16[12,256,128]{2,1,0:T(8,128)(2,1)S(1)}, bf16[12,256,128]{2,1,0:T(8,128)(2,1)S(1)}, u32[]{:S(2)}, u32[]{:S(2)}) %collective-permute-start.3) | collective-permute-done | bytes 786464 | tf_op jit(solution)/shard_map/ppermute | solution.py:232
  130.5 1.6 shard_map.103
  132.1 2.3 collective-permute-start.4
  134.4 0.9 collective-permute-done.4
  135.3 0.7 broadcast_in_dim.183
  136.0 3.4 %all-to-all-start.3 = ((bf16[4,256,128]{2,1,0:T(8,128)(2,1)}), bf16[4,256,128]{2,1,0:T(8,128)(2,1)S(1)}, u32[]{:S(2)}, u32[]{:S(2)}) async-start(bf16[4,256,128]{2,1,0:T(8,128)(2,1)} %broadcast_in_dim.183), calls=%async_computation.3 | async-start | bytes 524288 | tf_op jit(solution)/shard_map/all_to_all | solution.py:261
  139.4 11.6 %all-to-all-done.3 = bf16[4,256,128]{2,1,0:T(8,128)(2,1)S(1)} async-done(((bf16[4,256,128]{2,1,0:T(8,128)(2,1)}), bf16[4,256,128]{2,1,0:T(8,128)(2,1)S(1)}, u32[]{:S(2)}, u32[]{:S(2)}) %all-to-all-start.3) | async-done | bytes 262176 | tf_op jit(solution)/shard_map/all_to_all | solution.py:261
  151.2 0.2 fusion.19
  151.4 0.9 select_reduce_fusion
  152.4 7.9 %collective-permute-start.5 = (bf16[2,256,128]{2,1,0:T(8,128)(2,1)S(1)}, bf16[2,256,128]{2,1,0:T(8,128)(2,1)S(1)}, u32[]{:S(2)}, u32[]{:S(2)}) collective-permute-start(bf16[2,256,128]{2,1,0:T(8,128)(2,1)S(1)} %pad_maximum_fusion.3), channel_id=1, source_target_pairs={{0,1},{1,0},{2,3},{3,2},{4,5},{5,4},{6,7},{7,6},{8,9},{9,8},{10,11... | collective-permute-start | bytes 393224 | tf_op jit(solution)/shard_map/ppermute | solution.py:274
  160.3 1.0 collective-permute-done.5
  161.4 0.7 slice_bitcast_fusion
  162.0 1.6 shard_map.104
  163.7 4.8 %collective-permute-start.6 = (bf16[12,256,128]{2,1,0:T(8,128)(2,1)S(1)}, bf16[12,256,128]{2,1,0:T(8,128)(2,1)S(1)}, u32[]{:S(2)}, u32[]{:S(2)}) collective-permute-start(bf16[12,256,128]{2,1,0:T(8,128)(2,1)S(1)} %get-tuple-element.36), channel_id=1, source_target_pairs={{0,97},{97,0},{2,99},{99,2},{4,101},{101,4},{6,103},{103,6},{96,19... | collective-permute-start | bytes 2359304 | tf_op jit(solution)/shard_map/ppermute | solution.py:218
  168.5 9.7 %collective-permute-done.6 = bf16[12,256,128]{2,1,0:T(8,128)(2,1)S(1)} collective-permute-done((bf16[12,256,128]{2,1,0:T(8,128)(2,1)S(1)}, bf16[12,256,128]{2,1,0:T(8,128)(2,1)S(1)}, u32[]{:S(2)}, u32[]{:S(2)}) %collective-permute-start.6) | collective-permute-done | bytes 786464 | tf_op jit(solution)/shard_map/ppermute | solution.py:218
  178.2 0.2 add_convert_fusion
  178.4 16.8 %all_to_all.58 = bf16[12,256,128]{2,1,0:T(8,128)(2,1)S(1)} all-to-all(bf16[12,256,128]{2,1,0:T(8,128)(2,1)S(1)} %add_convert_fusion), channel_id=1, replica_groups=mesh['y'=8,'q'=12,'zh'=4,'c'=2] {'q'}, dimensions={0} | all-to-all | bytes 1572864 | tf_op jit(solution)/shard_map/all_to_all | solution.py:219
  195.2 0.3 fusion.3
  195.5 1.9 collective-permute-start.7
  197.4 3.1 collective-permute-done.7
  200.6 25.9 %all_to_all.59 = bf16[4,256,128]{2,1,0:T(8,128)(2,1)S(1)} all-to-all(bf16[4,256,128]{2,1,0:T(8,128)(2,1)S(1)} %broadcast_in_dim.186), channel_id=1, replica_groups={{0,194,388,582},{97,291,485,679},{96,290,484,678},{193,387,581,7},{192,..., dimensions={0} | all-to-all | bytes 524288 | tf_op jit(solution)/shard_map/all_to_all | solution.py:223
  226.5 1.9 collective-permute-start.8
  228.5 4.3 %collective-permute-done.8 = bf16[256,128]{1,0:T(8,128)(2,1)S(1)} collective-permute-done((bf16[256,128]{1,0:T(8,128)(2,1)S(1)}, bf16[256,128]{1,0:T(8,128)(2,1)S(1)}, u32[]{:S(2)}, u32[]{:S(2)}) %collective-permute-start.8) | collective-permute-done | bytes 65568 | tf_op jit(solution)/shard_map/ppermute | solution.py:229
  232.8 14.6 %all_to_all.60.near_ref = bf16[12,256,128]{2,1,0:T(8,128)(2,1)} all-to-all(bf16[12,256,128]{2,1,0:T(8,128)(2,1)S(1)} %broadcast_select_fusion), channel_id=1, replica_groups=mesh['y'=8,'q'=12,'zh'=4,'c'=2] {'q'}, dimensions={0} | all-to-all | bytes 1572864 | tf_op jit(solution)/shard_map/all_to_all | solution.py:231
  247.4 7.5 %collective-permute-start.9 = (bf16[12,256,128]{2,1,0:T(8,128)(2,1)}, bf16[12,256,128]{2,1,0:T(8,128)(2,1)}, u32[]{:S(2)}, u32[]{:S(2)}) collective-permute-start(bf16[12,256,128]{2,1,0:T(8,128)(2,1)} %all_to_all.60.near_ref), channel_id=1, source_target_pairs={{0,97},{97,0},{2,99},{99,2},{4,101},{101,4},{6,103},{103,6},{96,19... | collective-permute-start | bytes 2359304 | tf_op jit(solution)/shard_map/ppermute | solution.py:232
  254.9 0.7 copy.27
  255.7 0.7 copy.28
  256.4 0.7 copy.29
  257.1 7.8 %collective-permute-done.9.far_ref = bf16[12,256,128]{2,1,0:T(8,128)(2,1)} collective-permute-done((bf16[12,256,128]{2,1,0:T(8,128)(2,1)}, bf16[12,256,128]{2,1,0:T(8,128)(2,1)}, u32[]{:S(2)}, u32[]{:S(2)}) %collective-permute-start.9) | collective-permute-done | bytes 786464 | tf_op jit(solution)/shard_map/ppermute | solution.py:232
  264.9 2.5 shard_map.105
  267.4 1.8 convolution_bitcast_fusion
  269.2 0.2 convolution_convert_fusion.1
  269.4 0.6 fusion.6
  270.1 4.2 %collective-permute-start.10 = (bf16[1280,128]{0,1:T(8,128)(2,1)S(1)}, bf16[1280,128]{0,1:T(8,128)(2,1)S(1)}, u32[]{:S(2)}, u32[]{:S(2)}) collective-permute-start(bf16[1280,128]{0,1:T(8,128)(2,1)S(1)} %pad_maximum_fusion.1), channel_id=1, source_target_pairs={{0,1},{1,0},{2,3},{3,2},{4,5},{5,4},{6,7},{7,6},{8,9},{9,8},{10,11... | collective-permute-start | bytes 983048 | tf_op jit(solution)/shard_map/ppermute | solution.py:306
  274.4 0.2 fusion.14
  274.6 0.9 collective-permute-done.10
  275.8 0.2 copy.30
  276.1 10.7 %all_to_all.61 = bf16[12,112,128]{2,1,0:T(8,128)(2,1)S(1)} all-to-all(bf16[12,112,128]{2,1,0:T(8,128)(2,1)S(1)} %bitcast.50), channel_id=1, replica_groups=mesh['y'=8,'q'=12,'zh'=4,'c'=2] {'q'}, dimensions={0} | all-to-all | bytes 688128 | tf_op jit(solution)/shard_map/all_to_all | solution.py:311
  286.9 14.8 %all_to_all.62 = bf16[4,112,128]{2,1,0:T(8,128)(2,1)S(1)} all-to-all(bf16[4,112,128]{2,1,0:T(8,128)(2,1)S(1)} %broadcast_in_dim.194), channel_id=1, replica_groups=mesh['y'=8,'q'=12,'zh'=4,'c'=2] {'zh'}, dimensions={0} | all-to-all | bytes 229376 | tf_op jit(solution)/shard_map/all_to_all | solution.py:312
  301.8 11.4 %all_to_all.63 = bf16[8,112,128]{2,1,0:T(8,128)(2,1)S(1)} all-to-all(bf16[8,112,128]{2,1,0:T(8,128)(2,1)S(1)} %broadcast_in_dim.198), channel_id=1, replica_groups=mesh['y'=8,'q'=12,'zh'=4,'c'=2] {'y'}, dimensions={0} | all-to-all | bytes 458752 | tf_op jit(solution)/shard_map/all_to_all | solution.py:313
  313.3 13.5 %all_to_all.64 = bf16[12,112,128]{2,1,0:T(8,128)(2,1)S(1)} all-to-all(bf16[12,112,128]{2,1,0:T(8,128)(2,1)S(1)} %broadcast_in_dim.202), channel_id=1, replica_groups=mesh['y'=8,'q'=12,'zh'=4,'c'=2] {'q'}, dimensions={0} | all-to-all | bytes 688128 | tf_op jit(solution)/shard_map/all_to_all | solution.py:314
  326.9 6.4 %collective-permute-start.11 = (bf16[1344,128]{1,0:T(8,128)(2,1)S(1)}, bf16[1344,128]{1,0:T(8,128)(2,1)S(1)}, u32[]{:S(2)}, u32[]{:S(2)}) collective-permute-start(bf16[1344,128]{1,0:T(8,128)(2,1)S(1)} %bitcast.51), channel_id=1, source_target_pairs={{0,1},{1,0},{2,3},{3,2},{4,5},{5,4},{6,7},{7,6},{8,9},{9,8},{10,11... | collective-permute-start | bytes 1032200 | tf_op jit(solution)/shard_map/ppermute | solution.py:315
  333.3 1.3 collective-permute-done.11
  334.8 0.6 fusion.25
  335.4 0.7 pad_maximum_fusion.2
  336.7 1.0 pad_maximum_fusion
  (73 shorter events, 1.6 us)
Async XLA Ops:
  2.1 94.7 %copy-start.12 = (pred[12,1,128]{2,0,1:T(8,128)(4,1)}, pred[12,1,128]{2,0,1:T(8,128)(4,1)S(1)}, u32[]{:S(2)}) copy-start(pred[12,1,128]{2,0,1:T(8,128)(4,1)S(1)} %iota.17) | copy-start | bytes 4612
  2.9 0.7 copy-start.2
  3.5 0.7 copy-start.4
  8.2 0.8 copy-start
  9.0 16.1 %collective-permute-start = (bf16[12,256,128]{2,1,0:T(8,128)(2,1)S(1)}, bf16[12,256,128]{2,1,0:T(8,128)(2,1)S(1)}, u32[]{:S(2)}, u32[]{:S(2)}) collective-permute-start(bf16[12,256,128]{2,1,0:T(8,128)(2,1)S(1)} %get-tuple-element.27), channel_id=1, source_target_pairs={{0,97},{97,0},{2,99},{99,2},{4,101},{101,4},{6,103},{103,6},{96,19... | collective-permute-start | bytes 2359304 | tf_op jit(solution)/shard_map/ppermute | solution.py:218
  44.5 8.5 %collective-permute-start.1 = (bf16[256,128]{1,0:T(8,128)(2,1)S(1)}, bf16[256,128]{1,0:T(8,128)(2,1)S(1)}, u32[]{:S(2)}, u32[]{:S(2)}) collective-permute-start(bf16[256,128]{1,0:T(8,128)(2,1)S(1)} %get-tuple-element.42), channel_id=1, source_target_pairs={{96,0},{192,96},{288,192},{384,288},{480,384},{576,480},{672,576},... | collective-permute-start | bytes 196616 | tf_op jit(solution)/shard_map/ppermute | solution.py:221
  90.5 39.9 %copy-start.3 = (s32[1,1,12,2]{2,3,1,0:T(2,128)S(1)}, s32[1,1,12,2]{2,3,1,0:T(2,128)}, u32[]{:S(2)}) copy-start(s32[1,1,12,2]{2,3,1,0:T(2,128)} %param.11) | copy-start | bytes 292
  90.5 39.9 %copy-start.5 = (s32[1,1,12,2]{2,3,1,0:T(2,128)S(1)}, s32[1,1,12,2]{2,3,1,0:T(2,128)}, u32[]{:S(2)}) copy-start(s32[1,1,12,2]{2,3,1,0:T(2,128)} %param.12) | copy-start | bytes 292
  90.6 6.2 %collective-permute-start.2 = (bf16[256,128]{1,0:T(8,128)(2,1)S(1)}, bf16[256,128]{1,0:T(8,128)(2,1)S(1)}, u32[]{:S(2)}, u32[]{:S(2)}) collective-permute-start(bf16[256,128]{1,0:T(8,128)(2,1)S(1)} %multiply_convert_fusion.2), channel_id=1, source_target_pairs={{0,96},{96,192},{192,288},{288,384},{384,480},{480,576},{576,672},... | collective-permute-start | bytes 196616 | tf_op jit(solution)/shard_map/ppermute | solution.py:229
  111.4 19.1 %collective-permute-start.3 = (bf16[12,256,128]{2,1,0:T(8,128)(2,1)S(1)}, bf16[12,256,128]{2,1,0:T(8,128)(2,1)S(1)}, u32[]{:S(2)}, u32[]{:S(2)}) collective-permute-start(bf16[12,256,128]{2,1,0:T(8,128)(2,1)S(1)} %all_to_all.57.near_ref), channel_id=1, source_target_pairs={{0,97},{97,0},{2,99},{99,2},{4,101},{101,4},{6,103},{103,6},{96,19... | collective-permute-start | bytes 2359304 | tf_op jit(solution)/shard_map/ppermute | solution.py:232
  132.1 3.1 collective-permute-start.4
  136.0 15.0 %all-to-all-start.3 = ((bf16[4,256,128]{2,1,0:T(8,128)(2,1)}), bf16[4,256,128]{2,1,0:T(8,128)(2,1)S(1)}, u32[]{:S(2)}, u32[]{:S(2)}) async-start(bf16[4,256,128]{2,1,0:T(8,128)(2,1)} %broadcast_in_dim.183), calls=%async_computation.3 | async-start | bytes 524288 | tf_op jit(solution)/shard_map/all_to_all | solution.py:261
  152.4 8.9 %collective-permute-start.5 = (bf16[2,256,128]{2,1,0:T(8,128)(2,1)S(1)}, bf16[2,256,128]{2,1,0:T(8,128)(2,1)S(1)}, u32[]{:S(2)}, u32[]{:S(2)}) collective-permute-start(bf16[2,256,128]{2,1,0:T(8,128)(2,1)S(1)} %pad_maximum_fusion.3), channel_id=1, source_target_pairs={{0,1},{1,0},{2,3},{3,2},{4,5},{5,4},{6,7},{7,6},{8,9},{9,8},{10,11... | collective-permute-start | bytes 393224 | tf_op jit(solution)/shard_map/ppermute | solution.py:274
  163.7 14.5 %collective-permute-start.6 = (bf16[12,256,128]{2,1,0:T(8,128)(2,1)S(1)}, bf16[12,256,128]{2,1,0:T(8,128)(2,1)S(1)}, u32[]{:S(2)}, u32[]{:S(2)}) collective-permute-start(bf16[12,256,128]{2,1,0:T(8,128)(2,1)S(1)} %get-tuple-element.36), channel_id=1, source_target_pairs={{0,97},{97,0},{2,99},{99,2},{4,101},{101,4},{6,103},{103,6},{96,19... | collective-permute-start | bytes 2359304 | tf_op jit(solution)/shard_map/ppermute | solution.py:218
  178.4 16.9 %copy-start.13 = (pred[12,1,128]{2,0,1:T(8,128)(4,1)S(1)}, pred[12,1,128]{2,0,1:T(8,128)(4,1)}, u32[]{:S(2)}) copy-start(pred[12,1,128]{2,0,1:T(8,128)(4,1)} %copy-done.12) | copy-start | bytes 4612
  195.5 5.0 %collective-permute-start.7 = (bf16[256,128]{1,0:T(8,128)(2,1)S(1)}, bf16[256,128]{1,0:T(8,128)(2,1)S(1)}, u32[]{:S(2)}, u32[]{:S(2)}) collective-permute-start(bf16[256,128]{1,0:T(8,128)(2,1)S(1)} %get-tuple-element.40), channel_id=1, source_target_pairs={{96,0},{192,96},{288,192},{384,288},{480,384},{576,480},{672,576},... | collective-permute-start | bytes 196616 | tf_op jit(solution)/shard_map/ppermute | solution.py:221
  226.5 6.2 %collective-permute-start.8 = (bf16[256,128]{1,0:T(8,128)(2,1)S(1)}, bf16[256,128]{1,0:T(8,128)(2,1)S(1)}, u32[]{:S(2)}, u32[]{:S(2)}) collective-permute-start(bf16[256,128]{1,0:T(8,128)(2,1)S(1)} %multiply_convert_fusion), channel_id=1, source_target_pairs={{0,96},{96,192},{192,288},{288,384},{384,480},{480,576},{576,672},... | collective-permute-start | bytes 196616 | tf_op jit(solution)/shard_map/ppermute | solution.py:229
  247.4 17.5 %collective-permute-start.9 = (bf16[12,256,128]{2,1,0:T(8,128)(2,1)}, bf16[12,256,128]{2,1,0:T(8,128)(2,1)}, u32[]{:S(2)}, u32[]{:S(2)}) collective-permute-start(bf16[12,256,128]{2,1,0:T(8,128)(2,1)} %all_to_all.60.near_ref), channel_id=1, source_target_pairs={{0,97},{97,0},{2,99},{99,2},{4,101},{101,4},{6,103},{103,6},{96,19... | collective-permute-start | bytes 2359304 | tf_op jit(solution)/shard_map/ppermute | solution.py:232
  257.1 10.3 %copy-start.7 = (bf16[512,128]{1,0:T(8,128)(2,1)S(1)}, bf16[512,128]{1,0:T(8,128)(2,1)}, u32[]{:S(2)}) copy-start(bf16[512,128]{1,0:T(8,128)(2,1)} %far_second_ref.1) | copy-start | bytes 393220
  267.3 1.8 copy-start.1
  267.4 2.1 copy-start.6
  270.1 5.6 %copy-start.9 = (bf16[1,128]{0,1:T(8,128)(2,1)S(1)}, bf16[1,128]{0,1:T(8,128)(2,1)}, u32[]{:S(2)}) copy-start(bf16[1,128]{0,1:T(8,128)(2,1)} %copy.27) | copy-start | bytes 772
  270.1 5.6 %copy-start.10 = (bf16[1,128]{0,1:T(8,128)(2,1)S(1)}, bf16[1,128]{0,1:T(8,128)(2,1)}, u32[]{:S(2)}) copy-start(bf16[1,128]{0,1:T(8,128)(2,1)} %copy.28) | copy-start | bytes 772
  270.1 5.6 %copy-start.11 = (bf16[1,128]{0,1:T(8,128)(2,1)S(1)}, bf16[1,128]{0,1:T(8,128)(2,1)}, u32[]{:S(2)}) copy-start(bf16[1,128]{0,1:T(8,128)(2,1)} %copy.29) | copy-start | bytes 772
  270.1 5.5 %collective-permute-start.10 = (bf16[1280,128]{0,1:T(8,128)(2,1)S(1)}, bf16[1280,128]{0,1:T(8,128)(2,1)S(1)}, u32[]{:S(2)}, u32[]{:S(2)}) collective-permute-start(bf16[1280,128]{0,1:T(8,128)(2,1)S(1)} %pad_maximum_fusion.1), channel_id=1, source_target_pairs={{0,1},{1,0},{2,3},{3,2},{4,5},{5,4},{6,7},{7,6},{8,9},{9,8},{10,11... | collective-permute-start | bytes 983048 | tf_op jit(solution)/shard_map/ppermute | solution.py:306
  275.7 11.2 %copy-start.8 = (s32[112,128]{1,0:T(8,128)S(1)}, s32[112,128]{1,0:T(8,128)}, u32[]{:S(2)}) copy-start(s32[112,128]{1,0:T(8,128)} %iota.19) | copy-start | bytes 172036
  326.9 7.6 %collective-permute-start.11 = (bf16[1344,128]{1,0:T(8,128)(2,1)S(1)}, bf16[1344,128]{1,0:T(8,128)(2,1)S(1)}, u32[]{:S(2)}, u32[]{:S(2)}) collective-permute-start(bf16[1344,128]{1,0:T(8,128)(2,1)S(1)} %bitcast.51), channel_id=1, source_target_pairs={{0,1},{1,0},{2,3},{3,2},{4,5},{5,4},{6,7},{7,6},{8,9},{9,8},{10,11... | collective-permute-start | bytes 1032200 | tf_op jit(solution)/shard_map/ppermute | solution.py:315

commit v6 on v5

--- a/solution.py
+++ b/solution.py
@@ -50,8 +50,8 @@
 
 def first_kernel(
     place_ref,
-    rows_ref,
-    cols_ref,
+    far_rows_ref,
+    far_cols_ref,
     far_tiles_ref,
     far_features_ref,
     far_first_ref,
@@ -59,11 +59,14 @@
     mine_ref,
     away_ref,
     tiles_ref,
-    hidden_ref,
+    far_hidden_ref,
     base_ref,
     features_ref,
     first_ref,
     second_ref,
+    hidden_ref,
+    rows_ref,
+    cols_ref,
     arrived,
 ):
     copies = [
@@ -74,20 +77,26 @@
                 (far_first_ref, first_ref),
                 (far_second_ref, second_ref),
                 (far_tiles_ref, tiles_ref),
+                (far_rows_ref, rows_ref),
+                (far_cols_ref, cols_ref),
+                (hidden_ref, far_hidden_ref),
             )
         )
     ]
-    for copy in copies:
+    for copy in copies[:6]:
         copy.start()
     copies[0].wait()
     copies[1].wait()
     hidden = jnp.dot(features_ref[...], first_ref[...], preferred_element_type=F32)
     hidden_ref[...] = jnp.maximum(hidden, 0.0).astype(BF)
+    copies[6].start()
     copies[2].wait()
     base = jnp.dot(hidden_ref[...], second_ref[...], preferred_element_type=F32)
     base_ref[...] = base.astype(BF)
-    copies[3].wait()
+    for copy in copies[3:6]:
+        copy.wait()
     scatter_kernel(place_ref, rows_ref, cols_ref, tiles_ref, base_ref, mine_ref, away_ref)
+    copies[6].wait()
 
 
 def add_gathered(place_ref, rows_ref, cols_ref, tiles_ref, near_ref, far_ref, sum_ref):
@@ -129,21 +138,24 @@
     out_ref[...] = ((1.0 - ALPHA) * sum_ref[...]).astype(BF)
 
 
-def call(kernel, outs, scalars, operands, scratch=(), space=pltpu.VMEM, interpret=False):
+def call(kernel, outs, scalars, operands, scratch=(), far=(), far_outs=(), interpret=False):
     vmem = pl.BlockSpec(memory_space=pltpu.VMEM)
     smem = pl.BlockSpec(memory_space=pltpu.SMEM)
-    shapes = [jax.ShapeDtypeStruct(shape, dtype) for shape, dtype in outs]
-    if not interpret:
-        operands = [pltpu.with_memory_space_constraint(v, space) for v in operands]
+    hbm = pl.BlockSpec(memory_space=pltpu.HBM)
+    far = [v if interpret else pltpu.with_memory_space_constraint(v, pltpu.HBM) for v in far]
+    shapes = [
+        pltpu.HBM(shape, dtype) if k in far_outs else jax.ShapeDtypeStruct(shape, dtype)
+        for k, (shape, dtype) in enumerate(outs)
+    ]
     return pl.pallas_call(
         kernel,
         out_shape=shapes,
-        in_specs=[smem] * len(scalars) + [pl.BlockSpec(memory_space=space)] * len(operands),
-        out_specs=[vmem] * len(outs),
+        in_specs=[smem] * len(scalars) + [hbm] * len(far) + [vmem] * len(operands),
+        out_specs=[hbm if k in far_outs else vmem for k in range(len(outs))],
         scratch_shapes=list(scratch),
         compiler_params=pltpu.CompilerParams(vmem_limit_bytes=16 << 20),
         interpret=interpret,
-    )(*scalars, *operands)
+    )(*scalars, *far, *operands)
 
 
 def on_device(interpret, features, labels, w_first, w_second, block_rows, block_cols, block_vals):
@@ -214,16 +226,17 @@
             jnp.concatenate([other, mine], axis=-2),
         )
 
-    def reduced(mine, away):
+    def reduced(mine, away, *ahead):
         parts = (mine + lax.ppermute(away, yrep, pairs).astype(F32)).astype(BF)
         parts = lax.all_to_all(parts, "q", 0, 0, tiled=True).astype(F32)
         before = jnp.sum(jnp.where(from_same, 0.0, parts), axis=0).astype(BF)
         moved = lax.ppermute(before, "y", [((i + 1) % ny, i) for i in range(ny)])
         total = jnp.sum(jnp.where(from_same, parts, 0.0), axis=0) + moved.astype(F32)
+        total, *ahead = lax.optimization_barrier((total.astype(BF), *ahead))
         group = lax.all_to_all(
-            to_all(total.astype(BF), nzh), yrep, 0, 0, axis_index_groups=fours, tiled=True
-        )
-        return ((1.0 - ALPHA) * jnp.sum(group.astype(F32), axis=0)).astype(BF)
+            to_all(total, nzh), yrep, 0, 0, axis_index_groups=fours, tiled=True
+        )
+        return ((1.0 - ALPHA) * jnp.sum(group.astype(F32), axis=0)).astype(BF), *ahead
 
     def gathered(here):
         before = lax.ppermute(here, "y", [(i, (i + 1) % ny) for i in range(ny)])
@@ -233,22 +246,27 @@
 
     slots_here = [((steps, half, classes), F32), ((steps, half, classes), BF)]
     sum_here = pltpu.VMEM((nodes_here, classes), F32)
-    labels_half, plain, diagonal, from_same, loss_row = lax.optimization_barrier(
-        (labels_half, plain, diagonal, from_same, loss_row)
-    )
+    plain, diagonal, from_same = lax.optimization_barrier((plain, diagonal, from_same))
     operands = (tiles, features, w_first, w_second)
+    hidden_shape = (nodes_here, w_first.shape[1])
     mine, away, tiles, hidden, base = call(
         first_kernel,
-        slots_here
-        + [(tiles.shape, BF), ((nodes_here, w_first.shape[1]), BF), ((nodes_here, classes), BF)],
-        [diagonal] + scalars,
-        operands,
-        [pltpu.VMEM(v.shape, BF) for v in operands[1:]] + [pltpu.SemaphoreType.DMA((4,))],
-        pltpu.HBM,
+        slots_here + [(tiles.shape, BF), (hidden_shape, BF), ((nodes_here, classes), BF)],
+        [diagonal],
+        [],
+        [pltpu.VMEM(v.shape, BF) for v in operands[1:]]
+        + [pltpu.VMEM(hidden_shape, BF)]
+        + [pltpu.SMEM(v.shape, jnp.int32) for v in scalars]
+        + [pltpu.SemaphoreType.DMA((7,))],
+        [*scalars, *operands],
+        (3,),
         interpret=interpret,
     )
     base_half = lax.dynamic_slice_in_dim(base, c_id * half, half, 0)
-    near, far = gathered(reduced(mine, away))
+    current, base_half, labels_half, loss_row = reduced(
+        mine, away, base_half, labels_half, loss_row
+    )
+    near, far = gathered(current)
     mine, away = call(
         gather_kernel,
         [((half, classes), F32), ((half, classes), BF)],
@@ -277,7 +295,8 @@
     mine, away = call(
         scatter_kernel, slots_here, [plain] + scalars, [tiles, moving], interpret=interpret
     )
-    near, far = gathered(reduced(mine, away))
+    (current,) = reduced(mine, away)
+    near, far = gathered(current)
     (grad_b,) = call(
         last_kernel,
         [((nodes_here, classes), BF)],
@@ -287,7 +306,7 @@
         interpret=interpret,
     )
 
-    def weight_rows(core):
+    def weight_rows(core, grad_b):
         hidden_part = lax.dynamic_slice_in_dim(hidden, core * part, part, 1)
         second_part = lax.dynamic_slice_in_dim(w_second, core * part, part, 0)
         back = lax.dot_general(
@@ -303,8 +322,9 @@
         bands_here = [first[:, k * classes : (k + 1) * classes] for k in range(bands)]
         return jnp.concatenate(bands_here + [second])
 
-    away = lax.ppermute(weight_rows(1 - c_id).astype(BF), "c", cores)
-    sums = (weight_rows(c_id) + away.astype(F32)).astype(BF)
+    away, grad_b = lax.optimization_barrier((weight_rows(1 - c_id, grad_b).astype(BF), grad_b))
+    away = lax.ppermute(away, "c", cores)
+    sums = (weight_rows(c_id, grad_b) + away.astype(F32)).astype(BF)
     sums = jnp.concatenate(
         [sums, *ce_terms, jnp.zeros((each * nq - used - 3, classes), BF)]
     ).reshape(nq, each, classes)

time: 340 us -> 340 us (level)
  blocking collectives: 178 us -> 162 us
  waiting for transfers between devices: 67.8 us -> 80.8 us
  starting transfers between devices: 63 us -> 68.5 us
    all_to_all x2 -> x1, blocking collectives: 35.7 us -> 16.8 us  [reduced(): parts = lax.all_to_all(parts, 'q', 0, 0, tiled=True).astype(F32)]
    all_to_all x0 -> x1, waiting for transfers between devices: none -> 9.27 us  [reduced(): parts = lax.all_to_all(parts, 'q', 0, 0, tiled=True).astype(F32)]
    all_to_all x0 -> x1, starting transfers between devices: none -> 7.82 us  [reduced(): parts = lax.all_to_all(parts, 'q', 0, 0, tiled=True).astype(F32)]
    all_to_all x2, blocking collectives: 29.1 us -> 33.4 us  [gathered(): near = lax.all_to_all(near, 'q', 0, 0, tiled=True)]
    all_to_all x2, blocking collectives: 63.3 us -> 59.7 us  [reduced(): lax.all_to_all(to_all(total, nzh), yrep, 0, 0, axis_index_groups=fours, t...]
  transfers between devices with their start and end apart: 13 -> 14, of which waited for: 13 -> 14; matrix products, arithmetic and copies ran while one was open for 1% -> 1% of each run, Pallas kernels for 0% -> 0%
where the time goes in v6:
time: 340 us; the launch traced here: 339 us
  blocking collectives  162 us (48%)
  waiting for transfers between devices  80.8 us (24%)
  starting transfers between devices  68.5 us (20%)
  Pallas kernels  9.66 us (3%)
  other arithmetic  7.76 us (2%)
  local copies, waits for them, and re-layouts  5.17 us (2%)
    all_to_all x2, blocking collectives, reduced(): lax.all_to_all(to_all(total, nzh), yrep, 0, 0, axis_index_groups=fours, t...  59.7 us
    all_to_all x2, blocking collectives, gathered(): near = lax.all_to_all(near, 'q', 0, 0, tiled=True)  33.4 us
    ppermute x2, waiting for transfers between devices, reduced(): parts = (mine + lax.ppermute(away, yrep, pairs).astype(F32)).astype(BF)  21.2 us
    ppermute x2, waiting for transfers between devices, gathered(): return (near, lax.ppermute(near, yrep, pairs))  17.4 us
    all_to_all x1, blocking collectives, reduced(): parts = lax.all_to_all(parts, 'q', 0, 0, tiled=True).astype(F32)  16.8 us
    ppermute x2, starting transfers between devices, gathered(): return (near, lax.ppermute(near, yrep, pairs))  15.6 us
    all_to_all x1, blocking collectives, on_device(): sums = summed(lax.all_to_all(to_all(sums, nzh), 'zh', 0, 0, tiled=True))  15.1 us
    all_to_all x1, blocking collectives, on_device(): lax.all_to_all(to_all(sums, nq), 'q', 0, 0, tiled=True)  13.5 us
  transfers between devices with their start and end apart: 14, of which 14 were waited for; matrix products, arithmetic and copies ran while one was open for 1% of the time, Pallas kernels for 0%

profile of v6, /device:TPU:1, one launch (start us, length us, event | category | flops | bytes accessed | tf_op | source)
XLA Modules:
  0.0 339.3 jit_solution(7980852486000063701)
XLA Ops:
  0.8 4.1 %shard_map.102 = (f32[12,256,128]{2,1,0:T(8,128)S(1)}, bf16[12,256,128]{2,1,0:T(8,128)(2,1)S(1)}, bf16[12,2,256,256]{3,2,1,0:T(8,128)(2,1)S(1)}, bf16[512,512]{1,0:T(8,128)(2,1)}, bf16[512,128]{1,0:T(8,128)(2,1)S(1)}) custom-call(s32[3]{0:T(128)S(1)} %get-tuple-element.27.place_ref, s32[2,12]{1,0:T(2,128)} %bitcast.41, s32[2,12]{1,0:T(2,128)} %bitcast.45, ...), custom_call_target="tpu_custom_call" | custom-call | tf_op jit(solution)/shard_map/pallas_call | solution.py:150
  4.9 6.5 %collective-permute-start = (bf16[12,256,128]{2,1,0:T(8,128)(2,1)S(1)}, bf16[12,256,128]{2,1,0:T(8,128)(2,1)S(1)}, u32[]{:S(2)}, u32[]{:S(2)}) collective-permute-start(bf16[12,256,128]{2,1,0:T(8,128)(2,1)S(1)} %get-tuple-element.31), channel_id=1, source_target_pairs={{0,97},{97,0},{2,99},{99,2},{4,101},{101,4},{6,103},{103,6},{96,19... | collective-permute-start | bytes 2359304 | tf_op jit(solution)/shard_map/ppermute | solution.py:230
  11.4 9.7 %collective-permute-done = bf16[12,256,128]{2,1,0:T(8,128)(2,1)S(1)} collective-permute-done((bf16[12,256,128]{2,1,0:T(8,128)(2,1)S(1)}, bf16[12,256,128]{2,1,0:T(8,128)(2,1)S(1)}, u32[]{:S(2)}, u32[]{:S(2)}) %collective-permute-start) | collective-permute-done | bytes 786464 | tf_op jit(solution)/shard_map/ppermute | solution.py:230
  21.0 1.1 add_convert_fusion.1
  22.1 7.8 %all-to-all-start = ((bf16[12,256,128]{2,1,0:T(8,128)(2,1)}), bf16[12,256,128]{2,1,0:T(8,128)(2,1)}, u32[]{:S(2)}, u32[]{:S(2)}) async-start(bf16[12,256,128]{2,1,0:T(8,128)(2,1)} %add_convert_fusion.1), calls=%async_computation | async-start | bytes 1572864 | tf_op jit(solution)/shard_map/all_to_all | solution.py:231
  30.1 9.3 %all-to-all-done = bf16[12,256,128]{2,1,0:T(8,128)(2,1)} async-done(((bf16[12,256,128]{2,1,0:T(8,128)(2,1)}), bf16[12,256,128]{2,1,0:T(8,128)(2,1)}, u32[]{:S(2)}, u32[]{:S(2)}) %all-to-all-start) | async-done | bytes 786464 | tf_op jit(solution)/shard_map/all_to_all | solution.py:231
  39.3 1.4 fusion.1
  40.7 4.0 %collective-permute-start.1 = (bf16[256,128]{1,0:T(8,128)(2,1)S(1)}, bf16[256,128]{1,0:T(8,128)(2,1)S(1)}, u32[]{:S(2)}, u32[]{:S(2)}) collective-permute-start(bf16[256,128]{1,0:T(8,128)(2,1)S(1)} %get-tuple-element.50), channel_id=1, source_target_pairs={{96,0},{192,96},{288,192},{384,288},{480,384},{576,480},{672,576},... | collective-permute-start | bytes 196616 | tf_op jit(solution)/shard_map/ppermute | solution.py:233
  44.7 5.5 %collective-permute-done.1 = bf16[256,128]{1,0:T(8,128)(2,1)S(1)} collective-permute-done((bf16[256,128]{1,0:T(8,128)(2,1)S(1)}, bf16[256,128]{1,0:T(8,128)(2,1)S(1)}, u32[]{:S(2)}, u32[]{:S(2)}) %collective-permute-start.1) | collective-permute-done | bytes 65568 | tf_op jit(solution)/shard_map/ppermute | solution.py:233
  50.3 0.7 iota.19
  51.0 37.4 %all_to_all.55 = bf16[4,256,128]{2,1,0:T(8,128)(2,1)S(1)} all-to-all(bf16[4,256,128]{2,1,0:T(8,128)(2,1)S(1)} %broadcast_in_dim.180), channel_id=1, replica_groups={{0,194,388,582},{97,291,485,679},{96,290,484,678},{193,387,581,7},{192,..., dimensions={0} | all-to-all | bytes 524288 | tf_op jit(solution)/shard_map/all_to_all | solution.py:236
  88.5 1.9 collective-permute-start.2
  90.4 4.3 %collective-permute-done.2 = bf16[256,128]{1,0:T(8,128)(2,1)S(1)} collective-permute-done((bf16[256,128]{1,0:T(8,128)(2,1)S(1)}, bf16[256,128]{1,0:T(8,128)(2,1)S(1)}, u32[]{:S(2)}, u32[]{:S(2)}) %collective-permute-start.2) | collective-permute-done | bytes 65568 | tf_op jit(solution)/shard_map/ppermute | solution.py:242
  94.8 15.2 %all_to_all.56.near_ref = bf16[12,256,128]{2,1,0:T(8,128)(2,1)S(1)} all-to-all(bf16[12,256,128]{2,1,0:T(8,128)(2,1)S(1)} %broadcast_select_fusion.1), channel_id=1, replica_groups=mesh['y'=8,'q'=12,'zh'=4,'c'=2] {'q'}, dimensions={0} | all-to-all | bytes 1572864 | tf_op jit(solution)/shard_map/all_to_all | solution.py:244
  110.0 7.7 %collective-permute-start.3 = (bf16[12,256,128]{2,1,0:T(8,128)(2,1)S(1)}, bf16[12,256,128]{2,1,0:T(8,128)(2,1)S(1)}, u32[]{:S(2)}, u32[]{:S(2)}) collective-permute-start(bf16[12,256,128]{2,1,0:T(8,128)(2,1)S(1)} %all_to_all.56.near_ref), channel_id=1, source_target_pairs={{0,97},{97,0},{2,99},{99,2},{4,101},{101,4},{6,103},{103,6},{96,19... | collective-permute-start | bytes 2359304 | tf_op jit(solution)/shard_map/ppermute | solution.py:245
  117.7 9.7 %collective-permute-done.3.far_ref = bf16[12,256,128]{2,1,0:T(8,128)(2,1)S(1)} collective-permute-done((bf16[12,256,128]{2,1,0:T(8,128)(2,1)S(1)}, bf16[12,256,128]{2,1,0:T(8,128)(2,1)S(1)}, u32[]{:S(2)}, u32[]{:S(2)}) %collective-permute-start.3) | collective-permute-done | bytes 786464 | tf_op jit(solution)/shard_map/ppermute | solution.py:245
  127.4 1.6 shard_map.103
  128.9 4.1 %collective-permute-start.4 = (bf16[256,128]{1,0:T(8,128)(2,1)S(1)}, bf16[256,128]{1,0:T(8,128)(2,1)S(1)}, u32[]{:S(2)}, u32[]{:S(2)}) collective-permute-start(bf16[256,128]{1,0:T(8,128)(2,1)S(1)} %get-tuple-element.35), channel_id=1, source_target_pairs={{0,1},{1,0},{2,3},{3,2},{4,5},{5,4},{6,7},{7,6},{8,9},{9,8},{10,11... | collective-permute-start | bytes 196616 | tf_op jit(solution)/shard_map/ppermute | solution.py:278
  133.0 0.9 collective-permute-done.4
  133.9 0.7 broadcast_in_dim.183
  134.7 4.0 %all-to-all-start.3 = ((bf16[4,256,128]{2,1,0:T(8,128)(2,1)}), bf16[4,256,128]{2,1,0:T(8,128)(2,1)}, u32[]{:S(2)}, u32[]{:S(2)}) async-start(bf16[4,256,128]{2,1,0:T(8,128)(2,1)} %broadcast_in_dim.183), calls=%async_computation.3 | async-start | bytes 524288 | tf_op jit(solution)/shard_map/all_to_all | solution.py:279
  138.7 11.6 %all-to-all-done.3 = bf16[4,256,128]{2,1,0:T(8,128)(2,1)} async-done(((bf16[4,256,128]{2,1,0:T(8,128)(2,1)}), bf16[4,256,128]{2,1,0:T(8,128)(2,1)}, u32[]{:S(2)}, u32[]{:S(2)}) %all-to-all-start.3) | async-done | bytes 262176 | tf_op jit(solution)/shard_map/all_to_all | solution.py:279
  150.4 1.0 convert_reduce_fusion.2
  151.5 0.2 fusion.19
  151.7 0.2 select_reduce_fusion
  152.0 8.0 %collective-permute-start.5 = (bf16[2,256,128]{2,1,0:T(8,128)(2,1)S(1)}, bf16[2,256,128]{2,1,0:T(8,128)(2,1)S(1)}, u32[]{:S(2)}, u32[]{:S(2)}) collective-permute-start(bf16[2,256,128]{2,1,0:T(8,128)(2,1)S(1)} %pad_maximum_fusion.3), channel_id=1, source_target_pairs={{0,1},{1,0},{2,3},{3,2},{4,5},{5,4},{6,7},{7,6},{8,9},{9,8},{10,11... | collective-permute-start | bytes 393224 | tf_op jit(solution)/shard_map/ppermute | solution.py:292
  159.9 1.0 collective-permute-done.5
  161.0 0.7 slice_bitcast_fusion
  161.7 1.6 shard_map.104
  163.3 3.0 collective-permute-start.6
  166.3 11.5 %collective-permute-done.6 = bf16[12,256,128]{2,1,0:T(8,128)(2,1)S(1)} collective-permute-done((bf16[12,256,128]{2,1,0:T(8,128)(2,1)S(1)}, bf16[12,256,128]{2,1,0:T(8,128)(2,1)S(1)}, u32[]{:S(2)}, u32[]{:S(2)}) %collective-permute-start.6) | collective-permute-done | bytes 786464 | tf_op jit(solution)/shard_map/ppermute | solution.py:230
  177.8 0.2 add_convert_fusion
  178.0 16.8 %all_to_all.57 = bf16[12,256,128]{2,1,0:T(8,128)(2,1)S(1)} all-to-all(bf16[12,256,128]{2,1,0:T(8,128)(2,1)S(1)} %add_convert_fusion), channel_id=1, replica_groups=mesh['y'=8,'q'=12,'zh'=4,'c'=2] {'q'}, dimensions={0} | all-to-all | bytes 1572864 | tf_op jit(solution)/shard_map/all_to_all | solution.py:231
  194.8 0.3 fusion.3
  195.1 1.9 collective-permute-start.7
  197.0 3.1 collective-permute-done.7
  200.2 22.3 %all_to_all.58 = bf16[4,256,128]{2,1,0:T(8,128)(2,1)S(1)} all-to-all(bf16[4,256,128]{2,1,0:T(8,128)(2,1)S(1)} %broadcast_in_dim.186), channel_id=1, replica_groups={{0,194,388,582},{97,291,485,679},{96,290,484,678},{193,387,581,7},{192,..., dimensions={0} | all-to-all | bytes 524288 | tf_op jit(solution)/shard_map/all_to_all | solution.py:236
  222.6 1.9 collective-permute-start.8
  224.5 4.3 %collective-permute-done.8 = bf16[256,128]{1,0:T(8,128)(2,1)S(1)} collective-permute-done((bf16[256,128]{1,0:T(8,128)(2,1)S(1)}, bf16[256,128]{1,0:T(8,128)(2,1)S(1)}, u32[]{:S(2)}, u32[]{:S(2)}) %collective-permute-start.8) | collective-permute-done | bytes 65568 | tf_op jit(solution)/shard_map/ppermute | solution.py:242
  228.8 18.3 %all_to_all.59.near_ref = bf16[12,256,128]{2,1,0:T(8,128)(2,1)} all-to-all(bf16[12,256,128]{2,1,0:T(8,128)(2,1)S(1)} %broadcast_select_fusion), channel_id=1, replica_groups=mesh['y'=8,'q'=12,'zh'=4,'c'=2] {'q'}, dimensions={0} | all-to-all | bytes 1572864 | tf_op jit(solution)/shard_map/all_to_all | solution.py:244
  247.1 7.9 %collective-permute-start.9 = (bf16[12,256,128]{2,1,0:T(8,128)(2,1)}, bf16[12,256,128]{2,1,0:T(8,128)(2,1)}, u32[]{:S(2)}, u32[]{:S(2)}) collective-permute-start(bf16[12,256,128]{2,1,0:T(8,128)(2,1)} %all_to_all.59.near_ref), channel_id=1, source_target_pairs={{0,97},{97,0},{2,99},{99,2},{4,101},{101,4},{6,103},{103,6},{96,19... | collective-permute-start | bytes 2359304 | tf_op jit(solution)/shard_map/ppermute | solution.py:245
  255.0 0.7 copy.27
  255.7 0.7 copy.28
  256.5 0.7 copy.29
  257.2 7.8 %collective-permute-done.9.far_ref = bf16[12,256,128]{2,1,0:T(8,128)(2,1)} collective-permute-done((bf16[12,256,128]{2,1,0:T(8,128)(2,1)}, bf16[12,256,128]{2,1,0:T(8,128)(2,1)}, u32[]{:S(2)}, u32[]{:S(2)}) %collective-permute-start.9) | collective-permute-done | bytes 786464 | tf_op jit(solution)/shard_map/ppermute | solution.py:245
  265.0 2.4 shard_map.105
  267.4 0.2 convolution_convert_fusion.1
  267.7 1.8 fusion.6
  269.5 0.6 convolution_bitcast_fusion
  270.2 3.4 collective-permute-start.10
  273.5 0.2 fusion.14
  273.8 1.0 collective-permute-done.10
  274.9 0.1 concatenate.26
  275.0 0.2 copy.30
  275.2 10.6 %all_to_all.60 = bf16[12,112,128]{2,1,0:T(8,128)(2,1)S(1)} all-to-all(bf16[12,112,128]{2,1,0:T(8,128)(2,1)S(1)} %bitcast.50), channel_id=1, replica_groups=mesh['y'=8,'q'=12,'zh'=4,'c'=2] {'q'}, dimensions={0} | all-to-all | bytes 688128 | tf_op jit(solution)/shard_map/all_to_all | solution.py:331
  286.0 15.1 %all_to_all.61 = bf16[4,112,128]{2,1,0:T(8,128)(2,1)S(1)} all-to-all(bf16[4,112,128]{2,1,0:T(8,128)(2,1)S(1)} %broadcast_in_dim.194), channel_id=1, replica_groups=mesh['y'=8,'q'=12,'zh'=4,'c'=2] {'zh'}, dimensions={0} | all-to-all | bytes 229376 | tf_op jit(solution)/shard_map/all_to_all | solution.py:332
  301.3 12.4 %all_to_all.62 = bf16[8,112,128]{2,1,0:T(8,128)(2,1)S(1)} all-to-all(bf16[8,112,128]{2,1,0:T(8,128)(2,1)S(1)} %broadcast_in_dim.198), channel_id=1, replica_groups=mesh['y'=8,'q'=12,'zh'=4,'c'=2] {'y'}, dimensions={0} | all-to-all | bytes 458752 | tf_op jit(solution)/shard_map/all_to_all | solution.py:333
  313.7 13.5 %all_to_all.63 = bf16[12,112,128]{2,1,0:T(8,128)(2,1)S(1)} all-to-all(bf16[12,112,128]{2,1,0:T(8,128)(2,1)S(1)} %broadcast_in_dim.202), channel_id=1, replica_groups=mesh['y'=8,'q'=12,'zh'=4,'c'=2] {'q'}, dimensions={0} | all-to-all | bytes 688128 | tf_op jit(solution)/shard_map/all_to_all | solution.py:334
  327.3 6.4 %collective-permute-start.11 = (bf16[1344,128]{1,0:T(8,128)(2,1)S(1)}, bf16[1344,128]{1,0:T(8,128)(2,1)S(1)}, u32[]{:S(2)}, u32[]{:S(2)}) collective-permute-start(bf16[1344,128]{1,0:T(8,128)(2,1)S(1)} %bitcast.51), channel_id=1, source_target_pairs={{0,1},{1,0},{2,3},{3,2},{4,5},{5,4},{6,7},{7,6},{8,9},{9,8},{10,11... | collective-permute-start | bytes 1032200 | tf_op jit(solution)/shard_map/ppermute | solution.py:335
  333.6 1.3 collective-permute-done.11
  334.9 0.1 select_convert_fusion.1
  335.2 0.6 fusion.25
  335.8 0.7 pad_maximum_fusion.2
  337.1 1.0 pad_maximum_fusion
  (69 shorter events, 1.4 us)
Async XLA Ops:
  4.9 16.2 %collective-permute-start = (bf16[12,256,128]{2,1,0:T(8,128)(2,1)S(1)}, bf16[12,256,128]{2,1,0:T(8,128)(2,1)S(1)}, u32[]{:S(2)}, u32[]{:S(2)}) collective-permute-start(bf16[12,256,128]{2,1,0:T(8,128)(2,1)S(1)} %get-tuple-element.31), channel_id=1, source_target_pairs={{0,97},{97,0},{2,99},{99,2},{4,101},{101,4},{6,103},{103,6},{96,19... | collective-permute-start | bytes 2359304 | tf_op jit(solution)/shard_map/ppermute | solution.py:230
  22.1 7.8 %copy-start.10 = (s32[512]{0:T(512)S(1)}, s32[512]{0:T(512)}, u32[]{:S(2)}) copy-start(s32[512]{0:T(512)} %param.8) | copy-start | bytes 6148
  22.1 17.2 %all-to-all-start = ((bf16[12,256,128]{2,1,0:T(8,128)(2,1)}), bf16[12,256,128]{2,1,0:T(8,128)(2,1)}, u32[]{:S(2)}, u32[]{:S(2)}) async-start(bf16[12,256,128]{2,1,0:T(8,128)(2,1)} %add_convert_fusion.1), calls=%async_computation | async-start | bytes 1572864 | tf_op jit(solution)/shard_map/all_to_all | solution.py:231
  40.7 9.5 %collective-permute-start.1 = (bf16[256,128]{1,0:T(8,128)(2,1)S(1)}, bf16[256,128]{1,0:T(8,128)(2,1)S(1)}, u32[]{:S(2)}, u32[]{:S(2)}) collective-permute-start(bf16[256,128]{1,0:T(8,128)(2,1)S(1)} %get-tuple-element.50), channel_id=1, source_target_pairs={{96,0},{192,96},{288,192},{384,288},{480,384},{576,480},{672,576},... | collective-permute-start | bytes 196616 | tf_op jit(solution)/shard_map/ppermute | solution.py:233
  88.4 38.9 %copy-start = (s32[1,1,12,2]{2,3,1,0:T(2,128)S(1)}, s32[1,1,12,2]{2,3,1,0:T(2,128)}, u32[]{:S(2)}) copy-start(s32[1,1,12,2]{2,3,1,0:T(2,128)} %param.11) | copy-start | bytes 292
  88.4 38.9 %copy-start.1 = (s32[1,1,12,2]{2,3,1,0:T(2,128)S(1)}, s32[1,1,12,2]{2,3,1,0:T(2,128)}, u32[]{:S(2)}) copy-start(s32[1,1,12,2]{2,3,1,0:T(2,128)} %param.12) | copy-start | bytes 292
  88.5 6.2 %collective-permute-start.2 = (bf16[256,128]{1,0:T(8,128)(2,1)S(1)}, bf16[256,128]{1,0:T(8,128)(2,1)S(1)}, u32[]{:S(2)}, u32[]{:S(2)}) collective-permute-start(bf16[256,128]{1,0:T(8,128)(2,1)S(1)} %multiply_convert_fusion.2), channel_id=1, source_target_pairs={{0,96},{96,192},{192,288},{288,384},{384,480},{480,576},{576,672},... | collective-permute-start | bytes 196616 | tf_op jit(solution)/shard_map/ppermute | solution.py:242
  110.0 17.4 %collective-permute-start.3 = (bf16[12,256,128]{2,1,0:T(8,128)(2,1)S(1)}, bf16[12,256,128]{2,1,0:T(8,128)(2,1)S(1)}, u32[]{:S(2)}, u32[]{:S(2)}) collective-permute-start(bf16[12,256,128]{2,1,0:T(8,128)(2,1)S(1)} %all_to_all.56.near_ref), channel_id=1, source_target_pairs={{0,97},{97,0},{2,99},{99,2},{4,101},{101,4},{6,103},{103,6},{96,19... | collective-permute-start | bytes 2359304 | tf_op jit(solution)/shard_map/ppermute | solution.py:245
  128.9 5.0 %collective-permute-start.4 = (bf16[256,128]{1,0:T(8,128)(2,1)S(1)}, bf16[256,128]{1,0:T(8,128)(2,1)S(1)}, u32[]{:S(2)}, u32[]{:S(2)}) collective-permute-start(bf16[256,128]{1,0:T(8,128)(2,1)S(1)} %get-tuple-element.35), channel_id=1, source_target_pairs={{0,1},{1,0},{2,3},{3,2},{4,5},{5,4},{6,7},{7,6},{8,9},{9,8},{10,11... | collective-permute-start | bytes 196616 | tf_op jit(solution)/shard_map/ppermute | solution.py:278
  134.7 15.7 %all-to-all-start.3 = ((bf16[4,256,128]{2,1,0:T(8,128)(2,1)}), bf16[4,256,128]{2,1,0:T(8,128)(2,1)}, u32[]{:S(2)}, u32[]{:S(2)}) async-start(bf16[4,256,128]{2,1,0:T(8,128)(2,1)} %broadcast_in_dim.183), calls=%async_computation.3 | async-start | bytes 524288 | tf_op jit(solution)/shard_map/all_to_all | solution.py:279
  152.0 8.9 %collective-permute-start.5 = (bf16[2,256,128]{2,1,0:T(8,128)(2,1)S(1)}, bf16[2,256,128]{2,1,0:T(8,128)(2,1)S(1)}, u32[]{:S(2)}, u32[]{:S(2)}) collective-permute-start(bf16[2,256,128]{2,1,0:T(8,128)(2,1)S(1)} %pad_maximum_fusion.3), channel_id=1, source_target_pairs={{0,1},{1,0},{2,3},{3,2},{4,5},{5,4},{6,7},{7,6},{8,9},{9,8},{10,11... | collective-permute-start | bytes 393224 | tf_op jit(solution)/shard_map/ppermute | solution.py:292
  163.3 14.5 %collective-permute-start.6 = (bf16[12,256,128]{2,1,0:T(8,128)(2,1)S(1)}, bf16[12,256,128]{2,1,0:T(8,128)(2,1)S(1)}, u32[]{:S(2)}, u32[]{:S(2)}) collective-permute-start(bf16[12,256,128]{2,1,0:T(8,128)(2,1)S(1)} %get-tuple-element.42), channel_id=1, source_target_pairs={{0,97},{97,0},{2,99},{99,2},{4,101},{101,4},{6,103},{103,6},{96,19... | collective-permute-start | bytes 2359304 | tf_op jit(solution)/shard_map/ppermute | solution.py:230
  195.1 5.0 %collective-permute-start.7 = (bf16[256,128]{1,0:T(8,128)(2,1)S(1)}, bf16[256,128]{1,0:T(8,128)(2,1)S(1)}, u32[]{:S(2)}, u32[]{:S(2)}) collective-permute-start(bf16[256,128]{1,0:T(8,128)(2,1)S(1)} %get-tuple-element.48), channel_id=1, source_target_pairs={{96,0},{192,96},{288,192},{384,288},{480,384},{576,480},{672,576},... | collective-permute-start | bytes 196616 | tf_op jit(solution)/shard_map/ppermute | solution.py:233
  222.6 6.2 %collective-permute-start.8 = (bf16[256,128]{1,0:T(8,128)(2,1)S(1)}, bf16[256,128]{1,0:T(8,128)(2,1)S(1)}, u32[]{:S(2)}, u32[]{:S(2)}) collective-permute-start(bf16[256,128]{1,0:T(8,128)(2,1)S(1)} %multiply_convert_fusion), channel_id=1, source_target_pairs={{0,96},{96,192},{192,288},{288,384},{384,480},{480,576},{576,672},... | collective-permute-start | bytes 196616 | tf_op jit(solution)/shard_map/ppermute | solution.py:242
  247.1 17.9 %collective-permute-start.9 = (bf16[12,256,128]{2,1,0:T(8,128)(2,1)}, bf16[12,256,128]{2,1,0:T(8,128)(2,1)}, u32[]{:S(2)}, u32[]{:S(2)}) collective-permute-start(bf16[12,256,128]{2,1,0:T(8,128)(2,1)} %all_to_all.59.near_ref), channel_id=1, source_target_pairs={{0,97},{97,0},{2,99},{99,2},{4,101},{101,4},{6,103},{103,6},{96,19... | collective-permute-start | bytes 2359304 | tf_op jit(solution)/shard_map/ppermute | solution.py:245
  257.2 10.2 %copy-start.3 = (bf16[512,512]{1,0:T(8,128)(2,1)S(1)}, bf16[512,512]{1,0:T(8,128)(2,1)}, u32[]{:S(2)}) copy-start(bf16[512,512]{1,0:T(8,128)(2,1)} %get-tuple-element.40) | copy-start | bytes 1572868
  257.2 10.5 %copy-start.5 = (bf16[512,128]{1,0:T(8,128)(2,1)S(1)}, bf16[512,128]{1,0:T(8,128)(2,1)}, u32[]{:S(2)}) copy-start(bf16[512,128]{1,0:T(8,128)(2,1)} %far_second_ref.1) | copy-start | bytes 393220
  267.4 2.1 copy-start.2
  267.4 2.1 copy-start.4
  270.1 4.7 %copy-start.7 = (bf16[1,128]{0,1:T(8,128)(2,1)S(1)}, bf16[1,128]{0,1:T(8,128)(2,1)}, u32[]{:S(2)}) copy-start(bf16[1,128]{0,1:T(8,128)(2,1)} %copy.27) | copy-start | bytes 772
  270.1 4.7 %copy-start.8 = (bf16[1,128]{0,1:T(8,128)(2,1)S(1)}, bf16[1,128]{0,1:T(8,128)(2,1)}, u32[]{:S(2)}) copy-start(bf16[1,128]{0,1:T(8,128)(2,1)} %copy.28) | copy-start | bytes 772
  270.2 4.7 %copy-start.9 = (bf16[1,128]{0,1:T(8,128)(2,1)S(1)}, bf16[1,128]{0,1:T(8,128)(2,1)}, u32[]{:S(2)}) copy-start(bf16[1,128]{0,1:T(8,128)(2,1)} %copy.29) | copy-start | bytes 772
  270.2 4.6 %collective-permute-start.10 = (bf16[1280,128]{0,1:T(8,128)(2,1)S(1)}, bf16[1280,128]{0,1:T(8,128)(2,1)S(1)}, u32[]{:S(2)}, u32[]{:S(2)}) collective-permute-start(bf16[1280,128]{0,1:T(8,128)(2,1)S(1)} %pad_maximum_fusion.1), channel_id=1, source_target_pairs={{0,1},{1,0},{2,3},{3,2},{4,5},{5,4},{6,7},{7,6},{8,9},{9,8},{10,11... | collective-permute-start | bytes 983048 | tf_op jit(solution)/shard_map/ppermute | solution.py:326
  274.8 11.1 %copy-start.6 = (s32[112,128]{1,0:T(8,128)S(1)}, s32[112,128]{1,0:T(8,128)}, u32[]{:S(2)}) copy-start(s32[112,128]{1,0:T(8,128)} %iota.19) | copy-start | bytes 172036
  327.3 7.6 %collective-permute-start.11 = (bf16[1344,128]{1,0:T(8,128)(2,1)S(1)}, bf16[1344,128]{1,0:T(8,128)(2,1)S(1)}, u32[]{:S(2)}, u32[]{:S(2)}) collective-permute-start(bf16[1344,128]{1,0:T(8,128)(2,1)S(1)} %bitcast.51), channel_id=1, source_target_pairs={{0,1},{1,0},{2,3},{3,2},{4,5},{5,4},{6,7},{7,6},{8,9},{9,8},{10,11... | collective-permute-start | bytes 1032200 | tf_op jit(solution)/shard_map/ppermute | solution.py:335
